TPU v7x, 256 devices: a whole 4x4x8 slice. The times are simulated.
256 devices in a mesh: batch: 2 (over y_lo), tm: 64 (over z, x, y_hi), mp: 2 (over core).
Axes of the slice: x: 4, y: 4 (y_hi: 2, y_lo: 2; y = y_hi * 2 + y_lo), z: 8, core: 2. Of those that a mesh axis runs over, the one named last changes fastest.
Arguments:
- input_signal: bfloat16 [2, 8192, 1536], P('batch', 'tm'), may hold values from -6 to 6
- standardize_factor: float32 [1536], replicated, may hold values from 0.1 to 1.9
- triple_projection: bfloat16 [3, 1536, 768], P(None, None, 'mp'), may hold values from -0.15625 to 0.15625
- score_sharpening: float32 [8], P('mp'), may hold values from 1 to 3.5
- final_projection: bfloat16 [768, 1536], P('mp'), may hold values from -0.21875 to 0.21875
- filter_taps: float32 [31, 1536], replicated, may hold values from -1.2 to 1.2
- mixture_adjoint: bfloat16 [2, 8192, 1536], P('batch', 'tm'), may hold values from -16 to 16
Outputs:
- sublayer_result: bfloat16 [2, 8192, 1536], P('batch', 'tm')
- signal_adjoint: bfloat16 [2, 8192, 1536], P('batch', 'tm')
- filter_adjoint: float32 [31, 1536], P(None, ('batch', 'tm'))
- amplifier_adjoint: float32 [1536], P(('batch', 'tm'))
All inputs are finite; a program needn't handle non-finite values.
Results may differ from a plain program's by a relative error of at most 0.015.
Values may be sent and summed in bfloat16 or wider, within the bound.
No kernel may reach another device: no remote copies, remote signals or barrier semaphores. Data moves between devices by JAX's collectives and lax.ppermute only.
A program may use at most 128 MiB of HBM per device.

v0:
```python
import functools
import math

import jax
import jax.numpy as jnp
from jax import lax
from jax.experimental import pallas as pl
from jax.experimental.pallas import tpu as pltpu
from jax.sharding import PartitionSpec as P


INTERPRET = False
LIMIT = 24 * 1024 * 1024
TM = 64
F32 = jnp.float32
BF16 = jnp.bfloat16


def _split(t):
    return t // 16, (t // 8) % 2, (t // 2) % 4, t % 2


def _join(z4, z2, x, yh):
    return ((z4 % 4) * 2 + z2) * 8 + (x % 4) * 2 + yh


def move_z4(a, s):
    pairs = []
    for t in range(TM):
        z4, z2, x, yh = _split(t)
        pairs.append((t, _join(z4 + s, z2, x, yh)))
    return lax.ppermute(a, "tm", pairs)


def move_x(a, s):
    pairs = []
    for t in range(TM):
        z4, z2, x, yh = _split(t)
        pairs.append((t, _join(z4, z2, x + s, yh)))
    return lax.ppermute(a, "tm", pairs)


def move_zy(a, m):
    pairs = []
    for t in range(TM):
        z4, z2, x, yh = _split(t)
        pairs.append((t, _join(z4, z2 ^ (m & 1), x, yh ^ (m >> 1))))
    return lax.ppermute(a, "tm", pairs)


def vcall(kernel, out_shape, scratch=(), smem=0, n_in=0, out_hbm=(), in_hbm=()):
    space = [pl.BlockSpec(memory_space=pltpu.SMEM)] * smem
    space += [pl.BlockSpec(memory_space=pltpu.VMEM)] * n_in
    flat, tree = jax.tree.flatten(out_shape)
    held = flat
    if not INTERPRET:
        held = [o if i in out_hbm else pltpu.VMEM(o.shape, o.dtype) for i, o in enumerate(flat)]
    call = pl.pallas_call(
        kernel,
        out_shape=jax.tree.unflatten(tree, held),
        in_specs=space,
        out_specs=jax.tree.unflatten(tree, [pl.BlockSpec(memory_space=pltpu.VMEM)] * len(flat)),
        scratch_shapes=list(scratch),
        compiler_params=pltpu.CompilerParams(vmem_limit_bytes=LIMIT),
        interpret=INTERPRET,
    )

    def run(*args):
        if not INTERPRET:
            args = [
                a if i < smem or i - smem in in_hbm else pltpu.with_memory_space_constraint(a, pltpu.VMEM)
                for i, a in enumerate(args)
            ]
        return call(*args)

    return run


def dotf(a, b, ca=1, cb=0):
    if INTERPRET:
        a, b = a.astype(F32), b.astype(F32)
    return lax.dot_general(a, b, (((ca,), (cb,)), ((), ())), preferred_element_type=F32)


def front_kernel(idx, sharp, x, factor, w, o0, o1, o2, o3, qpay, qhat_o, khat_o, rad_o, pay, *, heads, hs):
    xf = x[...].astype(F32)
    centred = xf - jnp.mean(xf, axis=-1, keepdims=True)
    var = jnp.mean(centred * centred, axis=-1, keepdims=True)
    unit = centred * (1.0 / jnp.sqrt(var + 1e-05))
    normed = (unit * factor[...]).astype(BF16)
    kt = dotf(normed, w[1]).T
    vt = dotf(normed, w[2]).T
    qt = dotf(normed, w[0]).T
    for h in range(heads):
        lo, hi = h * hs, (h + 1) * hs
        q = qt[lo:hi]
        k = kt[lo:hi]
        qr = jnp.sqrt(jnp.mean(q * q, axis=0, keepdims=True) + 1e-06)
        kr = jnp.sqrt(jnp.mean(k * k, axis=0, keepdims=True) + 1e-06)
        qh = q / qr
        kh = k / kr
        qhat_o[lo:hi] = qh
        khat_o[lo:hi] = kh
        rad_o[h : h + 1] = qr
        rad_o[heads + h : heads + h + 1] = kr
        pay[h, 0:hs] = kh.astype(BF16)
        pay[h, hs : 2 * hs] = vt[lo:hi].astype(BF16)
        qpay[h] = (qh * (sharp[h] / math.sqrt(hs))).astype(BF16)
    for s, o in enumerate((o0, o1, o2, o3)):
        o[...] = pay[lax.rem(idx[0] + s, 4)]


def fill_pad(pad, left, own, right):
    reach = left.shape[0]
    rows = own.shape[0]
    pad[16 - reach : 16] = left[...].astype(F32)
    pad[16 : 16 + rows] = own[...].astype(F32)
    pad[16 + rows : 16 + rows + reach] = right[...].astype(F32)


def conv_rows(pad, taps, out, rows, flip):
    count = taps.shape[0]
    reach = count // 2

    def chunk(c, _):
        lanes = pl.ds(pl.multiple_of(c * 128, 128), 128)
        acc = pad[16 : 16 + rows, lanes]
        for phase in range(8):
            shifted = pad[phase : phase + rows + 24, lanes]
            for j in range(count):
                at = 16 + reach - j if flip else 16 - reach + j
                if at % 8 == phase:
                    acc = acc + taps[j : j + 1, lanes] * shifted[at - phase : at - phase + rows]
        out[:, lanes] = acc.astype(out.dtype)
        return 0

    lax.fori_loop(0, out.shape[1] // 128, chunk, 0)


def send_kernel(idx, left, own, right, taps, qpay, wf, o0, o1, o2, o3, gres, pad, g_s, *, hs):
    fill_pad(pad, left, own, right)
    conv_rows(pad, taps, gres, own.shape[0], True)
    gt = dotf(wf[...], gres[...].astype(BF16), 1, 1).astype(BF16)
    for h in range(4):
        g_s[h] = gt[h * hs : (h + 1) * hs]
    for s, o in enumerate((o0, o1, o2, o3)):
        at = lax.rem(idx[0] + s, 4)
        o[0:hs] = qpay[at]
        o[hs : 2 * hs] = g_s[at]


def tail_kernel(part, other, x, factor, left, own, right, gres, res_o, sig_o, sums, pad, resf, gain, *, rows, taps):
    fill_pad(pad, left, own, right)
    reach = taps // 2
    total = part[0:rows].astype(F32) + other[0:rows].astype(F32)
    xf = x[...].astype(F32)
    residual = (xf + total).astype(BF16)
    res_o[...] = residual
    resf[...] = residual.astype(F32)
    centred = xf - jnp.mean(xf, axis=-1, keepdims=True)
    var = jnp.mean(centred * centred, axis=-1, keepdims=True)
    inv = 1.0 / jnp.sqrt(var + 1e-05)
    unit = centred * inv
    grad = part[rows : 2 * rows].astype(F32) + other[rows : 2 * rows].astype(F32)
    prod = grad * unit
    gain[...] = jnp.sum(prod, axis=0, keepdims=True)
    f = factor[...]
    scaled = grad * f
    m1 = jnp.mean(scaled, axis=-1, keepdims=True)
    m2 = jnp.mean(prod * f, axis=-1, keepdims=True)
    sig_o[...] = (gres[...] + (scaled - m1 - unit * m2) * inv).astype(BF16)
    half = sums.shape[2] // 128

    for h in range(2):

        def chunk(c, _):
            lanes = pl.ds(pl.multiple_of((h * half + c) * 128, 128), 128)
            to = pl.ds(pl.multiple_of(c * 128, 128), 128)
            r = resf[:, lanes]
            for phase in range(8):
                shifted = pad[phase : phase + rows + 24, lanes]
                for j in range(taps):
                    at = 16 + reach - j
                    if at % 8 == phase:
                        moved = shifted[at - phase : at - phase + rows]
                        sums[h, j : j + 1, to] = jnp.sum(r * moved, axis=0, keepdims=True)
            sums[h, taps : taps + 1, to] = gain[:, lanes]
            return 0

        lax.fori_loop(0, half, chunk, 0)


def out_kernel(left, own, right, taps, out, pad):
    fill_pad(pad, left, own, right)
    conv_rows(pad, taps, out, own.shape[0], False)


KB = 512
UQ = 4
UK = 4


def to_rows(a):
    return a.astype(F32).T.astype(BF16)


def totals_kernel(*refs, hs):
    kv = refs[0:4]
    qg = refs[4:8]
    out = refs[8]
    kn, vn, qgs = refs[9:]
    span = kv[0].shape[1]
    for r in range(4):
        kn[r * span : (r + 1) * span] = to_rows(kv[r][0:hs])
        vn[r * span : (r + 1) * span] = to_rows(kv[r][hs : 2 * hs])
        qgs[r] = qg[r][...]
    blocks = 4 * span // KB

    def over_q(j, _):
        qt = qgs[j, 0:hs]
        gt = qgs[j, hs : 2 * hs]

        def over_k(b, state):
            tot, exp = state
            at = pl.multiple_of(b * KB, KB)
            w = jnp.exp(dotf(kn[pl.ds(at, KB)], qt))
            p = dotf(vn[pl.ds(at, KB)], gt)
            tot = tot + jnp.sum(w.reshape(KB // 8, 8, span), axis=0)
            exp = exp + jnp.sum((w * p).reshape(KB // 8, 8, span), axis=0)
            return tot, exp

        zero = jnp.zeros((8, span), F32)
        tot, exp = lax.fori_loop(0, blocks, over_k, (zero, zero), unroll=UK)
        out[j, 0:1] = jnp.sum(tot, axis=0, keepdims=True)
        out[j, 1:2] = jnp.sum(exp, axis=0, keepdims=True)
        return 0

    lax.fori_loop(0, 4, over_q, 0)


def grads_kernel(*refs, hs):
    te = refs[0:2]
    kv = refs[2:6]
    qg = refs[6:10]
    rows = refs[10:14]
    cols = refs[14:18]
    kn, vn, kvs, qgs, qn, gn, acc, inv, dlt, colacc = refs[18:]
    span = kv[0].shape[1]
    per = span // KB
    for r in range(4):
        kn[r * span : (r + 1) * span] = to_rows(kv[r][0:hs])
        vn[r * span : (r + 1) * span] = to_rows(kv[r][hs : 2 * hs])
        for c in range(per):
            kvs[r * per + c] = kv[r][:, c * KB : (c + 1) * KB]
        qgs[r] = qg[r][...]
        qn[r] = to_rows(qg[r][0:hs])
        gn[r] = to_rows(qg[r][hs : 2 * hs])
        t = te[0][r] + te[1][r ^ 2]
        one = 1.0 / t[0:1]
        inv[r] = one
        dlt[r] = t[1:2] * one
    acc[...] = jnp.zeros(acc.shape, F32)

    def over_k(b, _):
        at = pl.multiple_of(b * KB, KB)
        k = kn[pl.ds(at, KB)]
        v = vn[pl.ds(at, KB)]
        kt = kvs[b, 0:hs]
        vt = kvs[b, hs : 2 * hs]

        def over_q(j, state):
            gk, gv = state
            prob = jnp.exp(dotf(k, qgs[j, 0:hs])) * inv[j]
            slope = prob * (dotf(v, qgs[j, hs : 2 * hs]) - dlt[j])
            pb = prob.astype(BF16)
            sb = slope.astype(BF16)
            acc[j, 0:hs] += dotf(vt, pb)
            acc[j, hs : 2 * hs] += dotf(kt, sb)
            return gk + dotf(sb, qn[j]), gv + dotf(pb, gn[j])

        zero = jnp.zeros((KB, hs), F32)
        gk, gv = lax.fori_loop(0, 4, over_q, (zero, zero), unroll=UQ)
        colacc[b, 0:hs] = gk.T.astype(BF16)
        colacc[b, hs : 2 * hs] = gv.T.astype(BF16)
        return 0

    lax.fori_loop(0, 4 * per, over_k, 0)
    for r in range(4):
        rows[r][...] = acc[r].astype(BF16)
        for c in range(per):
            cols[r][:, c * KB : (c + 1) * KB] = colacc[r * per + c]


def run_totals(kv, qg, hs, span):
    return vcall(
        functools.partial(totals_kernel, hs=hs),
        jax.ShapeDtypeStruct((4, 2, span), F32),
        scratch=[
            pltpu.VMEM((4 * span, hs), BF16),
            pltpu.VMEM((4 * span, hs), BF16),
            pltpu.VMEM((4, 2 * hs, span), BF16),
        ],
        n_in=8,
    )(*kv, *qg)


def run_grads(te, kv, qg, hs, span):
    per = span // KB
    return vcall(
        functools.partial(grads_kernel, hs=hs),
        tuple(jax.ShapeDtypeStruct((2 * hs, span), BF16) for _ in range(8)),
        scratch=[
            pltpu.VMEM((4 * span, hs), BF16),
            pltpu.VMEM((4 * span, hs), BF16),
            pltpu.VMEM((4 * per, 2 * hs, KB), BF16),
            pltpu.VMEM((4, 2 * hs, span), BF16),
            pltpu.VMEM((4, span, hs), BF16),
            pltpu.VMEM((4, span, hs), BF16),
            pltpu.VMEM((4, 2 * hs, span), F32),
            pltpu.VMEM((4, 1, span), F32),
            pltpu.VMEM((4, 1, span), F32),
            pltpu.VMEM((4 * per, 2 * hs, KB), BF16),
        ],
        n_in=10,
    )(*te, *kv, *qg)


def sum_kernel(*refs, hs):
    row = refs[0][...].astype(F32)
    col = refs[4][...].astype(F32)
    for i in range(1, 4):
        row = row + refs[i][...].astype(F32)
        col = col + refs[4 + i][...].astype(F32)
    row = row.astype(BF16)
    col = col.astype(BF16)
    lanes = row.shape[1] // 4
    for s in range(4):
        refs[8 + s][0 : 2 * hs] = row[:, s * lanes : (s + 1) * lanes]
        refs[8 + s][2 * hs : 4 * hs] = col[:, s * lanes : (s + 1) * lanes]


def back_kernel(idx, sharp, b0, b1, b2, b3, qhat, khat, rad, wf, w, out, home, att, qgr, kgr, vgr, *, heads, hs):
    for s, b in enumerate((b0, b1, b2, b3)):
        home[lax.rem(idx[0] + s, 4)] = b[...]
    lanes = b0.shape[1]
    for h in range(heads):
        lo, hi = h * hs, (h + 1) * hs
        att[lo:hi] = home[h, 0:hs].astype(F32)
        gq = home[h, hs : 2 * hs].astype(F32) * (sharp[h] / math.sqrt(hs))
        gk = home[h, 2 * hs : 3 * hs].astype(F32)
        vgr[lo:hi] = home[h, 3 * hs : 4 * hs].astype(F32)
        qh = qhat[lo:hi]
        kh = khat[lo:hi]
        qgr[lo:hi] = (gq - qh * jnp.mean(gq * qh, axis=0, keepdims=True)) / rad[h : h + 1]
        kgr[lo:hi] = (gk - kh * jnp.mean(gk * kh, axis=0, keepdims=True)) / rad[heads + h : heads + h + 1]
    out[0:lanes] = dotf(att[...].T.astype(BF16), wf[...]).astype(BF16)
    normed = dotf(qgr[...].T.astype(BF16), w[0], 1, 1)
    normed = normed + dotf(kgr[...].T.astype(BF16), w[1], 1, 1)
    normed = normed + dotf(vgr[...].T.astype(BF16), w[2], 1, 1)
    out[lanes : 2 * lanes] = normed.astype(BF16)


def rims(cells, width):
    ends = TM - 1
    head = cells[:width]
    tail = cells[cells.shape[0] - width :]
    left = lax.ppermute(tail, "tm", [(i, i + 1) for i in range(ends)])
    right = lax.ppermute(head, "tm", [(i + 1, i) for i in range(ends)])
    return left, cells, right


def pieces(a, n):
    width = a.shape[1] // n
    return lambda i: lax.dynamic_slice_in_dim(a, i * width, width, axis=1)


def scatter_sum(a, batches):
    t = lax.axis_index("tm")
    z4, z2, x, yh = t // 16, (t // 8) % 2, (t // 2) % 4, t % 2
    if batches > 1:
        b = lax.axis_index("batch")
        away = lax.dynamic_index_in_dim(a, 1 - b, 0, keepdims=False)
        got = lax.ppermute(away, "batch", [(0, 1), (1, 0)])
        a = lax.dynamic_index_in_dim(a, b, 0, keepdims=False) + got
    else:
        a = jnp.concatenate([a[0], a[1]], axis=1)
    at = pieces(a, 4)
    got = [move_z4(at((z4 + s) % 4), s) for s in (1, 2, 3)]
    a = (at(z4) + got[0]) + (got[1] + got[2])
    at = pieces(a, 2)
    a = at(z2) + move_zy(at(1 - z2), 1)
    at = pieces(a, 4)
    got = [move_x(at((x + s) % 4), s) for s in (1, 2, 3)]
    a = (at(x) + got[0]) + (got[1] + got[2])
    at = pieces(a, 2)
    return at(yh) + move_zy(at(1 - yh), 2)


def step(input_signal, standardize_factor, triple_projection, score_sharpening, final_projection, filter_taps, mixture_adjoint, *, batches, mps):
    rows, width = input_signal.shape[1:]
    heads = score_sharpening.shape[0]
    hs = triple_projection.shape[2] // heads
    flat = heads * hs
    taps = filter_taps.shape[0]
    reach = taps // 2
    t = lax.axis_index("tm")
    z4 = (t // 16).astype(jnp.int32).reshape(1)
    x_in = input_signal[0]
    adj = mixture_adjoint[0]
    factor = standardize_factor[None]
    shape = jax.ShapeDtypeStruct
    adj_rims = rims(adj, reach)
    piece = shape((2 * hs, rows), BF16)
    *sent_kv, qpay, qhat, khat, rad = vcall(
        functools.partial(front_kernel, heads=heads, hs=hs),
        (piece,) * 4 + (shape((heads, hs, rows), BF16), shape((flat, rows), F32), shape((flat, rows), F32), shape((2 * heads, rows), F32)),
        scratch=[pltpu.VMEM((heads, 2 * hs, rows), BF16)],
        smem=2,
        n_in=3,
        in_hbm=(0, 1, 2),
    )(z4, score_sharpening, x_in, factor, triple_projection)
    got_kv = [sent_kv[0]] + [move_z4(sent_kv[s], s) for s in (1, 2, 3)]
    pad = pltpu.VMEM((rows + 32, width), F32)
    *sent_qg, grad_res = vcall(
        functools.partial(send_kernel, hs=hs),
        (piece,) * 4 + (shape((rows, width), F32),),
        scratch=[pad, pltpu.VMEM((4, hs, rows), BF16)],
        smem=1,
        n_in=6,
    )(z4, *adj_rims, filter_taps, qpay, final_projection)
    got_qg = [sent_qg[0]] + [move_z4(sent_qg[s], s) for s in (1, 2, 3)]
    kv0 = jnp.concatenate(got_kv, axis=1)
    qg0 = jnp.concatenate(got_qg, axis=1)
    kv = [kv0] + [move_x(kv0, s) for s in (1, 2, 3)]
    qg = [qg0] + [move_zy(qg0, m) for m in (1, 2, 3)]
    span = 4 * rows
    te0 = run_totals(kv, qg, hs, span)
    te1 = move_zy(te0, 1)
    te1 = te0 + jnp.stack([te1[r ^ 1] for r in range(4)])
    te = [te1, move_zy(te1, 2)]
    res = run_grads(te, kv, qg, hs, span)
    row = [res[0]] + [move_zy(res[m], m) for m in (1, 2, 3)]
    col = [res[4]] + [move_x(res[4 + s], -s) for s in (1, 2, 3)]
    home = vcall(
        functools.partial(sum_kernel, hs=hs),
        tuple(shape((4 * hs, rows), BF16) for _ in range(4)),
        n_in=8,
    )(*row, *col)
    back = [home[0]] + [move_z4(home[s], -s) for s in (1, 2, 3)]
    part = vcall(
        functools.partial(back_kernel, heads=heads, hs=hs),
        shape((2 * rows, width), BF16),
        scratch=[pltpu.VMEM((4, 4 * hs, rows), BF16)] + [pltpu.VMEM((flat, rows), F32)] * 4,
        smem=2,
        n_in=9,
    )(z4, score_sharpening, *back, qhat, khat, rad, final_projection, triple_projection)
    other = lax.ppermute(part, "mp", [(0, 1), (1, 0)]) if mps > 1 else jnp.zeros_like(part)
    residual, signal_adjoint, sums = vcall(
        functools.partial(tail_kernel, rows=rows, taps=taps),
        (shape((rows, width), BF16), shape((rows, width), BF16), shape((2, taps + 1, width // 2), F32)),
        scratch=[pad, pltpu.VMEM((rows, width), F32), pltpu.VMEM((1, width), F32)],
        n_in=8,
        out_hbm=(1,),
    )(part, other, x_in, factor, *adj_rims, grad_res)
    res_rims = rims(residual, reach)
    sublayer_result = vcall(out_kernel, shape((rows, width), BF16), scratch=[pad], n_in=4, out_hbm=(0,))(*res_rims, filter_taps)
    sums = scatter_sum(sums, batches)
    return (sublayer_result[None], signal_adjoint[None], sums[:taps], sums[taps])


def solution(mesh):
    call = mapped(mesh)
    return call


def mapped(mesh):
    return jax.shard_map(
        functools.partial(step, batches=mesh.shape["batch"], mps=mesh.shape["mp"]),
        mesh=mesh,
        in_specs=(
            P("batch", "tm", None),
            P(),
            P(None, None, "mp"),
            P("mp"),
            P("mp", None),
            P(),
            P("batch", "tm", None),
        ),
        out_specs=(
            P("batch", "tm", None),
            P("batch", "tm", None),
            P(None, ("batch", "tm")),
            P(("batch", "tm")),
        ),
        check_vma=False,
    )
```

profile of v0, /device:TPU:30, one launch (start us, length us, event | category | flops | bytes accessed | tf_op | source)
XLA Modules:
  0.0 173.1 jit_solution(6223844506431846179)
XLA Ops:
  6.7 3.4 %collective-permute-start = (bf16[192,128]{1,0:T(8,128)(2,1)S(1)}, bf16[192,128]{1,0:T(8,128)(2,1)S(1)}, u32[]{:S(2)}, u32[]{:S(2)}) collective-permute-start(bf16[192,128]{1,0:T(8,128)(2,1)S(1)} %get-tuple-element.33), channel_id=1, source_target_pairs={{0,32},{2,34},{4,36},{6,38},{8,40},{10,42},{12,44},{14,46},{16,48}... | collective-permute-start | bytes 147464 | tf_op jit(solution)/shard_map/ppermute | solution.py:32
  10.1 5.4 %collective-permute-start.1 = (bf16[192,128]{1,0:T(8,128)(2,1)S(1)}, bf16[192,128]{1,0:T(8,128)(2,1)S(1)}, u32[]{:S(2)}, u32[]{:S(2)}) collective-permute-start(bf16[192,128]{1,0:T(8,128)(2,1)S(1)} %get-tuple-element.34), channel_id=1, source_target_pairs={{0,64},{2,66},{4,68},{6,70},{8,72},{10,74},{12,76},{14,78},{16,80}... | collective-permute-start | bytes 147464 | tf_op jit(solution)/shard_map/ppermute | solution.py:32
  18.2 3.5 %collective-permute-start.6 = (bf16[15,1536]{1,0:T(8,128)(2,1)S(1)}, bf16[15,1536]{1,0:T(8,128)(2,1)S(1)}, u32[]{:S(2)}, u32[]{:S(2)}) collective-permute-start(bf16[15,1536]{1,0:T(8,128)(2,1)S(1)} %get-tuple-element.67), channel_id=1, source_target_pairs={{0,2},{2,4},{4,6},{6,8},{8,10},{10,12},{12,14},{14,16},{16,18},{18... | collective-permute-start | bytes 138248 | tf_op jit(solution)/shard_map/ppermute | solution.py:367
  21.7 3.8 %collective-permute-start.7 = (bf16[15,1536]{1,0:T(8,128)(2,1)S(1)}, bf16[15,1536]{1,0:T(8,128)(2,1)S(1)}, u32[]{:S(2)}, u32[]{:S(2)}) collective-permute-start(bf16[15,1536]{1,0:T(8,128)(2,1)S(1)} %get-tuple-element.66), channel_id=1, source_target_pairs={{2,0},{4,2},{6,4},{8,6},{10,8},{12,10},{14,12},{16,14},{18,16},{20... | collective-permute-start | bytes 138248 | tf_op jit(solution)/shard_map/ppermute | solution.py:368
  25.6 6.5 %collective-permute-done.7.right = bf16[15,1536]{1,0:T(8,128)(2,1)S(1)} collective-permute-done((bf16[15,1536]{1,0:T(8,128)(2,1)S(1)}, bf16[15,1536]{1,0:T(8,128)(2,1)S(1)}, u32[]{:S(2)}, u32[]{:S(2)}) %collective-permute-start.7) | collective-permute-done | bytes 46112 | tf_op jit(solution)/shard_map/ppermute | solution.py:368
  32.2 4.5 %shard_map.103 = (bf16[192,128]{1,0:T(8,128)(2,1)S(1)}, bf16[192,128]{1,0:T(8,128)(2,1)S(1)}, bf16[192,128]{1,0:T(8,128)(2,1)S(1)}, bf16[192,128]{1,0:T(8,128)(2,1)S(1)}, f32[128,1536]{1,0:T(8,128)S(1)}) custom-call(s32[1]{0:T(128)} %bitcast.idx, bf16[15,1536]{1,0:T(8,128)(2,1)S(1)} %collective-permute-done.6.left, bf16[128,1536]{1,0:T(8,128)(2,1)S(1)} %bitcast.16, ...), custom_call_target="tpu_custom_call" | custom-call | tf_op jit(solution)/shard_map/pallas_call | solution.py:74
  39.2 2.8 %collective-permute-start.10 = (bf16[192,128]{1,0:T(8,128)(2,1)S(1)}, bf16[192,128]{1,0:T(8,128)(2,1)S(1)}, u32[]{:S(2)}, u32[]{:S(2)}) collective-permute-start(bf16[192,128]{1,0:T(8,128)(2,1)S(1)} %get-tuple-element.40), channel_id=1, source_target_pairs={{0,96},{2,98},{4,100},{6,102},{8,104},{10,106},{12,108},{14,110},{... | collective-permute-start | bytes 147464 | tf_op jit(solution)/shard_map/ppermute | solution.py:32
  48.1 3.0 %collective-permute-start.13 = (bf16[192,512]{1,0:T(8,128)(2,1)S(1)}, bf16[192,512]{1,0:T(8,128)(2,1)S(1)}, u32[]{:S(2)}, u32[]{:S(2)}) collective-permute-start(bf16[192,512]{1,0:T(8,128)(2,1)S(1)} %constant_dynamic-update-slice_fusion.4.refs_4_.refs_6_), channel_id=1, source_target_pairs={{0,18},{2,16},{4,22},{6,20},{8,26},{10,24},{12,30},{14,28},{16,2},... | collective-permute-start | bytes 589832 | tf_op jit(solution)/shard_map/ppermute | solution.py:48
  53.8 3.5 %collective-permute-done.12.refs_6_.refs_8_ = bf16[192,512]{1,0:T(8,128)(2,1)S(1)} collective-permute-done((bf16[192,512]{1,0:T(8,128)(2,1)S(1)}, bf16[192,512]{1,0:T(8,128)(2,1)S(1)}, u32[]{:S(2)}, u32[]{:S(2)}) %collective-permute-start.12) | collective-permute-done | bytes 196640 | tf_op jit(solution)/shard_map/ppermute | solution.py:48
  57.3 5.4 %shard_map.104 = f32[4,2,512]{2,1,0:T(2,128)S(1)} custom-call(bf16[192,512]{1,0:T(8,128)(2,1)S(1)} %constant_dynamic-update-slice_fusion.refs_0_.refs_2_, bf16[192,512]{1,0:T(8,128)(2,1)S(1)} %collective-permute-done.3.refs_1_.refs_3_, bf16[192,512]{1,0:T(8,128)(2,1)S(1)} %collective-permute-done.4.refs_2_.refs_4_, ...), custom_call_target="tpu_custom_call" | custom-call | tf_op jit(solution)/shard_map/pallas_call | solution.py:74
  63.6 3.2 %collective-permute-done.14 = f32[4,2,512]{2,1,0:T(2,128)S(1)} collective-permute-done((f32[4,2,512]{2,1,0:T(2,128)S(1)}, f32[4,2,512]{2,1,0:T(2,128)S(1)}, u32[]{:S(2)}, u32[]{:S(2)}) %collective-permute-start.14) | collective-permute-done | bytes 16416 | tf_op jit(solution)/shard_map/ppermute | solution.py:48
  68.6 3.5 %collective-permute-done.15.refs_1_ = f32[4,2,512]{2,1,0:T(2,128)S(1)} collective-permute-done((f32[4,2,512]{2,1,0:T(2,128)S(1)}, f32[4,2,512]{2,1,0:T(2,128)S(1)}, u32[]{:S(2)}, u32[]{:S(2)}) %collective-permute-start.15) | collective-permute-done | bytes 16416 | tf_op jit(solution)/shard_map/ppermute | solution.py:48
  72.1 13.8 %shard_map.105 = (bf16[192,512]{1,0:T(8,128)(2,1)S(1)}, bf16[192,512]{1,0:T(8,128)(2,1)S(1)}, bf16[192,512]{1,0:T(8,128)(2,1)S(1)}, bf16[192,512]{1,0:T(8,128)(2...) custom-call(f32[4,2,512]{2,1,0:T(2,128)S(1)} %maximum_add_fusion.ref, ...), custom_call_target="tpu_custom_call" | custom-call | tf_op jit(solution)/shard_map/pallas_call | solution.py:74
  91.0 3.0 %collective-permute-start.20 = (bf16[192,512]{1,0:T(8,128)(2,1)S(1)}, bf16[192,512]{1,0:T(8,128)(2,1)S(1)}, u32[]{:S(2)}, u32[]{:S(2)}) collective-permute-start(bf16[192,512]{1,0:T(8,128)(2,1)S(1)} %get-tuple-element.47), channel_id=1, source_target_pairs={{0,8},{2,10},{4,12},{6,14},{8,0},{10,2},{12,4},{14,6},{16,24},{18,... | collective-permute-start | bytes 589832 | tf_op jit(solution)/shard_map/ppermute | solution.py:40
  96.5 3.5 %collective-permute-done.19.refs_5_ = bf16[192,512]{1,0:T(8,128)(2,1)S(1)} collective-permute-done((bf16[192,512]{1,0:T(8,128)(2,1)S(1)}, bf16[192,512]{1,0:T(8,128)(2,1)S(1)}, u32[]{:S(2)}, u32[]{:S(2)}) %collective-permute-start.19) | collective-permute-done | bytes 196640 | tf_op jit(solution)/shard_map/ppermute | solution.py:40
  103.3 3.5 %collective-permute-start.23 = (bf16[384,128]{1,0:T(8,128)(2,1)S(1)}, bf16[384,128]{1,0:T(8,128)(2,1)S(1)}, u32[]{:S(2)}, u32[]{:S(2)}) collective-permute-start(bf16[384,128]{1,0:T(8,128)(2,1)S(1)} %get-tuple-element.51), channel_id=1, source_target_pairs={{0,64},{2,66},{4,68},{6,70},{8,72},{10,74},{12,76},{14,78},{16,80}... | collective-permute-start | bytes 294920 | tf_op jit(solution)/shard_map/ppermute | solution.py:32
  107.8 4.1 %collective-permute-done.23.b2 = bf16[384,128]{1,0:T(8,128)(2,1)S(1)} collective-permute-done((bf16[384,128]{1,0:T(8,128)(2,1)S(1)}, bf16[384,128]{1,0:T(8,128)(2,1)S(1)}, u32[]{:S(2)}, u32[]{:S(2)}) %collective-permute-start.23) | collective-permute-done | bytes 98336 | tf_op jit(solution)/shard_map/ppermute | solution.py:32
  119.9 3.9 %shard_map.108 = (bf16[128,1536]{1,0:T(8,128)(2,1)S(1)}, bf16[128,1536]{1,0:T(8,128)(2,1)}, f32[2,32,768]{2,1,0:T(8,128)S(1)}) custom-call(bf16[256,1536]{1,0:T(8,128)(2,1)S(1)} %shard_map.107.part, bf16[256,1536]{1,0:T(8,128)(2,1)S(1)} %collective-permute-done.25.other, bf16[128,1536]{1,0:T(8,128)(2,1)S(1)} %bitcast.19, ...), custom_call_target="tpu_custom_call" | custom-call | tf_op jit(solution)/shard_map/pallas_call | solution.py:74
  125.0 4.6 %collective-permute-done.28 = f32[32,768]{1,0:T(8,128)S(1)} collective-permute-done((f32[32,768]{1,0:T(8,128)S(1)}, f32[32,768]{1,0:T(8,128)S(1)}, u32[]{:S(2)}, u32[]{:S(2)}) %collective-permute-start.28) | collective-permute-done | bytes 98336 | tf_op jit(solution)/shard_map/ppermute | solution.py:383
  129.7 3.3 %collective-permute-start.30 = (f32[32,192]{1,0:T(8,128)S(1)}, f32[32,192]{1,0:T(8,128)S(1)}, u32[]{:S(2)}, u32[]{:S(2)}) collective-permute-start(f32[32,192]{1,0:T(8,128)S(1)} %get-tuple-element.70), channel_id=1, source_target_pairs={{0,64},{2,66},{4,68},{6,70},{8,72},{10,74},{12,76},{14,78},{16,80}... | collective-permute-start | bytes 73736 | tf_op jit(solution)/shard_map/ppermute | solution.py:32
  149.7 5.8 %collective-permute-start.26 = (bf16[15,1536]{1,0:T(8,128)(2,1)S(1)}, bf16[15,1536]{1,0:T(8,128)(2,1)S(1)}, u32[]{:S(2)}, u32[]{:S(2)}) collective-permute-start(bf16[15,1536]{1,0:T(8,128)(2,1)S(1)} %get-tuple-element.65), channel_id=1, source_target_pairs={{0,2},{2,4},{4,6},{6,8},{8,10},{10,12},{12,14},{14,16},{16,18},{18... | collective-permute-start | bytes 138248 | tf_op jit(solution)/shard_map/ppermute | solution.py:367
  157.6 2.8 %collective-permute-start.36 = (f32[32,12]{1,0:T(8,128)S(1)}, f32[32,12]{1,0:T(8,128)S(1)}, u32[]{:S(2)}, u32[]{:S(2)}) collective-permute-start(f32[32,12]{1,0:T(8,128)S(1)} %constant_dynamic-slice_fusion), channel_id=1, source_target_pairs={{0,2},{2,0},{4,6},{6,4},{8,10},{10,8},{12,14},{14,12},{16,18},{18,... | collective-permute-start | bytes 4616 | tf_op jit(solution)/shard_map/ppermute | solution.py:48
  160.4 5.6 %collective-permute-done.27.right = bf16[15,1536]{1,0:T(8,128)(2,1)S(1)} collective-permute-done((bf16[15,1536]{1,0:T(8,128)(2,1)S(1)}, bf16[15,1536]{1,0:T(8,128)(2,1)S(1)}, u32[]{:S(2)}, u32[]{:S(2)}) %collective-permute-start.27) | collective-permute-done | bytes 46112 | tf_op jit(solution)/shard_map/ppermute | solution.py:368
  167.0 4.8 %shard_map.109 = bf16[128,1536]{1,0:T(8,128)(2,1)} custom-call(bf16[15,1536]{1,0:T(8,128)(2,1)S(1)} %collective-permute-done.26.left, bf16[128,1536]{1,0:T(8,128)(2,1)S(1)} %copy-done.8, bf16[15,1536]{1,0:T(8,128)(2,1)S(1)} %collective-permute-done.27.right, f32[31,1536]{1,0:T(8,128)S(1)} %copy-done.6), custom_call_target="tpu_custom_call" | custom-call | tf_op jit(solution)/shard_map/pallas_call | solution.py:74
  (113 shorter events, 65.0 us)
Async XLA Ops:
  6.7 32.5 %collective-permute-start = (bf16[192,128]{1,0:T(8,128)(2,1)S(1)}, bf16[192,128]{1,0:T(8,128)(2,1)S(1)}, u32[]{:S(2)}, u32[]{:S(2)}) collective-permute-start(bf16[192,128]{1,0:T(8,128)(2,1)S(1)} %get-tuple-element.33), channel_id=1, source_target_pairs={{0,32},{2,34},{4,36},{6,38},{8,40},{10,42},{12,44},{14,46},{16,48}... | collective-permute-start | bytes 147464 | tf_op jit(solution)/shard_map/ppermute | solution.py:32
  10.1 31.9 %collective-permute-start.1 = (bf16[192,128]{1,0:T(8,128)(2,1)S(1)}, bf16[192,128]{1,0:T(8,128)(2,1)S(1)}, u32[]{:S(2)}, u32[]{:S(2)}) collective-permute-start(bf16[192,128]{1,0:T(8,128)(2,1)S(1)} %get-tuple-element.34), channel_id=1, source_target_pairs={{0,64},{2,66},{4,68},{6,70},{8,72},{10,74},{12,76},{14,78},{16,80}... | collective-permute-start | bytes 147464 | tf_op jit(solution)/shard_map/ppermute | solution.py:32
  15.5 26.6 %collective-permute-start.2 = (bf16[192,128]{1,0:T(8,128)(2,1)S(1)}, bf16[192,128]{1,0:T(8,128)(2,1)S(1)}, u32[]{:S(2)}, u32[]{:S(2)}) collective-permute-start(bf16[192,128]{1,0:T(8,128)(2,1)S(1)} %get-tuple-element.35), channel_id=1, source_target_pairs={{0,96},{2,98},{4,100},{6,102},{8,104},{10,106},{12,108},{14,110},{... | collective-permute-start | bytes 147464 | tf_op jit(solution)/shard_map/ppermute | solution.py:32
  18.2 7.5 %collective-permute-start.6 = (bf16[15,1536]{1,0:T(8,128)(2,1)S(1)}, bf16[15,1536]{1,0:T(8,128)(2,1)S(1)}, u32[]{:S(2)}, u32[]{:S(2)}) collective-permute-start(bf16[15,1536]{1,0:T(8,128)(2,1)S(1)} %get-tuple-element.67), channel_id=1, source_target_pairs={{0,2},{2,4},{4,6},{6,8},{8,10},{10,12},{12,14},{14,16},{16,18},{18... | collective-permute-start | bytes 138248 | tf_op jit(solution)/shard_map/ppermute | solution.py:367
  21.7 10.5 %collective-permute-start.7 = (bf16[15,1536]{1,0:T(8,128)(2,1)S(1)}, bf16[15,1536]{1,0:T(8,128)(2,1)S(1)}, u32[]{:S(2)}, u32[]{:S(2)}) collective-permute-start(bf16[15,1536]{1,0:T(8,128)(2,1)S(1)} %get-tuple-element.66), channel_id=1, source_target_pairs={{2,0},{4,2},{6,4},{8,6},{10,8},{12,10},{14,12},{16,14},{18,16},{20... | collective-permute-start | bytes 138248 | tf_op jit(solution)/shard_map/ppermute | solution.py:368
  37.1 8.2 %collective-permute-start.9 = (bf16[192,128]{1,0:T(8,128)(2,1)S(1)}, bf16[192,128]{1,0:T(8,128)(2,1)S(1)}, u32[]{:S(2)}, u32[]{:S(2)}) collective-permute-start(bf16[192,128]{1,0:T(8,128)(2,1)S(1)} %get-tuple-element.39), channel_id=1, source_target_pairs={{0,64},{2,66},{4,68},{6,70},{8,72},{10,74},{12,76},{14,78},{16,80}... | collective-permute-start | bytes 147464 | tf_op jit(solution)/shard_map/ppermute | solution.py:32
  42.2 9.0 %collective-permute-start.4 = (bf16[192,512]{1,0:T(8,128)(2,1)S(1)}, bf16[192,512]{1,0:T(8,128)(2,1)S(1)}, u32[]{:S(2)}, u32[]{:S(2)}) collective-permute-start(bf16[192,512]{1,0:T(8,128)(2,1)S(1)} %constant_dynamic-update-slice_fusion.refs_0_.refs_2_), channel_id=1, source_target_pairs={{0,8},{2,10},{4,12},{6,14},{8,0},{10,2},{12,4},{14,6},{16,24},{18,... | collective-permute-start | bytes 589832 | tf_op jit(solution)/shard_map/ppermute | solution.py:40
  43.2 8.6 %collective-permute-start.5 = (bf16[192,512]{1,0:T(8,128)(2,1)S(1)}, bf16[192,512]{1,0:T(8,128)(2,1)S(1)}, u32[]{:S(2)}, u32[]{:S(2)}) collective-permute-start(bf16[192,512]{1,0:T(8,128)(2,1)S(1)} %constant_dynamic-update-slice_fusion.refs_0_.refs_2_), channel_id=1, source_target_pairs={{0,12},{2,14},{4,0},{6,2},{8,4},{10,6},{12,8},{14,10},{16,28},{18,... | collective-permute-start | bytes 589832 | tf_op jit(solution)/shard_map/ppermute | solution.py:40
  46.0 7.8 %collective-permute-start.11 = (bf16[192,512]{1,0:T(8,128)(2,1)S(1)}, bf16[192,512]{1,0:T(8,128)(2,1)S(1)}, u32[]{:S(2)}, u32[]{:S(2)}) collective-permute-start(bf16[192,512]{1,0:T(8,128)(2,1)S(1)} %constant_dynamic-update-slice_fusion.4.refs_4_.refs_6_), channel_id=1, source_target_pairs={{0,16},{2,18},{4,20},{6,22},{8,24},{10,26},{12,28},{14,30},{16,0},... | collective-permute-start | bytes 589832 | tf_op jit(solution)/shard_map/ppermute | solution.py:48
  47.4 9.9 %collective-permute-start.12 = (bf16[192,512]{1,0:T(8,128)(2,1)S(1)}, bf16[192,512]{1,0:T(8,128)(2,1)S(1)}, u32[]{:S(2)}, u32[]{:S(2)}) collective-permute-start(bf16[192,512]{1,0:T(8,128)(2,1)S(1)} %constant_dynamic-update-slice_fusion.4.refs_4_.refs_6_), channel_id=1, source_target_pairs={{0,2},{2,0},{4,6},{6,4},{8,10},{10,8},{12,14},{14,12},{16,18},{18,... | collective-permute-start | bytes 589832 | tf_op jit(solution)/shard_map/ppermute | solution.py:48
  48.1 9.2 %collective-permute-start.13 = (bf16[192,512]{1,0:T(8,128)(2,1)S(1)}, bf16[192,512]{1,0:T(8,128)(2,1)S(1)}, u32[]{:S(2)}, u32[]{:S(2)}) collective-permute-start(bf16[192,512]{1,0:T(8,128)(2,1)S(1)} %constant_dynamic-update-slice_fusion.4.refs_4_.refs_6_), channel_id=1, source_target_pairs={{0,18},{2,16},{4,22},{6,20},{8,26},{10,24},{12,30},{14,28},{16,2},... | collective-permute-start | bytes 589832 | tf_op jit(solution)/shard_map/ppermute | solution.py:48
  85.9 8.1 %collective-permute-start.16 = (bf16[192,512]{1,0:T(8,128)(2,1)S(1)}, bf16[192,512]{1,0:T(8,128)(2,1)S(1)}, u32[]{:S(2)}, u32[]{:S(2)}) collective-permute-start(bf16[192,512]{1,0:T(8,128)(2,1)S(1)} %get-tuple-element.42), channel_id=1, source_target_pairs={{0,16},{2,18},{4,20},{6,22},{8,24},{10,26},{12,28},{14,30},{16,0},... | collective-permute-start | bytes 589832 | tf_op jit(solution)/shard_map/ppermute | solution.py:48
  86.6 8.6 %collective-permute-start.17 = (bf16[192,512]{1,0:T(8,128)(2,1)S(1)}, bf16[192,512]{1,0:T(8,128)(2,1)S(1)}, u32[]{:S(2)}, u32[]{:S(2)}) collective-permute-start(bf16[192,512]{1,0:T(8,128)(2,1)S(1)} %get-tuple-element.43), channel_id=1, source_target_pairs={{0,2},{2,0},{4,6},{6,4},{8,10},{10,8},{12,14},{14,12},{16,18},{18,... | collective-permute-start | bytes 589832 | tf_op jit(solution)/shard_map/ppermute | solution.py:48
  88.5 8.1 %collective-permute-start.18 = (bf16[192,512]{1,0:T(8,128)(2,1)S(1)}, bf16[192,512]{1,0:T(8,128)(2,1)S(1)}, u32[]{:S(2)}, u32[]{:S(2)}) collective-permute-start(bf16[192,512]{1,0:T(8,128)(2,1)S(1)} %get-tuple-element.44), channel_id=1, source_target_pairs={{0,18},{2,16},{4,22},{6,20},{8,26},{10,24},{12,30},{14,28},{16,2},... | collective-permute-start | bytes 589832 | tf_op jit(solution)/shard_map/ppermute | solution.py:48
  91.0 9.0 %collective-permute-start.19 = (bf16[192,512]{1,0:T(8,128)(2,1)S(1)}, bf16[192,512]{1,0:T(8,128)(2,1)S(1)}, u32[]{:S(2)}, u32[]{:S(2)}) collective-permute-start(bf16[192,512]{1,0:T(8,128)(2,1)S(1)} %get-tuple-element.46), channel_id=1, source_target_pairs={{0,12},{2,14},{4,0},{6,2},{8,4},{10,6},{12,8},{14,10},{16,28},{18,... | collective-permute-start | bytes 589832 | tf_op jit(solution)/shard_map/ppermute | solution.py:40
  91.0 9.0 %collective-permute-start.20 = (bf16[192,512]{1,0:T(8,128)(2,1)S(1)}, bf16[192,512]{1,0:T(8,128)(2,1)S(1)}, u32[]{:S(2)}, u32[]{:S(2)}) collective-permute-start(bf16[192,512]{1,0:T(8,128)(2,1)S(1)} %get-tuple-element.47), channel_id=1, source_target_pairs={{0,8},{2,10},{4,12},{6,14},{8,0},{10,2},{12,4},{14,6},{16,24},{18,... | collective-permute-start | bytes 589832 | tf_op jit(solution)/shard_map/ppermute | solution.py:40
  103.3 8.6 %collective-permute-start.23 = (bf16[384,128]{1,0:T(8,128)(2,1)S(1)}, bf16[384,128]{1,0:T(8,128)(2,1)S(1)}, u32[]{:S(2)}, u32[]{:S(2)}) collective-permute-start(bf16[384,128]{1,0:T(8,128)(2,1)S(1)} %get-tuple-element.51), channel_id=1, source_target_pairs={{0,64},{2,66},{4,68},{6,70},{8,72},{10,74},{12,76},{14,78},{16,80}... | collective-permute-start | bytes 294920 | tf_op jit(solution)/shard_map/ppermute | solution.py:32
  129.7 7.9 %collective-permute-start.30 = (f32[32,192]{1,0:T(8,128)S(1)}, f32[32,192]{1,0:T(8,128)S(1)}, u32[]{:S(2)}, u32[]{:S(2)}) collective-permute-start(f32[32,192]{1,0:T(8,128)S(1)} %get-tuple-element.70), channel_id=1, source_target_pairs={{0,64},{2,66},{4,68},{6,70},{8,72},{10,74},{12,76},{14,78},{16,80}... | collective-permute-start | bytes 73736 | tf_op jit(solution)/shard_map/ppermute | solution.py:32
  144.8 12.7 %collective-permute-start.34 = (f32[32,24]{1,0:T(8,128)S(1)}, f32[32,24]{1,0:T(8,128)S(1)}, u32[]{:S(2)}, u32[]{:S(2)}) collective-permute-start(f32[32,24]{1,0:T(8,128)S(1)} %get-tuple-element.73), channel_id=1, source_target_pairs={{0,8},{2,10},{4,12},{6,14},{8,0},{10,2},{12,4},{14,6},{16,24},{18,... | collective-permute-start | bytes 9224 | tf_op jit(solution)/shard_map/ppermute | solution.py:40
  145.6 11.9 %collective-permute-start.35 = (f32[32,24]{1,0:T(8,128)S(1)}, f32[32,24]{1,0:T(8,128)S(1)}, u32[]{:S(2)}, u32[]{:S(2)}) collective-permute-start(f32[32,24]{1,0:T(8,128)S(1)} %get-tuple-element.72), channel_id=1, source_target_pairs={{0,12},{2,14},{4,0},{6,2},{8,4},{10,6},{12,8},{14,10},{16,28},{18,... | collective-permute-start | bytes 9224 | tf_op jit(solution)/shard_map/ppermute | solution.py:40
  148.1 9.3 %collective-permute-start.33 = (f32[32,24]{1,0:T(8,128)S(1)}, f32[32,24]{1,0:T(8,128)S(1)}, u32[]{:S(2)}, u32[]{:S(2)}) collective-permute-start(f32[32,24]{1,0:T(8,128)S(1)} %get-tuple-element.71), channel_id=1, source_target_pairs={{0,4},{2,6},{4,8},{6,10},{8,12},{10,14},{12,0},{14,2},{16,20},{18,... | collective-permute-start | bytes 9224 | tf_op jit(solution)/shard_map/ppermute | solution.py:40
  149.7 10.8 %collective-permute-start.26 = (bf16[15,1536]{1,0:T(8,128)(2,1)S(1)}, bf16[15,1536]{1,0:T(8,128)(2,1)S(1)}, u32[]{:S(2)}, u32[]{:S(2)}) collective-permute-start(bf16[15,1536]{1,0:T(8,128)(2,1)S(1)} %get-tuple-element.65), channel_id=1, source_target_pairs={{0,2},{2,4},{4,6},{6,8},{8,10},{10,12},{12,14},{14,16},{16,18},{18... | collective-permute-start | bytes 138248 | tf_op jit(solution)/shard_map/ppermute | solution.py:367
  155.5 10.5 %collective-permute-start.27 = (bf16[15,1536]{1,0:T(8,128)(2,1)S(1)}, bf16[15,1536]{1,0:T(8,128)(2,1)S(1)}, u32[]{:S(2)}, u32[]{:S(2)}) collective-permute-start(bf16[15,1536]{1,0:T(8,128)(2,1)S(1)} %get-tuple-element.64), channel_id=1, source_target_pairs={{2,0},{4,2},{6,4},{8,6},{10,8},{12,10},{14,12},{16,14},{18,16},{20... | collective-permute-start | bytes 138248 | tf_op jit(solution)/shard_map/ppermute | solution.py:368
  157.6 14.2 %collective-permute-start.36 = (f32[32,12]{1,0:T(8,128)S(1)}, f32[32,12]{1,0:T(8,128)S(1)}, u32[]{:S(2)}, u32[]{:S(2)}) collective-permute-start(f32[32,12]{1,0:T(8,128)S(1)} %constant_dynamic-slice_fusion), channel_id=1, source_target_pairs={{0,2},{2,0},{4,6},{6,4},{8,10},{10,8},{12,14},{14,12},{16,18},{18,... | collective-permute-start | bytes 4616 | tf_op jit(solution)/shard_map/ppermute | solution.py:48
  (28 other events, 352.9 us)
where the time goes:
time: 174 us; the launch traced here: 173 us
  starting transfers between devices  72.8 us (42%)
  waiting for transfers between devices  52.3 us (30%)
  Pallas kernels  36.5 us (21%)
  local copies, waits for them, and re-layouts  10.2 us (6%)
    pallas_call x8, Pallas kernels, run(): return call(*args)  36.5 us
    ppermute x12, starting transfers between devices, move_z4(): return lax.ppermute(a, 'tm', pairs)  29.3 us
    ppermute x10, starting transfers between devices, move_zy(): return lax.ppermute(a, 'tm', pairs)  17.4 us
    ppermute x10, waiting for transfers between devices, move_zy(): return lax.ppermute(a, 'tm', pairs)  15.3 us
    ppermute x12, waiting for transfers between devices, move_z4(): return lax.ppermute(a, 'tm', pairs)  12.3 us
    ppermute x2, waiting for transfers between devices, rims(): right = lax.ppermute(head, 'tm', [(i + 1, i) for i in range(ends)])  12.1 us
    ppermute x9, starting transfers between devices, move_x(): return lax.ppermute(a, 'tm', pairs)  10.3 us
    ppermute x2, starting transfers between devices, rims(): left = lax.ppermute(tail, 'tm', [(i, i + 1) for i in range(ends)])  9.35 us
  transfers between devices with their start and end apart: 37, of which 23 were waited for; matrix products, arithmetic and copies ran while one was open for 1% of the time, Pallas kernels for 5%

commit v1 on v0

--- a/solution.py
+++ b/solution.py
@@ -48,9 +48,15 @@
     return lax.ppermute(a, "tm", pairs)
 
 
-def vcall(kernel, out_shape, scratch=(), smem=0, n_in=0, out_hbm=(), in_hbm=()):
+def ordered(move, shifts):
+    got = {s: move(s) for s in shifts}
+    return [got[s] for s in (1, 2, 3)]
+
+
+def vcall(kernel, out_shape, scratch=(), smem=0, n_in=0, raw=0, out_hbm=()):
     space = [pl.BlockSpec(memory_space=pltpu.SMEM)] * smem
     space += [pl.BlockSpec(memory_space=pltpu.VMEM)] * n_in
+    space += [pl.BlockSpec(memory_space=pltpu.HBM if not INTERPRET else pl.ANY)] * raw
     flat, tree = jax.tree.flatten(out_shape)
     held = flat
     if not INTERPRET:
@@ -68,7 +74,7 @@
     def run(*args):
         if not INTERPRET:
             args = [
-                a if i < smem or i - smem in in_hbm else pltpu.with_memory_space_constraint(a, pltpu.VMEM)
+                a if i < smem else pltpu.with_memory_space_constraint(a, pltpu.VMEM if i < smem + n_in else pltpu.HBM)
                 for i, a in enumerate(args)
             ]
         return call(*args)
@@ -82,14 +88,25 @@
     return lax.dot_general(a, b, (((ca,), (cb,)), ((), ())), preferred_element_type=F32)
 
 
-def front_kernel(idx, sharp, x, factor, w, o0, o1, o2, o3, qpay, qhat_o, khat_o, rad_o, pay, *, heads, hs):
+def front_kernel(
+    idx, sharp, factor, x_hbm, w_hbm, o0, o1, o2, o3, qpay, qhat_o, khat_o, rad_o, pay, x, w, sem, *, heads, hs
+):
+    x_copy = pltpu.make_async_copy(x_hbm, x, sem.at[0])
+    x_copy.start()
+    copies = [pltpu.make_async_copy(w_hbm.at[i], w.at[i], sem.at[1 + i]) for i in range(3)]
+    for i in (1, 2, 0):
+        copies[i].start()
+    x_copy.wait()
     xf = x[...].astype(F32)
     centred = xf - jnp.mean(xf, axis=-1, keepdims=True)
     var = jnp.mean(centred * centred, axis=-1, keepdims=True)
     unit = centred * (1.0 / jnp.sqrt(var + 1e-05))
     normed = (unit * factor[...]).astype(BF16)
+    copies[1].wait()
     kt = dotf(normed, w[1]).T
+    copies[2].wait()
     vt = dotf(normed, w[2]).T
+    copies[0].wait()
     qt = dotf(normed, w[0]).T
     for h in range(heads):
         lo, hi = h * hs, (h + 1) * hs
@@ -149,13 +166,15 @@
         o[hs : 2 * hs] = g_s[at]
 
 
-def tail_kernel(part, other, x, factor, left, own, right, gres, res_o, sig_o, sums, pad, resf, gain, *, rows, taps):
+def tail_kernel(part, other, x, factor, left, own, right, gres, res_o, sig_o, sums, first, last, pad, resf, gain, *, rows, taps):
     fill_pad(pad, left, own, right)
     reach = taps // 2
     total = part[0:rows].astype(F32) + other[0:rows].astype(F32)
     xf = x[...].astype(F32)
     residual = (xf + total).astype(BF16)
     res_o[...] = residual
+    first[...] = residual[:reach]
+    last[...] = residual[rows - reach :]
     resf[...] = residual.astype(F32)
     centred = xf - jnp.mean(xf, axis=-1, keepdims=True)
     var = jnp.mean(centred * centred, axis=-1, keepdims=True)
@@ -195,132 +214,106 @@
     conv_rows(pad, taps, out, own.shape[0], False)
 
 
-KB = 512
-UQ = 4
-UK = 4
-
-
 def to_rows(a):
     return a.astype(F32).T.astype(BF16)
 
 
-def totals_kernel(*refs, hs):
+def rows_kernel(*refs, hs):
     kv = refs[0:4]
     qg = refs[4:8]
-    out = refs[8]
-    kn, vn, qgs = refs[9:]
+    te, acc = refs[8:10]
+    kn, vn, qgs = refs[10:]
     span = kv[0].shape[1]
     for r in range(4):
-        kn[r * span : (r + 1) * span] = to_rows(kv[r][0:hs])
-        vn[r * span : (r + 1) * span] = to_rows(kv[r][hs : 2 * hs])
+        kn[r] = to_rows(kv[r][0:hs])
+        vn[r] = to_rows(kv[r][hs : 2 * hs])
         qgs[r] = qg[r][...]
-    blocks = 4 * span // KB
 
     def over_q(j, _):
         qt = qgs[j, 0:hs]
         gt = qgs[j, hs : 2 * hs]
-
-        def over_k(b, state):
-            tot, exp = state
-            at = pl.multiple_of(b * KB, KB)
-            w = jnp.exp(dotf(kn[pl.ds(at, KB)], qt))
-            p = dotf(vn[pl.ds(at, KB)], gt)
-            tot = tot + jnp.sum(w.reshape(KB // 8, 8, span), axis=0)
-            exp = exp + jnp.sum((w * p).reshape(KB // 8, 8, span), axis=0)
-            return tot, exp
-
-        zero = jnp.zeros((8, span), F32)
-        tot, exp = lax.fori_loop(0, blocks, over_k, (zero, zero), unroll=UK)
-        out[j, 0:1] = jnp.sum(tot, axis=0, keepdims=True)
-        out[j, 1:2] = jnp.sum(exp, axis=0, keepdims=True)
+        tot = jnp.zeros((8, span), F32)
+        exp = jnp.zeros((8, span), F32)
+        low = jnp.zeros((2 * hs, span), F32)
+        high = jnp.zeros((hs, span), F32)
+        for r in range(4):
+            w = jnp.exp(dotf(kn[r], qt))
+            wp = w * dotf(vn[r], gt)
+            tot = tot + jnp.sum(w.reshape(span // 8, 8, span), axis=0)
+            exp = exp + jnp.sum(wp.reshape(span // 8, 8, span), axis=0)
+            low = low + dotf(kv[r][...], w.astype(BF16))
+            high = high + dotf(kv[r][0:hs], wp.astype(BF16))
+        acc[j, 0 : 2 * hs] = low
+        acc[j, 2 * hs : 3 * hs] = high
+        te[j, 0:1] = jnp.sum(tot, axis=0, keepdims=True)
+        te[j, 1:2] = jnp.sum(exp, axis=0, keepdims=True)
         return 0
 
     lax.fori_loop(0, 4, over_q, 0)
 
 
-def grads_kernel(*refs, hs):
+def norm_kernel(te0, te1, acc, *rows, hs):
+    for r in range(4):
+        t = te0[r] + te1[r ^ 2]
+        inv = 1.0 / t[0:1]
+        delta = t[1:2] * inv
+        rows[r][0:hs] = (acc[r, hs : 2 * hs] * inv).astype(BF16)
+        rows[r][hs : 2 * hs] = ((acc[r, 2 * hs : 3 * hs] - delta * acc[r, 0:hs]) * inv).astype(BF16)
+
+
+def cols_kernel(*refs, hs):
     te = refs[0:2]
     kv = refs[2:6]
     qg = refs[6:10]
-    rows = refs[10:14]
-    cols = refs[14:18]
-    kn, vn, kvs, qgs, qn, gn, acc, inv, dlt, colacc = refs[18:]
+    cols = refs[10:14]
+    kn, vn, qn, gn, inv, dlt, colacc = refs[14:]
     span = kv[0].shape[1]
-    per = span // KB
     for r in range(4):
-        kn[r * span : (r + 1) * span] = to_rows(kv[r][0:hs])
-        vn[r * span : (r + 1) * span] = to_rows(kv[r][hs : 2 * hs])
-        for c in range(per):
-            kvs[r * per + c] = kv[r][:, c * KB : (c + 1) * KB]
-        qgs[r] = qg[r][...]
+        kn[r] = to_rows(kv[r][0:hs])
+        vn[r] = to_rows(kv[r][hs : 2 * hs])
         qn[r] = to_rows(qg[r][0:hs])
         gn[r] = to_rows(qg[r][hs : 2 * hs])
         t = te[0][r] + te[1][r ^ 2]
         one = 1.0 / t[0:1]
         inv[r] = one
         dlt[r] = t[1:2] * one
-    acc[...] = jnp.zeros(acc.shape, F32)
 
     def over_k(b, _):
-        at = pl.multiple_of(b * KB, KB)
-        k = kn[pl.ds(at, KB)]
-        v = vn[pl.ds(at, KB)]
-        kt = kvs[b, 0:hs]
-        vt = kvs[b, hs : 2 * hs]
-
-        def over_q(j, state):
-            gk, gv = state
-            prob = jnp.exp(dotf(k, qgs[j, 0:hs])) * inv[j]
-            slope = prob * (dotf(v, qgs[j, hs : 2 * hs]) - dlt[j])
-            pb = prob.astype(BF16)
-            sb = slope.astype(BF16)
-            acc[j, 0:hs] += dotf(vt, pb)
-            acc[j, hs : 2 * hs] += dotf(kt, sb)
-            return gk + dotf(sb, qn[j]), gv + dotf(pb, gn[j])
-
-        zero = jnp.zeros((KB, hs), F32)
-        gk, gv = lax.fori_loop(0, 4, over_q, (zero, zero), unroll=UQ)
+        k = kn[b]
+        v = vn[b]
+        gk = jnp.zeros((span, hs), F32)
+        gv = jnp.zeros((span, hs), F32)
+        for j in range(4):
+            prob = jnp.exp(dotf(k, qg[j][0:hs])) * inv[j]
+            slope = prob * (dotf(v, qg[j][hs : 2 * hs]) - dlt[j])
+            gv = gv + dotf(prob.astype(BF16), gn[j])
+            gk = gk + dotf(slope.astype(BF16), qn[j])
         colacc[b, 0:hs] = gk.T.astype(BF16)
         colacc[b, hs : 2 * hs] = gv.T.astype(BF16)
         return 0
 
-    lax.fori_loop(0, 4 * per, over_k, 0)
+    lax.fori_loop(0, 4, over_k, 0)
     for r in range(4):
-        rows[r][...] = acc[r].astype(BF16)
-        for c in range(per):
-            cols[r][:, c * KB : (c + 1) * KB] = colacc[r * per + c]
-
-
-def run_totals(kv, qg, hs, span):
+        cols[r][...] = colacc[r]
+
+
+def run_rows(kv, qg, hs, span):
+    nat = pltpu.VMEM((4, span, hs), BF16)
     return vcall(
-        functools.partial(totals_kernel, hs=hs),
-        jax.ShapeDtypeStruct((4, 2, span), F32),
-        scratch=[
-            pltpu.VMEM((4 * span, hs), BF16),
-            pltpu.VMEM((4 * span, hs), BF16),
-            pltpu.VMEM((4, 2 * hs, span), BF16),
-        ],
+        functools.partial(rows_kernel, hs=hs),
+        (jax.ShapeDtypeStruct((4, 2, span), F32), jax.ShapeDtypeStruct((4, 3 * hs, span), F32)),
+        scratch=[nat, nat, pltpu.VMEM((4, 2 * hs, span), BF16)],
         n_in=8,
     )(*kv, *qg)
 
 
-def run_grads(te, kv, qg, hs, span):
-    per = span // KB
+def run_cols(te, kv, qg, hs, span):
+    nat = pltpu.VMEM((4, span, hs), BF16)
+    row = pltpu.VMEM((4, 1, span), F32)
     return vcall(
-        functools.partial(grads_kernel, hs=hs),
-        tuple(jax.ShapeDtypeStruct((2 * hs, span), BF16) for _ in range(8)),
-        scratch=[
-            pltpu.VMEM((4 * span, hs), BF16),
-            pltpu.VMEM((4 * span, hs), BF16),
-            pltpu.VMEM((4 * per, 2 * hs, KB), BF16),
-            pltpu.VMEM((4, 2 * hs, span), BF16),
-            pltpu.VMEM((4, span, hs), BF16),
-            pltpu.VMEM((4, span, hs), BF16),
-            pltpu.VMEM((4, 2 * hs, span), F32),
-            pltpu.VMEM((4, 1, span), F32),
-            pltpu.VMEM((4, 1, span), F32),
-            pltpu.VMEM((4 * per, 2 * hs, KB), BF16),
-        ],
+        functools.partial(cols_kernel, hs=hs),
+        tuple(jax.ShapeDtypeStruct((2 * hs, span), BF16) for _ in range(4)),
+        scratch=[nat, nat, nat, nat, row, row, pltpu.VMEM((4, 2 * hs, span), BF16)],
         n_in=10,
     )(*te, *kv, *qg)
 
@@ -360,10 +353,8 @@
     out[lanes : 2 * lanes] = normed.astype(BF16)
 
 
-def rims(cells, width):
+def rims(cells, head, tail):
     ends = TM - 1
-    head = cells[:width]
-    tail = cells[cells.shape[0] - width :]
     left = lax.ppermute(tail, "tm", [(i, i + 1) for i in range(ends)])
     right = lax.ppermute(head, "tm", [(i + 1, i) for i in range(ends)])
     return left, cells, right
@@ -385,12 +376,12 @@
     else:
         a = jnp.concatenate([a[0], a[1]], axis=1)
     at = pieces(a, 4)
-    got = [move_z4(at((z4 + s) % 4), s) for s in (1, 2, 3)]
+    got = ordered(lambda s: move_z4(at((z4 + s) % 4), s), (2, 1, 3))
     a = (at(z4) + got[0]) + (got[1] + got[2])
     at = pieces(a, 2)
     a = at(z2) + move_zy(at(1 - z2), 1)
     at = pieces(a, 4)
-    got = [move_x(at((x + s) % 4), s) for s in (1, 2, 3)]
+    got = ordered(lambda s: move_x(at((x + s) % 4), s), (2, 1, 3))
     a = (at(x) + got[0]) + (got[1] + got[2])
     at = pieces(a, 2)
     return at(yh) + move_zy(at(1 - yh), 2)
@@ -409,17 +400,22 @@
     adj = mixture_adjoint[0]
     factor = standardize_factor[None]
     shape = jax.ShapeDtypeStruct
-    adj_rims = rims(adj, reach)
+    adj_rims = rims(adj, adj[:reach], adj[rows - reach :])
     piece = shape((2 * hs, rows), BF16)
     *sent_kv, qpay, qhat, khat, rad = vcall(
         functools.partial(front_kernel, heads=heads, hs=hs),
         (piece,) * 4 + (shape((heads, hs, rows), BF16), shape((flat, rows), F32), shape((flat, rows), F32), shape((2 * heads, rows), F32)),
-        scratch=[pltpu.VMEM((heads, 2 * hs, rows), BF16)],
+        scratch=[
+            pltpu.VMEM((heads, 2 * hs, rows), BF16),
+            pltpu.VMEM((rows, width), BF16),
+            pltpu.VMEM((3, width, flat), BF16),
+            pltpu.SemaphoreType.DMA((4,)),
+        ],
         smem=2,
-        n_in=3,
-        in_hbm=(0, 1, 2),
-    )(z4, score_sharpening, x_in, factor, triple_projection)
-    got_kv = [sent_kv[0]] + [move_z4(sent_kv[s], s) for s in (1, 2, 3)]
+        n_in=1,
+        raw=2,
+    )(z4, score_sharpening, factor, x_in, triple_projection)
+    got_kv = [sent_kv[0]] + ordered(lambda s: move_z4(sent_kv[s], s), (2, 1, 3))
     pad = pltpu.VMEM((rows + 32, width), F32)
     *sent_qg, grad_res = vcall(
         functools.partial(send_kernel, hs=hs),
@@ -428,25 +424,26 @@
         smem=1,
         n_in=6,
     )(z4, *adj_rims, filter_taps, qpay, final_projection)
-    got_qg = [sent_qg[0]] + [move_z4(sent_qg[s], s) for s in (1, 2, 3)]
+    got_qg = [sent_qg[0]] + ordered(lambda s: move_z4(sent_qg[s], s), (2, 1, 3))
     kv0 = jnp.concatenate(got_kv, axis=1)
     qg0 = jnp.concatenate(got_qg, axis=1)
-    kv = [kv0] + [move_x(kv0, s) for s in (1, 2, 3)]
-    qg = [qg0] + [move_zy(qg0, m) for m in (1, 2, 3)]
+    kv = [kv0] + ordered(lambda s: move_x(kv0, s), (2, 1, 3))
+    qg = [qg0] + ordered(lambda m: move_zy(qg0, m), (3, 2, 1))
     span = 4 * rows
-    te0 = run_totals(kv, qg, hs, span)
+    te0, acc = run_rows(kv, qg, hs, span)
     te1 = move_zy(te0, 1)
     te1 = te0 + jnp.stack([te1[r ^ 1] for r in range(4)])
     te = [te1, move_zy(te1, 2)]
-    res = run_grads(te, kv, qg, hs, span)
-    row = [res[0]] + [move_zy(res[m], m) for m in (1, 2, 3)]
-    col = [res[4]] + [move_x(res[4 + s], -s) for s in (1, 2, 3)]
+    rowp = vcall(functools.partial(norm_kernel, hs=hs), (shape((2 * hs, span), BF16),) * 4, n_in=3)(*te, acc)
+    row = [rowp[0]] + ordered(lambda m: move_zy(rowp[m], m), (3, 2, 1))
+    colp = run_cols(te, kv, qg, hs, span)
+    col = [colp[0]] + ordered(lambda s: move_x(colp[s], -s), (2, 1, 3))
     home = vcall(
         functools.partial(sum_kernel, hs=hs),
         tuple(shape((4 * hs, rows), BF16) for _ in range(4)),
         n_in=8,
     )(*row, *col)
-    back = [home[0]] + [move_z4(home[s], -s) for s in (1, 2, 3)]
+    back = [home[0]] + ordered(lambda s: move_z4(home[s], -s), (2, 1, 3))
     part = vcall(
         functools.partial(back_kernel, heads=heads, hs=hs),
         shape((2 * rows, width), BF16),
@@ -455,14 +452,15 @@
         n_in=9,
     )(z4, score_sharpening, *back, qhat, khat, rad, final_projection, triple_projection)
     other = lax.ppermute(part, "mp", [(0, 1), (1, 0)]) if mps > 1 else jnp.zeros_like(part)
-    residual, signal_adjoint, sums = vcall(
+    edge = shape((reach, width), BF16)
+    residual, signal_adjoint, sums, first, last = vcall(
         functools.partial(tail_kernel, rows=rows, taps=taps),
-        (shape((rows, width), BF16), shape((rows, width), BF16), shape((2, taps + 1, width // 2), F32)),
+        (shape((rows, width), BF16), shape((rows, width), BF16), shape((2, taps + 1, width // 2), F32), edge, edge),
         scratch=[pad, pltpu.VMEM((rows, width), F32), pltpu.VMEM((1, width), F32)],
         n_in=8,
         out_hbm=(1,),
     )(part, other, x_in, factor, *adj_rims, grad_res)
-    res_rims = rims(residual, reach)
+    res_rims = rims(residual, first, last)
     sublayer_result = vcall(out_kernel, shape((rows, width), BF16), scratch=[pad], n_in=4, out_hbm=(0,))(*res_rims, filter_taps)
     sums = scatter_sum(sums, batches)
     return (sublayer_result[None], signal_adjoint[None], sums[:taps], sums[taps])

time: 174 us -> 174 us (level)
  local copies, waits for them, and re-layouts: 10.2 us -> 7.77 us
  starting transfers between devices: 72.8 us -> 75.1 us
    unnamed x37 -> x39, local copies, waits for them, and re-layouts: 7.79 us -> 6.03 us
    pallas_call x8 -> x9, Pallas kernels: 36.5 us -> 37.7 us  [run(): return call(*args)]
  transfers between devices with their start and end apart: 37 -> 37, of which waited for: 23 -> 20; matrix products, arithmetic and copies ran while one was open for 1% -> 0% of each run, Pallas kernels for 5% -> 11%
where the time goes in v1:
time: 174 us; the launch traced here: 173 us
  starting transfers between devices  75.1 us (43%)
  waiting for transfers between devices  51.4 us (30%)
  Pallas kernels  37.7 us (22%)
  local copies, waits for them, and re-layouts  7.77 us (4%)
    pallas_call x9, Pallas kernels, run(): return call(*args)  37.7 us
    ppermute x12, starting transfers between devices, move_z4(): return lax.ppermute(a, 'tm', pairs)  31.1 us
    ppermute x10, starting transfers between devices, move_zy(): return lax.ppermute(a, 'tm', pairs)  17.7 us
    ppermute x10, waiting for transfers between devices, move_zy(): return lax.ppermute(a, 'tm', pairs)  14.1 us
    ppermute x2, waiting for transfers between devices, rims(): right = lax.ppermute(head, 'tm', [(i + 1, i) for i in range(ends)])  11.9 us
    ppermute x12, waiting for transfers between devices, move_z4(): return lax.ppermute(a, 'tm', pairs)  11.3 us
    ppermute x9, starting transfers between devices, move_x(): return lax.ppermute(a, 'tm', pairs)  10.6 us
    ppermute x2, starting transfers between devices, rims(): left = lax.ppermute(tail, 'tm', [(i, i + 1) for i in range(ends)])  9.83 us
  transfers between devices with their start and end apart: 37, of which 20 were waited for; matrix products, arithmetic and copies ran while one was open for 0% of the time, Pallas kernels for 11%

profile of v1, /device:TPU:30, one launch (start us, length us, event | category | flops | bytes accessed | tf_op | source)
XLA Modules:
  0.0 173.4 jit_solution(1467453791196355200)
XLA Ops:
  2.2 3.4 %shard_map.102 = (bf16[192,128]{1,0:T(8,128)(2,1)S(1)}, bf16[192,128]{1,0:T(8,128)(2,1)S(1)}, bf16[192,128]{1,0:T(8,128)(2,1)S(1)}, bf16[192,128]{1,0:T(8,128)(2...) custom-call(s32[1]{0:T(128)} %bitcast.idx, ...), custom_call_target="tpu_custom_call" | custom-call | tf_op jit(solution)/shard_map/pallas_call | solution.py:80
  5.6 3.3 %collective-permute-start = (bf16[192,128]{1,0:T(8,128)(2,1)S(1)}, bf16[192,128]{1,0:T(8,128)(2,1)S(1)}, u32[]{:S(2)}, u32[]{:S(2)}) collective-permute-start(bf16[192,128]{1,0:T(8,128)(2,1)S(1)} %get-tuple-element.37), channel_id=1, source_target_pairs={{0,32},{2,34},{4,36},{6,38},{8,40},{10,42},{12,44},{14,46},{16,48}... | collective-permute-start | bytes 147464 | tf_op jit(solution)/shard_map/ppermute | solution.py:32
  8.9 5.4 %collective-permute-start.1 = (bf16[192,128]{1,0:T(8,128)(2,1)S(1)}, bf16[192,128]{1,0:T(8,128)(2,1)S(1)}, u32[]{:S(2)}, u32[]{:S(2)}) collective-permute-start(bf16[192,128]{1,0:T(8,128)(2,1)S(1)} %get-tuple-element.38), channel_id=1, source_target_pairs={{0,64},{2,66},{4,68},{6,70},{8,72},{10,74},{12,76},{14,78},{16,80}... | collective-permute-start | bytes 147464 | tf_op jit(solution)/shard_map/ppermute | solution.py:32
  17.0 3.5 %collective-permute-start.6 = (bf16[15,1536]{1,0:T(8,128)(2,1)S(1)}, bf16[15,1536]{1,0:T(8,128)(2,1)S(1)}, u32[]{:S(2)}, u32[]{:S(2)}) collective-permute-start(bf16[15,1536]{1,0:T(8,128)(2,1)S(1)} %get-tuple-element.73), channel_id=1, source_target_pairs={{0,2},{2,4},{4,6},{6,8},{8,10},{10,12},{12,14},{14,16},{16,18},{18... | collective-permute-start | bytes 138248 | tf_op jit(solution)/shard_map/ppermute | solution.py:358
  20.5 3.8 %collective-permute-start.7 = (bf16[15,1536]{1,0:T(8,128)(2,1)S(1)}, bf16[15,1536]{1,0:T(8,128)(2,1)S(1)}, u32[]{:S(2)}, u32[]{:S(2)}) collective-permute-start(bf16[15,1536]{1,0:T(8,128)(2,1)S(1)} %get-tuple-element.72), channel_id=1, source_target_pairs={{2,0},{4,2},{6,4},{8,6},{10,8},{12,10},{14,12},{16,14},{18,16},{20... | collective-permute-start | bytes 138248 | tf_op jit(solution)/shard_map/ppermute | solution.py:359
  24.5 6.5 %collective-permute-done.7.right = bf16[15,1536]{1,0:T(8,128)(2,1)S(1)} collective-permute-done((bf16[15,1536]{1,0:T(8,128)(2,1)S(1)}, bf16[15,1536]{1,0:T(8,128)(2,1)S(1)}, u32[]{:S(2)}, u32[]{:S(2)}) %collective-permute-start.7) | collective-permute-done | bytes 46112 | tf_op jit(solution)/shard_map/ppermute | solution.py:359
  31.0 4.5 %shard_map.103 = (bf16[192,128]{1,0:T(8,128)(2,1)S(1)}, bf16[192,128]{1,0:T(8,128)(2,1)S(1)}, bf16[192,128]{1,0:T(8,128)(2,1)S(1)}, bf16[192,128]{1,0:T(8,128)(2,1)S(1)}, f32[128,1536]{1,0:T(8,128)S(1)}) custom-call(s32[1]{0:T(128)} %bitcast.idx, bf16[15,1536]{1,0:T(8,128)(2,1)S(1)} %collective-permute-done.6.left, bf16[128,1536]{1,0:T(8,128)(2,1)S(1)} %bitcast.16, ...), custom_call_target="tpu_custom_call" | custom-call | tf_op jit(solution)/shard_map/pallas_call | solution.py:80
  46.9 3.1 %collective-permute-start.13 = (bf16[192,512]{1,0:T(8,128)(2,1)S(1)}, bf16[192,512]{1,0:T(8,128)(2,1)S(1)}, u32[]{:S(2)}, u32[]{:S(2)}) collective-permute-start(bf16[192,512]{1,0:T(8,128)(2,1)S(1)} %constant_dynamic-update-slice_fusion.4.refs_4_.refs_6_), channel_id=1, source_target_pairs={{0,18},{2,16},{4,22},{6,20},{8,26},{10,24},{12,30},{14,28},{16,2},... | collective-permute-start | bytes 589832 | tf_op jit(solution)/shard_map/ppermute | solution.py:48
  52.7 3.5 %collective-permute-done.12.refs_6_.refs_8_ = bf16[192,512]{1,0:T(8,128)(2,1)S(1)} collective-permute-done((bf16[192,512]{1,0:T(8,128)(2,1)S(1)}, bf16[192,512]{1,0:T(8,128)(2,1)S(1)}, u32[]{:S(2)}, u32[]{:S(2)}) %collective-permute-start.12) | collective-permute-done | bytes 196640 | tf_op jit(solution)/shard_map/ppermute | solution.py:48
  56.1 8.2 %shard_map.104 = (f32[4,2,512]{2,1,0:T(2,128)S(1)}, f32[4,288,512]{2,1,0:T(8,128)S(1)}) custom-call(bf16[192,512]{1,0:T(8,128)(2,1)S(1)} %constant_dynamic-update-slice_fusion.refs_0_.refs_2_, bf16[192,512]{1,0:T(8,128)(2,1)S(1)} %collective-permute-done.3.refs_1_.refs_3_, bf16[192,512]{1,0:T(8,128)(2,1)S(1)} %collective-permute-done.4.refs_2_.refs_4_, ...), custom_call_target="tpu_custom_call" | custom-call | tf_op jit(solution)/shard_map/pallas_call | solution.py:80
  65.0 3.1 %collective-permute-done.14 = f32[4,2,512]{2,1,0:T(2,128)S(1)} collective-permute-done((f32[4,2,512]{2,1,0:T(2,128)S(1)}, f32[4,2,512]{2,1,0:T(2,128)S(1)}, u32[]{:S(2)}, u32[]{:S(2)}) %collective-permute-start.14) | collective-permute-done | bytes 16416 | tf_op jit(solution)/shard_map/ppermute | solution.py:48
  70.0 3.7 %collective-permute-done.15.te1.refs_1_ = f32[4,2,512]{2,1,0:T(2,128)S(1)} collective-permute-done((f32[4,2,512]{2,1,0:T(2,128)S(1)}, f32[4,2,512]{2,1,0:T(2,128)S(1)}, u32[]{:S(2)}, u32[]{:S(2)}) %collective-permute-start.15) | collective-permute-done | bytes 16416 | tf_op jit(solution)/shard_map/ppermute | solution.py:48
  78.9 10.4 %shard_map.106 = (bf16[192,512]{1,0:T(8,128)(2,1)S(1)}, bf16[192,512]{1,0:T(8,128)(2,1)S(1)}, bf16[192,512]{1,0:T(8,128)(2,1)S(1)}, bf16[192,512]{1,0:T(8,128)(2,1)S(1)}) custom-call(f32[4,2,512]{2,1,0:T(2,128)S(1)} %maximum_add_fusion.te0.refs_0_, f32[4,2,512]{2,1,0:T(2,128)S(1)} %collective-permute-done.15.te1.refs_1_, ...), custom_call_target="tpu_custom_call" | custom-call | tf_op jit(solution)/shard_map/pallas_call | solution.py:80
  89.4 2.9 %collective-permute-start.20 = (bf16[192,512]{1,0:T(8,128)(2,1)S(1)}, bf16[192,512]{1,0:T(8,128)(2,1)S(1)}, u32[]{:S(2)}, u32[]{:S(2)}) collective-permute-start(bf16[192,512]{1,0:T(8,128)(2,1)S(1)} %get-tuple-element.53), channel_id=1, source_target_pairs={{0,8},{2,10},{4,12},{6,14},{8,0},{10,2},{12,4},{14,6},{16,24},{18,... | collective-permute-start | bytes 589832 | tf_op jit(solution)/shard_map/ppermute | solution.py:40
  93.5 4.9 %collective-permute-done.19.refs_5_ = bf16[192,512]{1,0:T(8,128)(2,1)S(1)} collective-permute-done((bf16[192,512]{1,0:T(8,128)(2,1)S(1)}, bf16[192,512]{1,0:T(8,128)(2,1)S(1)}, u32[]{:S(2)}, u32[]{:S(2)}) %collective-permute-start.19) | collective-permute-done | bytes 196640 | tf_op jit(solution)/shard_map/ppermute | solution.py:40
  101.7 4.7 %collective-permute-start.23 = (bf16[384,128]{1,0:T(8,128)(2,1)S(1)}, bf16[384,128]{1,0:T(8,128)(2,1)S(1)}, u32[]{:S(2)}, u32[]{:S(2)}) collective-permute-start(bf16[384,128]{1,0:T(8,128)(2,1)S(1)} %get-tuple-element.57), channel_id=1, source_target_pairs={{0,64},{2,66},{4,68},{6,70},{8,72},{10,74},{12,76},{14,78},{16,80}... | collective-permute-start | bytes 294920 | tf_op jit(solution)/shard_map/ppermute | solution.py:32
  110.2 3.5 %collective-permute-done.24.b3 = bf16[384,128]{1,0:T(8,128)(2,1)S(1)} collective-permute-done((bf16[384,128]{1,0:T(8,128)(2,1)S(1)}, bf16[384,128]{1,0:T(8,128)(2,1)S(1)}, u32[]{:S(2)}, u32[]{:S(2)}) %collective-permute-start.24) | collective-permute-done | bytes 98336 | tf_op jit(solution)/shard_map/ppermute | solution.py:32
  119.8 4.0 %shard_map.109 = (bf16[128,1536]{1,0:T(8,128)(2,1)S(1)}, bf16[128,1536]{1,0:T(8,128)(2,1)}, f32[2,32,768]{2,1,0:T(8,128)S(1)}, bf16[15,1536]{1,0:T(8,128)(2,1)S(1)}, bf16[15,1536]{1,0:T(8,128)(2,1)S(1)}) custom-call(bf16[256,1536]{1,0:T(8,128)(2,1)S(1)} %shard_map.108.part, bf16[256,1536]{1,0:T(8,128)(2,1)S(1)} %collective-permute-done.25.other, ...), custom_call_target="tpu_custom_call" | custom-call | tf_op jit(solution)/shard_map/pallas_call | solution.py:80
  125.9 4.8 %collective-permute-done.28 = f32[32,768]{1,0:T(8,128)S(1)} collective-permute-done((f32[32,768]{1,0:T(8,128)S(1)}, f32[32,768]{1,0:T(8,128)S(1)}, u32[]{:S(2)}, u32[]{:S(2)}) %collective-permute-start.28) | collective-permute-done | bytes 98336 | tf_op jit(solution)/shard_map/ppermute | solution.py:374
  130.8 2.9 %collective-permute-start.30 = (f32[32,192]{1,0:T(8,128)S(1)}, f32[32,192]{1,0:T(8,128)S(1)}, u32[]{:S(2)}, u32[]{:S(2)}) collective-permute-start(f32[32,192]{1,0:T(8,128)S(1)} %get-tuple-element.76), channel_id=1, source_target_pairs={{0,64},{2,66},{4,68},{6,70},{8,72},{10,74},{12,76},{14,78},{16,80}... | collective-permute-start | bytes 73736 | tf_op jit(solution)/shard_map/ppermute | solution.py:32
  149.3 6.3 %collective-permute-start.26 = (bf16[15,1536]{1,0:T(8,128)(2,1)}, bf16[15,1536]{1,0:T(8,128)(2,1)S(1)}, u32[]{:S(2)}, u32[]{:S(2)}) collective-permute-start(bf16[15,1536]{1,0:T(8,128)(2,1)} %copy-done.15), channel_id=1, source_target_pairs={{0,2},{2,4},{4,6},{6,8},{8,10},{10,12},{12,14},{14,16},{16,18},{18... | collective-permute-start | bytes 138248 | tf_op jit(solution)/shard_map/ppermute | solution.py:358
  157.7 3.2 %collective-permute-start.36 = (f32[32,12]{1,0:T(8,128)S(1)}, f32[32,12]{1,0:T(8,128)S(1)}, u32[]{:S(2)}, u32[]{:S(2)}) collective-permute-start(f32[32,12]{1,0:T(8,128)S(1)} %constant_dynamic-slice_fusion), channel_id=1, source_target_pairs={{0,2},{2,0},{4,6},{6,4},{8,10},{10,8},{12,14},{14,12},{16,18},{18,... | collective-permute-start | bytes 4616 | tf_op jit(solution)/shard_map/ppermute | solution.py:48
  160.9 5.4 %collective-permute-done.27.right = bf16[15,1536]{1,0:T(8,128)(2,1)S(1)} collective-permute-done((bf16[15,1536]{1,0:T(8,128)(2,1)}, bf16[15,1536]{1,0:T(8,128)(2,1)S(1)}, u32[]{:S(2)}, u32[]{:S(2)}) %collective-permute-start.27) | collective-permute-done | bytes 46112 | tf_op jit(solution)/shard_map/ppermute | solution.py:359
  167.3 4.8 %shard_map.110 = bf16[128,1536]{1,0:T(8,128)(2,1)} custom-call(bf16[15,1536]{1,0:T(8,128)(2,1)S(1)} %collective-permute-done.26.left, bf16[128,1536]{1,0:T(8,128)(2,1)S(1)} %copy-done.7, bf16[15,1536]{1,0:T(8,128)(2,1)S(1)} %collective-permute-done.27.right, f32[31,1536]{1,0:T(8,128)S(1)} %copy-done.5), custom_call_target="tpu_custom_call" | custom-call | tf_op jit(solution)/shard_map/pallas_call | solution.py:80
  (115 shorter events, 62.6 us)
Async XLA Ops:
  5.6 32.4 %collective-permute-start = (bf16[192,128]{1,0:T(8,128)(2,1)S(1)}, bf16[192,128]{1,0:T(8,128)(2,1)S(1)}, u32[]{:S(2)}, u32[]{:S(2)}) collective-permute-start(bf16[192,128]{1,0:T(8,128)(2,1)S(1)} %get-tuple-element.37), channel_id=1, source_target_pairs={{0,32},{2,34},{4,36},{6,38},{8,40},{10,42},{12,44},{14,46},{16,48}... | collective-permute-start | bytes 147464 | tf_op jit(solution)/shard_map/ppermute | solution.py:32
  8.9 31.9 %collective-permute-start.1 = (bf16[192,128]{1,0:T(8,128)(2,1)S(1)}, bf16[192,128]{1,0:T(8,128)(2,1)S(1)}, u32[]{:S(2)}, u32[]{:S(2)}) collective-permute-start(bf16[192,128]{1,0:T(8,128)(2,1)S(1)} %get-tuple-element.38), channel_id=1, source_target_pairs={{0,64},{2,66},{4,68},{6,70},{8,72},{10,74},{12,76},{14,78},{16,80}... | collective-permute-start | bytes 147464 | tf_op jit(solution)/shard_map/ppermute | solution.py:32
  14.3 26.5 %collective-permute-start.2 = (bf16[192,128]{1,0:T(8,128)(2,1)S(1)}, bf16[192,128]{1,0:T(8,128)(2,1)S(1)}, u32[]{:S(2)}, u32[]{:S(2)}) collective-permute-start(bf16[192,128]{1,0:T(8,128)(2,1)S(1)} %get-tuple-element.39), channel_id=1, source_target_pairs={{0,96},{2,98},{4,100},{6,102},{8,104},{10,106},{12,108},{14,110},{... | collective-permute-start | bytes 147464 | tf_op jit(solution)/shard_map/ppermute | solution.py:32
  20.5 10.5 %collective-permute-start.7 = (bf16[15,1536]{1,0:T(8,128)(2,1)S(1)}, bf16[15,1536]{1,0:T(8,128)(2,1)S(1)}, u32[]{:S(2)}, u32[]{:S(2)}) collective-permute-start(bf16[15,1536]{1,0:T(8,128)(2,1)S(1)} %get-tuple-element.72), channel_id=1, source_target_pairs={{2,0},{4,2},{6,4},{8,6},{10,8},{12,10},{14,12},{16,14},{18,16},{20... | collective-permute-start | bytes 138248 | tf_op jit(solution)/shard_map/ppermute | solution.py:359
  35.9 8.2 %collective-permute-start.9 = (bf16[192,128]{1,0:T(8,128)(2,1)S(1)}, bf16[192,128]{1,0:T(8,128)(2,1)S(1)}, u32[]{:S(2)}, u32[]{:S(2)}) collective-permute-start(bf16[192,128]{1,0:T(8,128)(2,1)S(1)} %get-tuple-element.43), channel_id=1, source_target_pairs={{0,64},{2,66},{4,68},{6,70},{8,72},{10,74},{12,76},{14,78},{16,80}... | collective-permute-start | bytes 147464 | tf_op jit(solution)/shard_map/ppermute | solution.py:32
  41.0 9.0 %collective-permute-start.4 = (bf16[192,512]{1,0:T(8,128)(2,1)S(1)}, bf16[192,512]{1,0:T(8,128)(2,1)S(1)}, u32[]{:S(2)}, u32[]{:S(2)}) collective-permute-start(bf16[192,512]{1,0:T(8,128)(2,1)S(1)} %constant_dynamic-update-slice_fusion.refs_0_.refs_2_), channel_id=1, source_target_pairs={{0,8},{2,10},{4,12},{6,14},{8,0},{10,2},{12,4},{14,6},{16,24},{18,... | collective-permute-start | bytes 589832 | tf_op jit(solution)/shard_map/ppermute | solution.py:40
  42.0 8.6 %collective-permute-start.5 = (bf16[192,512]{1,0:T(8,128)(2,1)S(1)}, bf16[192,512]{1,0:T(8,128)(2,1)S(1)}, u32[]{:S(2)}, u32[]{:S(2)}) collective-permute-start(bf16[192,512]{1,0:T(8,128)(2,1)S(1)} %constant_dynamic-update-slice_fusion.refs_0_.refs_2_), channel_id=1, source_target_pairs={{0,12},{2,14},{4,0},{6,2},{8,4},{10,6},{12,8},{14,10},{16,28},{18,... | collective-permute-start | bytes 589832 | tf_op jit(solution)/shard_map/ppermute | solution.py:40
  44.9 7.8 %collective-permute-start.11 = (bf16[192,512]{1,0:T(8,128)(2,1)S(1)}, bf16[192,512]{1,0:T(8,128)(2,1)S(1)}, u32[]{:S(2)}, u32[]{:S(2)}) collective-permute-start(bf16[192,512]{1,0:T(8,128)(2,1)S(1)} %constant_dynamic-update-slice_fusion.4.refs_4_.refs_6_), channel_id=1, source_target_pairs={{0,16},{2,18},{4,20},{6,22},{8,24},{10,26},{12,28},{14,30},{16,0},... | collective-permute-start | bytes 589832 | tf_op jit(solution)/shard_map/ppermute | solution.py:48
  46.2 9.9 %collective-permute-start.12 = (bf16[192,512]{1,0:T(8,128)(2,1)S(1)}, bf16[192,512]{1,0:T(8,128)(2,1)S(1)}, u32[]{:S(2)}, u32[]{:S(2)}) collective-permute-start(bf16[192,512]{1,0:T(8,128)(2,1)S(1)} %constant_dynamic-update-slice_fusion.4.refs_4_.refs_6_), channel_id=1, source_target_pairs={{0,2},{2,0},{4,6},{6,4},{8,10},{10,8},{12,14},{14,12},{16,18},{18,... | collective-permute-start | bytes 589832 | tf_op jit(solution)/shard_map/ppermute | solution.py:48
  46.9 9.3 %collective-permute-start.13 = (bf16[192,512]{1,0:T(8,128)(2,1)S(1)}, bf16[192,512]{1,0:T(8,128)(2,1)S(1)}, u32[]{:S(2)}, u32[]{:S(2)}) collective-permute-start(bf16[192,512]{1,0:T(8,128)(2,1)S(1)} %constant_dynamic-update-slice_fusion.4.refs_4_.refs_6_), channel_id=1, source_target_pairs={{0,18},{2,16},{4,22},{6,20},{8,26},{10,24},{12,30},{14,28},{16,2},... | collective-permute-start | bytes 589832 | tf_op jit(solution)/shard_map/ppermute | solution.py:48
  73.9 18.5 %collective-permute-start.16 = (bf16[192,512]{1,0:T(8,128)(2,1)S(1)}, bf16[192,512]{1,0:T(8,128)(2,1)S(1)}, u32[]{:S(2)}, u32[]{:S(2)}) collective-permute-start(bf16[192,512]{1,0:T(8,128)(2,1)S(1)} %get-tuple-element.48), channel_id=1, source_target_pairs={{0,16},{2,18},{4,20},{6,22},{8,24},{10,26},{12,28},{14,30},{16,0},... | collective-permute-start | bytes 589832 | tf_op jit(solution)/shard_map/ppermute | solution.py:48
  74.5 19.0 %collective-permute-start.17 = (bf16[192,512]{1,0:T(8,128)(2,1)S(1)}, bf16[192,512]{1,0:T(8,128)(2,1)S(1)}, u32[]{:S(2)}, u32[]{:S(2)}) collective-permute-start(bf16[192,512]{1,0:T(8,128)(2,1)S(1)} %get-tuple-element.49), channel_id=1, source_target_pairs={{0,2},{2,0},{4,6},{6,4},{8,10},{10,8},{12,14},{14,12},{16,18},{18,... | collective-permute-start | bytes 589832 | tf_op jit(solution)/shard_map/ppermute | solution.py:48
  76.2 17.3 %collective-permute-start.18 = (bf16[192,512]{1,0:T(8,128)(2,1)S(1)}, bf16[192,512]{1,0:T(8,128)(2,1)S(1)}, u32[]{:S(2)}, u32[]{:S(2)}) collective-permute-start(bf16[192,512]{1,0:T(8,128)(2,1)S(1)} %get-tuple-element.50), channel_id=1, source_target_pairs={{0,18},{2,16},{4,22},{6,20},{8,26},{10,24},{12,30},{14,28},{16,2},... | collective-permute-start | bytes 589832 | tf_op jit(solution)/shard_map/ppermute | solution.py:48
  89.3 9.1 %collective-permute-start.19 = (bf16[192,512]{1,0:T(8,128)(2,1)S(1)}, bf16[192,512]{1,0:T(8,128)(2,1)S(1)}, u32[]{:S(2)}, u32[]{:S(2)}) collective-permute-start(bf16[192,512]{1,0:T(8,128)(2,1)S(1)} %get-tuple-element.52), channel_id=1, source_target_pairs={{0,12},{2,14},{4,0},{6,2},{8,4},{10,6},{12,8},{14,10},{16,28},{18,... | collective-permute-start | bytes 589832 | tf_op jit(solution)/shard_map/ppermute | solution.py:40
  89.4 9.0 %collective-permute-start.20 = (bf16[192,512]{1,0:T(8,128)(2,1)S(1)}, bf16[192,512]{1,0:T(8,128)(2,1)S(1)}, u32[]{:S(2)}, u32[]{:S(2)}) collective-permute-start(bf16[192,512]{1,0:T(8,128)(2,1)S(1)} %get-tuple-element.53), channel_id=1, source_target_pairs={{0,8},{2,10},{4,12},{6,14},{8,0},{10,2},{12,4},{14,6},{16,24},{18,... | collective-permute-start | bytes 589832 | tf_op jit(solution)/shard_map/ppermute | solution.py:40
  99.4 8.6 %collective-permute-start.22 = (bf16[384,128]{1,0:T(8,128)(2,1)S(1)}, bf16[384,128]{1,0:T(8,128)(2,1)S(1)}, u32[]{:S(2)}, u32[]{:S(2)}) collective-permute-start(bf16[384,128]{1,0:T(8,128)(2,1)S(1)} %get-tuple-element.56), channel_id=1, source_target_pairs={{0,96},{2,98},{4,100},{6,102},{8,104},{10,106},{12,108},{14,110},{... | collective-permute-start | bytes 294920 | tf_op jit(solution)/shard_map/ppermute | solution.py:32
  101.7 8.5 %collective-permute-start.23 = (bf16[384,128]{1,0:T(8,128)(2,1)S(1)}, bf16[384,128]{1,0:T(8,128)(2,1)S(1)}, u32[]{:S(2)}, u32[]{:S(2)}) collective-permute-start(bf16[384,128]{1,0:T(8,128)(2,1)S(1)} %get-tuple-element.57), channel_id=1, source_target_pairs={{0,64},{2,66},{4,68},{6,70},{8,72},{10,74},{12,76},{14,78},{16,80}... | collective-permute-start | bytes 294920 | tf_op jit(solution)/shard_map/ppermute | solution.py:32
  130.8 8.4 %collective-permute-start.30 = (f32[32,192]{1,0:T(8,128)S(1)}, f32[32,192]{1,0:T(8,128)S(1)}, u32[]{:S(2)}, u32[]{:S(2)}) collective-permute-start(f32[32,192]{1,0:T(8,128)S(1)} %get-tuple-element.76), channel_id=1, source_target_pairs={{0,64},{2,66},{4,68},{6,70},{8,72},{10,74},{12,76},{14,78},{16,80}... | collective-permute-start | bytes 73736 | tf_op jit(solution)/shard_map/ppermute | solution.py:32
  145.0 12.5 %collective-permute-start.34 = (f32[32,24]{1,0:T(8,128)S(1)}, f32[32,24]{1,0:T(8,128)S(1)}, u32[]{:S(2)}, u32[]{:S(2)}) collective-permute-start(f32[32,24]{1,0:T(8,128)S(1)} %get-tuple-element.79), channel_id=1, source_target_pairs={{0,8},{2,10},{4,12},{6,14},{8,0},{10,2},{12,4},{14,6},{16,24},{18,... | collective-permute-start | bytes 9224 | tf_op jit(solution)/shard_map/ppermute | solution.py:40
  146.0 11.5 %collective-permute-start.35 = (f32[32,24]{1,0:T(8,128)S(1)}, f32[32,24]{1,0:T(8,128)S(1)}, u32[]{:S(2)}, u32[]{:S(2)}) collective-permute-start(f32[32,24]{1,0:T(8,128)S(1)} %get-tuple-element.78), channel_id=1, source_target_pairs={{0,12},{2,14},{4,0},{6,2},{8,4},{10,6},{12,8},{14,10},{16,28},{18,... | collective-permute-start | bytes 9224 | tf_op jit(solution)/shard_map/ppermute | solution.py:40
  148.3 9.2 %collective-permute-start.33 = (f32[32,24]{1,0:T(8,128)S(1)}, f32[32,24]{1,0:T(8,128)S(1)}, u32[]{:S(2)}, u32[]{:S(2)}) collective-permute-start(f32[32,24]{1,0:T(8,128)S(1)} %get-tuple-element.77), channel_id=1, source_target_pairs={{0,4},{2,6},{4,8},{6,10},{8,12},{10,14},{12,0},{14,2},{16,20},{18,... | collective-permute-start | bytes 9224 | tf_op jit(solution)/shard_map/ppermute | solution.py:40
  149.3 11.7 %collective-permute-start.26 = (bf16[15,1536]{1,0:T(8,128)(2,1)}, bf16[15,1536]{1,0:T(8,128)(2,1)S(1)}, u32[]{:S(2)}, u32[]{:S(2)}) collective-permute-start(bf16[15,1536]{1,0:T(8,128)(2,1)} %copy-done.15), channel_id=1, source_target_pairs={{0,2},{2,4},{4,6},{6,8},{8,10},{10,12},{12,14},{14,16},{16,18},{18... | collective-permute-start | bytes 138248 | tf_op jit(solution)/shard_map/ppermute | solution.py:358
  155.6 10.7 %collective-permute-start.27 = (bf16[15,1536]{1,0:T(8,128)(2,1)}, bf16[15,1536]{1,0:T(8,128)(2,1)S(1)}, u32[]{:S(2)}, u32[]{:S(2)}) collective-permute-start(bf16[15,1536]{1,0:T(8,128)(2,1)} %copy-done.14), channel_id=1, source_target_pairs={{2,0},{4,2},{6,4},{8,6},{10,8},{12,10},{14,12},{16,14},{18,16},{20... | collective-permute-start | bytes 138248 | tf_op jit(solution)/shard_map/ppermute | solution.py:359
  157.7 14.4 %collective-permute-start.36 = (f32[32,12]{1,0:T(8,128)S(1)}, f32[32,12]{1,0:T(8,128)S(1)}, u32[]{:S(2)}, u32[]{:S(2)}) collective-permute-start(f32[32,12]{1,0:T(8,128)S(1)} %constant_dynamic-slice_fusion), channel_id=1, source_target_pairs={{0,2},{2,0},{4,6},{6,4},{8,10},{10,8},{12,14},{14,12},{16,18},{18,... | collective-permute-start | bytes 4616 | tf_op jit(solution)/shard_map/ppermute | solution.py:48
  (29 other events, 378.8 us)

commit v2 on v1

--- a/solution.py
+++ b/solution.py
@@ -24,28 +24,35 @@
     return ((z4 % 4) * 2 + z2) * 8 + (x % 4) * 2 + yh
 
 
-def move_z4(a, s):
+def send(a, axis, pairs, core=None):
+    if core is None:
+        return lax.ppermute(a, axis, pairs)
+    cores = lax.axis_size("mp")
+    return lax.ppermute(a, (axis, "mp"), [(i * cores + core, j * cores + core) for i, j in pairs])
+
+
+def move_z4(a, s, core=None):
     pairs = []
     for t in range(TM):
         z4, z2, x, yh = _split(t)
         pairs.append((t, _join(z4 + s, z2, x, yh)))
-    return lax.ppermute(a, "tm", pairs)
-
-
-def move_x(a, s):
+    return send(a, "tm", pairs, core)
+
+
+def move_x(a, s, core=None):
     pairs = []
     for t in range(TM):
         z4, z2, x, yh = _split(t)
         pairs.append((t, _join(z4, z2, x + s, yh)))
-    return lax.ppermute(a, "tm", pairs)
-
-
-def move_zy(a, m):
+    return send(a, "tm", pairs, core)
+
+
+def move_zy(a, m, core=None):
     pairs = []
     for t in range(TM):
         z4, z2, x, yh = _split(t)
         pairs.append((t, _join(z4, z2 ^ (m & 1), x, yh ^ (m >> 1))))
-    return lax.ppermute(a, "tm", pairs)
+    return send(a, "tm", pairs, core)
 
 
 def ordered(move, shifts):
@@ -89,7 +96,7 @@
 
 
 def front_kernel(
-    idx, sharp, factor, x_hbm, w_hbm, o0, o1, o2, o3, qpay, qhat_o, khat_o, rad_o, pay, x, w, sem, *, heads, hs
+    idx, factor, x_hbm, w_hbm, o0, o1, o2, o3, qhat_o, khat_o, rad_o, pay, x, w, sem, *, heads, hs
 ):
     x_copy = pltpu.make_async_copy(x_hbm, x, sem.at[0])
     x_copy.start()
@@ -122,7 +129,6 @@
         rad_o[heads + h : heads + h + 1] = kr
         pay[h, 0:hs] = kh.astype(BF16)
         pay[h, hs : 2 * hs] = vt[lo:hi].astype(BF16)
-        qpay[h] = (qh * (sharp[h] / math.sqrt(hs))).astype(BF16)
     for s, o in enumerate((o0, o1, o2, o3)):
         o[...] = pay[lax.rem(idx[0] + s, 4)]
 
@@ -154,19 +160,24 @@
     lax.fori_loop(0, out.shape[1] // 128, chunk, 0)
 
 
-def send_kernel(idx, left, own, right, taps, qpay, wf, o0, o1, o2, o3, gres, pad, g_s, *, hs):
+def send_kernel(idx, sharp, left, own, right, taps, qhat, wf, o0, o1, o2, o3, gres_o, pad, g_s, gres, *, hs):
     fill_pad(pad, left, own, right)
     conv_rows(pad, taps, gres, own.shape[0], True)
+    gres_o[...] = gres[...]
     gt = dotf(wf[...], gres[...].astype(BF16), 1, 1).astype(BF16)
     for h in range(4):
-        g_s[h] = gt[h * hs : (h + 1) * hs]
+        g_s[h, 0:hs] = (qhat[h * hs : (h + 1) * hs] * (sharp[h] / math.sqrt(hs))).astype(BF16)
+        g_s[h, hs : 2 * hs] = gt[h * hs : (h + 1) * hs]
     for s, o in enumerate((o0, o1, o2, o3)):
-        at = lax.rem(idx[0] + s, 4)
-        o[0:hs] = qpay[at]
-        o[hs : 2 * hs] = g_s[at]
-
-
-def tail_kernel(part, other, x, factor, left, own, right, gres, res_o, sig_o, sums, first, last, pad, resf, gain, *, rows, taps):
+        o[...] = g_s[lax.rem(idx[0] + s, 4)]
+
+
+def tail_kernel(
+    core, part, other, x, factor, left, own, right, gres_hbm, res_o, sig_o, sums, first, last, pad, resf, gain, gres, sem,
+    *, rows, taps, red,
+):
+    fetch = pltpu.make_async_copy(gres_hbm, gres, sem)
+    fetch.start()
     fill_pad(pad, left, own, right)
     reach = taps // 2
     total = part[0:rows].astype(F32) + other[0:rows].astype(F32)
@@ -187,31 +198,44 @@
     scaled = grad * f
     m1 = jnp.mean(scaled, axis=-1, keepdims=True)
     m2 = jnp.mean(prod * f, axis=-1, keepdims=True)
+    fetch.wait()
     sig_o[...] = (gres[...] + (scaled - m1 - unit * m2) * inv).astype(BF16)
     half = sums.shape[2] // 128
 
-    for h in range(2):
-
-        def chunk(c, _):
-            lanes = pl.ds(pl.multiple_of((h * half + c) * 128, 128), 128)
-            to = pl.ds(pl.multiple_of(c * 128, 128), 128)
-            r = resf[:, lanes]
-            for phase in range(8):
-                shifted = pad[phase : phase + rows + 24, lanes]
-                for j in range(taps):
-                    at = 16 + reach - j
-                    if at % 8 == phase:
-                        moved = shifted[at - phase : at - phase + rows]
-                        sums[h, j : j + 1, to] = jnp.sum(r * moved, axis=0, keepdims=True)
-            sums[h, taps : taps + 1, to] = gain[:, lanes]
-            return 0
-
-        lax.fori_loop(0, half, chunk, 0)
-
-
-def out_kernel(left, own, right, taps, out, pad):
-    fill_pad(pad, left, own, right)
-    conv_rows(pad, taps, out, own.shape[0], False)
+    @pl.when(core[0] == red)
+    def _():
+        for h in range(2):
+
+            def chunk(c, _):
+                lanes = pl.ds(pl.multiple_of((h * half + c) * 128, 128), 128)
+                to = pl.ds(pl.multiple_of(c * 128, 128), 128)
+                r = resf[:, lanes]
+                for phase in range(8):
+                    shifted = pad[phase : phase + rows + 24, lanes]
+                    for j in range(taps):
+                        at = 16 + reach - j
+                        if at % 8 == phase:
+                            moved = shifted[at - phase : at - phase + rows]
+                            sums[h, j : j + 1, to] = jnp.sum(r * moved, axis=0, keepdims=True)
+                sums[h, taps : taps + 1, to] = gain[:, lanes]
+                return 0
+
+            lax.fori_loop(0, half, chunk, 0)
+
+    @pl.when(core[0] != red)
+    def _():
+        sums[...] = jnp.zeros(sums.shape, F32)
+
+
+def out_kernel(core, left, own, right, taps, out, pad):
+    @pl.when(core[0] == 0)
+    def _():
+        fill_pad(pad, left, own, right)
+        conv_rows(pad, taps, out, own.shape[0], False)
+
+    @pl.when(core[0] != 0)
+    def _():
+        out[...] = jnp.zeros(out.shape, BF16)
 
 
 def to_rows(a):
@@ -353,10 +377,10 @@
     out[lanes : 2 * lanes] = normed.astype(BF16)
 
 
-def rims(cells, head, tail):
+def rims(cells, head, tail, core=None):
     ends = TM - 1
-    left = lax.ppermute(tail, "tm", [(i, i + 1) for i in range(ends)])
-    right = lax.ppermute(head, "tm", [(i + 1, i) for i in range(ends)])
+    left = send(tail, "tm", [(i, i + 1) for i in range(ends)], core)
+    right = send(head, "tm", [(i + 1, i) for i in range(ends)], core)
     return left, cells, right
 
 
@@ -365,26 +389,26 @@
     return lambda i: lax.dynamic_slice_in_dim(a, i * width, width, axis=1)
 
 
-def scatter_sum(a, batches):
+def scatter_sum(a, batches, core):
     t = lax.axis_index("tm")
     z4, z2, x, yh = t // 16, (t // 8) % 2, (t // 2) % 4, t % 2
     if batches > 1:
         b = lax.axis_index("batch")
         away = lax.dynamic_index_in_dim(a, 1 - b, 0, keepdims=False)
-        got = lax.ppermute(away, "batch", [(0, 1), (1, 0)])
+        got = send(away, "batch", [(0, 1), (1, 0)], core)
         a = lax.dynamic_index_in_dim(a, b, 0, keepdims=False) + got
     else:
         a = jnp.concatenate([a[0], a[1]], axis=1)
     at = pieces(a, 4)
-    got = ordered(lambda s: move_z4(at((z4 + s) % 4), s), (2, 1, 3))
+    got = ordered(lambda s: move_z4(at((z4 + s) % 4), s, core), (2, 1, 3))
     a = (at(z4) + got[0]) + (got[1] + got[2])
     at = pieces(a, 2)
-    a = at(z2) + move_zy(at(1 - z2), 1)
+    a = at(z2) + move_zy(at(1 - z2), 1, core)
     at = pieces(a, 4)
-    got = ordered(lambda s: move_x(at((x + s) % 4), s), (2, 1, 3))
+    got = ordered(lambda s: move_x(at((x + s) % 4), s, core), (2, 1, 3))
     a = (at(x) + got[0]) + (got[1] + got[2])
     at = pieces(a, 2)
-    return at(yh) + move_zy(at(1 - yh), 2)
+    return at(yh) + move_zy(at(1 - yh), 2, core)
 
 
 def step(input_signal, standardize_factor, triple_projection, score_sharpening, final_projection, filter_taps, mixture_adjoint, *, batches, mps):
@@ -402,28 +426,29 @@
     shape = jax.ShapeDtypeStruct
     adj_rims = rims(adj, adj[:reach], adj[rows - reach :])
     piece = shape((2 * hs, rows), BF16)
-    *sent_kv, qpay, qhat, khat, rad = vcall(
+    *sent_kv, qhat, khat, rad = vcall(
         functools.partial(front_kernel, heads=heads, hs=hs),
-        (piece,) * 4 + (shape((heads, hs, rows), BF16), shape((flat, rows), F32), shape((flat, rows), F32), shape((2 * heads, rows), F32)),
+        (piece,) * 4 + (shape((flat, rows), F32), shape((flat, rows), F32), shape((2 * heads, rows), F32)),
         scratch=[
             pltpu.VMEM((heads, 2 * hs, rows), BF16),
             pltpu.VMEM((rows, width), BF16),
             pltpu.VMEM((3, width, flat), BF16),
             pltpu.SemaphoreType.DMA((4,)),
         ],
-        smem=2,
+        smem=1,
         n_in=1,
         raw=2,
-    )(z4, score_sharpening, factor, x_in, triple_projection)
+    )(z4, factor, x_in, triple_projection)
     got_kv = [sent_kv[0]] + ordered(lambda s: move_z4(sent_kv[s], s), (2, 1, 3))
     pad = pltpu.VMEM((rows + 32, width), F32)
     *sent_qg, grad_res = vcall(
         functools.partial(send_kernel, hs=hs),
         (piece,) * 4 + (shape((rows, width), F32),),
-        scratch=[pad, pltpu.VMEM((4, hs, rows), BF16)],
-        smem=1,
+        scratch=[pad, pltpu.VMEM((4, 2 * hs, rows), BF16), pltpu.VMEM((rows, width), F32)],
+        out_hbm=(4,),
+        smem=2,
         n_in=6,
-    )(z4, *adj_rims, filter_taps, qpay, final_projection)
+    )(z4, score_sharpening, *adj_rims, filter_taps, qhat, final_projection)
     got_qg = [sent_qg[0]] + ordered(lambda s: move_z4(sent_qg[s], s), (2, 1, 3))
     kv0 = jnp.concatenate(got_kv, axis=1)
     qg0 = jnp.concatenate(got_qg, axis=1)
@@ -453,17 +478,34 @@
     )(z4, score_sharpening, *back, qhat, khat, rad, final_projection, triple_projection)
     other = lax.ppermute(part, "mp", [(0, 1), (1, 0)]) if mps > 1 else jnp.zeros_like(part)
     edge = shape((reach, width), BF16)
+    core = lax.axis_index("mp").astype(jnp.int32)
+    red = mps - 1
     residual, signal_adjoint, sums, first, last = vcall(
-        functools.partial(tail_kernel, rows=rows, taps=taps),
+        functools.partial(tail_kernel, rows=rows, taps=taps, red=red),
         (shape((rows, width), BF16), shape((rows, width), BF16), shape((2, taps + 1, width // 2), F32), edge, edge),
-        scratch=[pad, pltpu.VMEM((rows, width), F32), pltpu.VMEM((1, width), F32)],
-        n_in=8,
+        scratch=[
+            pad,
+            pltpu.VMEM((rows, width), F32),
+            pltpu.VMEM((1, width), F32),
+            pltpu.VMEM((rows, width), F32),
+            pltpu.SemaphoreType.DMA(()),
+        ],
+        smem=1,
+        n_in=7,
+        raw=1,
         out_hbm=(1,),
-    )(part, other, x_in, factor, *adj_rims, grad_res)
-    res_rims = rims(residual, first, last)
-    sublayer_result = vcall(out_kernel, shape((rows, width), BF16), scratch=[pad], n_in=4, out_hbm=(0,))(*res_rims, filter_taps)
-    sums = scatter_sum(sums, batches)
-    return (sublayer_result[None], signal_adjoint[None], sums[:taps], sums[taps])
+    )(core.reshape(1), part, other, x_in, factor, *adj_rims, grad_res)
+    res_rims = rims(residual, first, last, 0)
+    result = vcall(out_kernel, shape((rows, width), BF16), scratch=[pad], smem=1, n_in=4)(
+        core.reshape(1), *res_rims, filter_taps
+    )
+    sums = scatter_sum(sums, batches, red)
+    if mps > 1:
+        moved = lax.ppermute(result, "mp", [(0, 1)])
+        result = jnp.where(core == 0, result, moved)
+        moved = lax.ppermute(sums, "mp", [(1, 0)])
+        sums = jnp.where(core == 1, sums, moved)
+    return (result[None], signal_adjoint[None], sums[:taps], sums[taps])
 
 
 def solution(mesh):

time: 174 us -> 175 us (level)
  the two profiles are of different devices: /device:TPU:30 before, /device:TPU:1 now
where the time goes in v2:
time: 175 us
  starting transfers between devices  90.4 us (52%)
  waiting for transfers between devices  45.5 us (26%)
  Pallas kernels  33.7 us (19%)
  local copies, waits for them, and re-layouts  2.54 us (1%)
    ppermute x25, starting transfers between devices, send(): return lax.ppermute(a, axis, pairs)  47.1 us
    pallas_call x9, Pallas kernels, run(): return call(*args)  33.7 us
    ppermute x25, waiting for transfers between devices, send(): return lax.ppermute(a, axis, pairs)  30 us
    ppermute x11, starting transfers between devices, send(): lax.ppermute(a, (axis, 'mp'), [(i * cores + core, j * cores + core) for i...  28.2 us
    ppermute x1, starting transfers between devices, step(): lax.ppermute(part, 'mp', [(0, 1), (1, 0)])  12.6 us
    ppermute x11, waiting for transfers between devices, send(): lax.ppermute(a, (axis, 'mp'), [(i * cores + core, j * cores + core) for i...  12.5 us
  transfers between devices with their start and end apart: 39, of which 19 were waited for; matrix products, arithmetic and copies ran while one was open for 1% of the time, Pallas kernels for 9%

profile of v2, /device:TPU:1, one launch (start us, length us, event | category | flops | bytes accessed | tf_op | source)
XLA Modules:
  0.0 174.5 jit_solution(10295446156062184497)
XLA Ops:
  1.5 2.9 %shard_map.102 = (bf16[192,128]{1,0:T(8,128)(2,1)S(1)}, bf16[192,128]{1,0:T(8,128)(2,1)S(1)}, bf16[192,128]{1,0:T(8,128)(2,1)S(1)}, bf16[192,128]{1,0:T(8,128)(2...) custom-call(s32[1]{0:T(128)} %bitcast.1.idx, ...), custom_call_target="tpu_custom_call" | custom-call | tf_op jit(solution)/shard_map/pallas_call | solution.py:87
  4.4 3.9 %collective-permute-start = (bf16[192,128]{1,0:T(8,128)(2,1)S(1)}, bf16[192,128]{1,0:T(8,128)(2,1)S(1)}, u32[]{:S(2)}, u32[]{:S(2)}) collective-permute-start(bf16[192,128]{1,0:T(8,128)(2,1)S(1)} %get-tuple-element.36), channel_id=1, source_target_pairs={{0,32},{2,34},{4,36},{6,38},{8,40},{10,42},{12,44},{14,46},{16,48}... | collective-permute-start | bytes 147464 | tf_op jit(solution)/shard_map/ppermute | solution.py:29
  8.3 5.1 %collective-permute-start.1 = (bf16[192,128]{1,0:T(8,128)(2,1)S(1)}, bf16[192,128]{1,0:T(8,128)(2,1)S(1)}, u32[]{:S(2)}, u32[]{:S(2)}) collective-permute-start(bf16[192,128]{1,0:T(8,128)(2,1)S(1)} %get-tuple-element.37), channel_id=1, source_target_pairs={{0,64},{2,66},{4,68},{6,70},{8,72},{10,74},{12,76},{14,78},{16,80}... | collective-permute-start | bytes 147464 | tf_op jit(solution)/shard_map/ppermute | solution.py:29
  15.8 4.8 %collective-permute-start.6 = (bf16[15,1536]{1,0:T(8,128)(2,1)S(1)}, bf16[15,1536]{1,0:T(8,128)(2,1)S(1)}, u32[]{:S(2)}, u32[]{:S(2)}) collective-permute-start(bf16[15,1536]{1,0:T(8,128)(2,1)S(1)} %get-tuple-element.71), channel_id=1, source_target_pairs={{0,2},{2,4},{4,6},{6,8},{8,10},{10,12},{12,14},{14,16},{16,18},{18... | collective-permute-start | bytes 138248 | tf_op jit(solution)/shard_map/ppermute | solution.py:29
  21.9 5.0 %collective-permute-done.7.right = bf16[15,1536]{1,0:T(8,128)(2,1)S(1)} collective-permute-done((bf16[15,1536]{1,0:T(8,128)(2,1)S(1)}, bf16[15,1536]{1,0:T(8,128)(2,1)S(1)}, u32[]{:S(2)}, u32[]{:S(2)}) %collective-permute-start.7) | collective-permute-done | bytes 46112 | tf_op jit(solution)/shard_map/ppermute | solution.py:29
  27.0 5.1 %shard_map.103 = (bf16[192,128]{1,0:T(8,128)(2,1)S(1)}, bf16[192,128]{1,0:T(8,128)(2,1)S(1)}, bf16[192,128]{1,0:T(8,128)(2,1)S(1)}, bf16[192,128]{1,0:T(8,128)(2,1)S(1)}, f32[128,1536]{1,0:T(8,128)S(1)}) custom-call(s32[1]{0:T(128)} %bitcast.1.idx, f32[4]{0:T(128)S(1)} %copy-done.6, bf16[15,1536]{1,0:T(8,128)(2,1)S(1)} %collective-permute-done.6.left, ...), custom_call_target="tpu_custom_call" | custom-call | tf_op jit(solution)/shard_map/pallas_call | solution.py:87
  34.7 3.1 %collective-permute-start.10 = (bf16[192,128]{1,0:T(8,128)(2,1)S(1)}, bf16[192,128]{1,0:T(8,128)(2,1)S(1)}, u32[]{:S(2)}, u32[]{:S(2)}) collective-permute-start(bf16[192,128]{1,0:T(8,128)(2,1)S(1)} %get-tuple-element.43), channel_id=1, source_target_pairs={{0,96},{2,98},{4,100},{6,102},{8,104},{10,106},{12,108},{14,110},{... | collective-permute-start | bytes 147464 | tf_op jit(solution)/shard_map/ppermute | solution.py:29
  48.9 4.1 %collective-permute-done.13.refs_7_.refs_9_ = bf16[192,512]{1,0:T(8,128)(2,1)S(1)} collective-permute-done((bf16[192,512]{1,0:T(8,128)(2,1)S(1)}, bf16[192,512]{1,0:T(8,128)(2,1)S(1)}, u32[]{:S(2)}, u32[]{:S(2)}) %collective-permute-start.13) | collective-permute-done | bytes 196640 | tf_op jit(solution)/shard_map/ppermute | solution.py:29
  53.1 8.2 %shard_map.104 = (f32[4,2,512]{2,1,0:T(2,128)S(1)}, f32[4,288,512]{2,1,0:T(8,128)S(1)}) custom-call(bf16[192,512]{1,0:T(8,128)(2,1)S(1)} %constant_dynamic-update-slice_fusion.refs_0_.refs_2_, bf16[192,512]{1,0:T(8,128)(2,1)S(1)} %collective-permute-done.3.refs_1_.refs_3_, bf16[192,512]{1,0:T(8,128)(2,1)S(1)} %collective-permute-done.4.refs_2_.refs_4_, ...), custom_call_target="tpu_custom_call" | custom-call | tf_op jit(solution)/shard_map/pallas_call | solution.py:87
  65.1 3.0 %collective-permute-done.15.te1.refs_1_ = f32[4,2,512]{2,1,0:T(2,128)S(1)} collective-permute-done((f32[4,2,512]{2,1,0:T(2,128)S(1)}, f32[4,2,512]{2,1,0:T(2,128)S(1)}, u32[]{:S(2)}, u32[]{:S(2)}) %collective-permute-start.15) | collective-permute-done | bytes 16416 | tf_op jit(solution)/shard_map/ppermute | solution.py:29
  72.6 10.4 %shard_map.106 = (bf16[192,512]{1,0:T(8,128)(2,1)S(1)}, bf16[192,512]{1,0:T(8,128)(2,1)S(1)}, bf16[192,512]{1,0:T(8,128)(2,1)S(1)}, bf16[192,512]{1,0:T(8,128)(2,1)S(1)}) custom-call(f32[4,2,512]{2,1,0:T(2,128)S(1)} %maximum_add_fusion.te0.refs_0_, f32[4,2,512]{2,1,0:T(2,128)S(1)} %collective-permute-done.15.te1.refs_1_, ...), custom_call_target="tpu_custom_call" | custom-call | tf_op jit(solution)/shard_map/pallas_call | solution.py:87
  82.9 3.9 %collective-permute-start.19 = (bf16[192,512]{1,0:T(8,128)(2,1)S(1)}, bf16[192,512]{1,0:T(8,128)(2,1)S(1)}, u32[]{:S(2)}, u32[]{:S(2)}) collective-permute-start(bf16[192,512]{1,0:T(8,128)(2,1)S(1)} %get-tuple-element.51), channel_id=1, source_target_pairs={{0,12},{2,14},{4,0},{6,2},{8,4},{10,6},{12,8},{14,10},{16,28},{18,... | collective-permute-start | bytes 589832 | tf_op jit(solution)/shard_map/ppermute | solution.py:29
  87.5 4.0 %collective-permute-done.19.refs_5_ = bf16[192,512]{1,0:T(8,128)(2,1)S(1)} collective-permute-done((bf16[192,512]{1,0:T(8,128)(2,1)S(1)}, bf16[192,512]{1,0:T(8,128)(2,1)S(1)}, u32[]{:S(2)}, u32[]{:S(2)}) %collective-permute-start.19) | collective-permute-done | bytes 196640 | tf_op jit(solution)/shard_map/ppermute | solution.py:29
  96.2 3.3 %collective-permute-start.23 = (bf16[384,128]{1,0:T(8,128)(2,1)S(1)}, bf16[384,128]{1,0:T(8,128)(2,1)S(1)}, u32[]{:S(2)}, u32[]{:S(2)}) collective-permute-start(bf16[384,128]{1,0:T(8,128)(2,1)S(1)} %get-tuple-element.56), channel_id=1, source_target_pairs={{0,64},{2,66},{4,68},{6,70},{8,72},{10,74},{12,76},{14,78},{16,80}... | collective-permute-start | bytes 294920 | tf_op jit(solution)/shard_map/ppermute | solution.py:29
  100.4 4.3 %collective-permute-done.23.b2 = bf16[384,128]{1,0:T(8,128)(2,1)S(1)} collective-permute-done((bf16[384,128]{1,0:T(8,128)(2,1)S(1)}, bf16[384,128]{1,0:T(8,128)(2,1)S(1)}, u32[]{:S(2)}, u32[]{:S(2)}) %collective-permute-start.23) | collective-permute-done | bytes 98336 | tf_op jit(solution)/shard_map/ppermute | solution.py:29
  107.9 12.6 %collective-permute-start.25 = (bf16[256,1536]{1,0:T(8,128)(2,1)S(1)}, bf16[256,1536]{1,0:T(8,128)(2,1)S(1)}, u32[]{:S(2)}, u32[]{:S(2)}) collective-permute-start(bf16[256,1536]{1,0:T(8,128)(2,1)S(1)} %shard_map.108.part), channel_id=1, source_target_pairs={{0,1},{1,0},{2,3},{3,2},{4,5},{5,4},{6,7},{7,6},{8,9},{9,8},{10,11... | collective-permute-start | bytes 2359304 | tf_op jit(solution)/shard_map/ppermute | solution.py:479
  122.3 4.7 %shard_map.109 = (bf16[128,1536]{1,0:T(8,128)(2,1)S(1)}, bf16[128,1536]{1,0:T(8,128)(2,1)}, f32[2,32,768]{2,1,0:T(8,128)S(1)}, bf16[15,1536]{1,0:T(8,128)(2,1)S(1)}, bf16[15,1536]{1,0:T(8,128)(2,1)S(1)}) custom-call(s32[1]{0:T(128)} %bitcast.core, bf16[256,1536]{1,0:T(8,128)(2,1)S(1)} %shard_map.108.part, ...), custom_call_target="tpu_custom_call" | custom-call | tf_op jit(solution)/shard_map/pallas_call | solution.py:87
  127.0 3.8 %collective-permute-start.29 = (f32[32,768]{1,0:T(8,128)S(1)}, f32[32,768]{1,0:T(8,128)S(1)}, u32[]{:S(2)}, u32[]{:S(2)}) collective-permute-start(f32[32,768]{1,0:T(8,128)S(1)} %dynamic-slice_bitcast_fusion), channel_id=1, source_target_pairs={{1,129},{129,1},{3,131},{131,3},{5,133},{133,5},{7,135},{135,7},{9... | collective-permute-start | bytes 294920 | tf_op jit(solution)/shard_map/ppermute | solution.py:31
  132.9 3.6 %collective-permute-start.31 = (f32[32,192]{1,0:T(8,128)S(1)}, f32[32,192]{1,0:T(8,128)S(1)}, u32[]{:S(2)}, u32[]{:S(2)}) collective-permute-start(f32[32,192]{1,0:T(8,128)S(1)} %get-tuple-element.74), channel_id=1, source_target_pairs={{1,65},{3,67},{5,69},{7,71},{9,73},{11,75},{13,77},{15,79},{17,81}... | collective-permute-start | bytes 73736 | tf_op jit(solution)/shard_map/ppermute | solution.py:31
  136.5 3.7 %collective-permute-start.32 = (f32[32,192]{1,0:T(8,128)S(1)}, f32[32,192]{1,0:T(8,128)S(1)}, u32[]{:S(2)}, u32[]{:S(2)}) collective-permute-start(f32[32,192]{1,0:T(8,128)S(1)} %get-tuple-element.73), channel_id=1, source_target_pairs={{1,97},{3,99},{5,101},{7,103},{9,105},{11,107},{13,109},{15,111},{... | collective-permute-start | bytes 73736 | tf_op jit(solution)/shard_map/ppermute | solution.py:31
  142.7 4.3 %collective-permute-done.30 = f32[32,192]{1,0:T(8,128)S(1)} collective-permute-done((f32[32,192]{1,0:T(8,128)S(1)}, f32[32,192]{1,0:T(8,128)S(1)}, u32[]{:S(2)}, u32[]{:S(2)}) %collective-permute-start.30) | collective-permute-done | bytes 24608 | tf_op jit(solution)/shard_map/ppermute | solution.py:31
  147.2 3.7 %collective-permute-start.33 = (f32[32,96]{1,0:T(8,128)S(1)}, f32[32,96]{1,0:T(8,128)S(1)}, u32[]{:S(2)}, u32[]{:S(2)}) collective-permute-start(f32[32,96]{1,0:T(8,128)S(1)} %constant_dynamic-slice_fusion.4), channel_id=1, source_target_pairs={{1,17},{3,19},{5,21},{7,23},{9,25},{11,27},{13,29},{15,31},{17,1},... | collective-permute-start | bytes 36872 | tf_op jit(solution)/shard_map/ppermute | solution.py:31
  154.1 2.8 %collective-permute-start.36 = (f32[32,24]{1,0:T(8,128)S(1)}, f32[32,24]{1,0:T(8,128)S(1)}, u32[]{:S(2)}, u32[]{:S(2)}) collective-permute-start(f32[32,24]{1,0:T(8,128)S(1)} %get-tuple-element.76), channel_id=1, source_target_pairs={{1,13},{3,15},{5,1},{7,3},{9,5},{11,7},{13,9},{15,11},{17,29},{19,... | collective-permute-start | bytes 9224 | tf_op jit(solution)/shard_map/ppermute | solution.py:31
  159.4 3.1 %collective-permute-done.34 = f32[32,24]{1,0:T(8,128)S(1)} collective-permute-done((f32[32,24]{1,0:T(8,128)S(1)}, f32[32,24]{1,0:T(8,128)S(1)}, u32[]{:S(2)}, u32[]{:S(2)}) %collective-permute-start.34) | collective-permute-done | bytes 3104 | tf_op jit(solution)/shard_map/ppermute | solution.py:31
  (103 shorter events, 60.0 us)
Async XLA Ops:
  4.4 30.3 %collective-permute-start = (bf16[192,128]{1,0:T(8,128)(2,1)S(1)}, bf16[192,128]{1,0:T(8,128)(2,1)S(1)}, u32[]{:S(2)}, u32[]{:S(2)}) collective-permute-start(bf16[192,128]{1,0:T(8,128)(2,1)S(1)} %get-tuple-element.36), channel_id=1, source_target_pairs={{0,32},{2,34},{4,36},{6,38},{8,40},{10,42},{12,44},{14,46},{16,48}... | collective-permute-start | bytes 147464 | tf_op jit(solution)/shard_map/ppermute | solution.py:29
  8.3 29.5 %collective-permute-start.1 = (bf16[192,128]{1,0:T(8,128)(2,1)S(1)}, bf16[192,128]{1,0:T(8,128)(2,1)S(1)}, u32[]{:S(2)}, u32[]{:S(2)}) collective-permute-start(bf16[192,128]{1,0:T(8,128)(2,1)S(1)} %get-tuple-element.37), channel_id=1, source_target_pairs={{0,64},{2,66},{4,68},{6,70},{8,72},{10,74},{12,76},{14,78},{16,80}... | collective-permute-start | bytes 147464 | tf_op jit(solution)/shard_map/ppermute | solution.py:29
  13.4 24.4 %collective-permute-start.2 = (bf16[192,128]{1,0:T(8,128)(2,1)S(1)}, bf16[192,128]{1,0:T(8,128)(2,1)S(1)}, u32[]{:S(2)}, u32[]{:S(2)}) collective-permute-start(bf16[192,128]{1,0:T(8,128)(2,1)S(1)} %get-tuple-element.38), channel_id=1, source_target_pairs={{0,96},{2,98},{4,100},{6,102},{8,104},{10,106},{12,108},{14,110},{... | collective-permute-start | bytes 147464 | tf_op jit(solution)/shard_map/ppermute | solution.py:29
  20.6 6.3 %collective-permute-start.7 = (bf16[15,1536]{1,0:T(8,128)(2,1)S(1)}, bf16[15,1536]{1,0:T(8,128)(2,1)S(1)}, u32[]{:S(2)}, u32[]{:S(2)}) collective-permute-start(bf16[15,1536]{1,0:T(8,128)(2,1)S(1)} %get-tuple-element.70), channel_id=1, source_target_pairs={{2,0},{4,2},{6,4},{8,6},{10,8},{12,10},{14,12},{16,14},{18,16},{20... | collective-permute-start | bytes 138248 | tf_op jit(solution)/shard_map/ppermute | solution.py:29
  32.1 8.5 %collective-permute-start.8 = (bf16[192,128]{1,0:T(8,128)(2,1)S(1)}, bf16[192,128]{1,0:T(8,128)(2,1)S(1)}, u32[]{:S(2)}, u32[]{:S(2)}) collective-permute-start(bf16[192,128]{1,0:T(8,128)(2,1)S(1)} %get-tuple-element.41), channel_id=1, source_target_pairs={{0,32},{2,34},{4,36},{6,38},{8,40},{10,42},{12,44},{14,46},{16,48}... | collective-permute-start | bytes 147464 | tf_op jit(solution)/shard_map/ppermute | solution.py:29
  32.7 9.0 %collective-permute-start.9 = (bf16[192,128]{1,0:T(8,128)(2,1)S(1)}, bf16[192,128]{1,0:T(8,128)(2,1)S(1)}, u32[]{:S(2)}, u32[]{:S(2)}) collective-permute-start(bf16[192,128]{1,0:T(8,128)(2,1)S(1)} %get-tuple-element.42), channel_id=1, source_target_pairs={{0,64},{2,66},{4,68},{6,70},{8,72},{10,74},{12,76},{14,78},{16,80}... | collective-permute-start | bytes 147464 | tf_op jit(solution)/shard_map/ppermute | solution.py:29
  34.7 7.1 %collective-permute-start.10 = (bf16[192,128]{1,0:T(8,128)(2,1)S(1)}, bf16[192,128]{1,0:T(8,128)(2,1)S(1)}, u32[]{:S(2)}, u32[]{:S(2)}) collective-permute-start(bf16[192,128]{1,0:T(8,128)(2,1)S(1)} %get-tuple-element.43), channel_id=1, source_target_pairs={{0,96},{2,98},{4,100},{6,102},{8,104},{10,106},{12,108},{14,110},{... | collective-permute-start | bytes 147464 | tf_op jit(solution)/shard_map/ppermute | solution.py:29
  37.8 7.2 %collective-permute-start.3 = (bf16[192,512]{1,0:T(8,128)(2,1)S(1)}, bf16[192,512]{1,0:T(8,128)(2,1)S(1)}, u32[]{:S(2)}, u32[]{:S(2)}) collective-permute-start(bf16[192,512]{1,0:T(8,128)(2,1)S(1)} %constant_dynamic-update-slice_fusion.refs_0_.refs_2_), channel_id=1, source_target_pairs={{0,4},{2,6},{4,8},{6,10},{8,12},{10,14},{12,0},{14,2},{16,20},{18,... | collective-permute-start | bytes 589832 | tf_op jit(solution)/shard_map/ppermute | solution.py:29
  38.1 8.4 %collective-permute-start.4 = (bf16[192,512]{1,0:T(8,128)(2,1)S(1)}, bf16[192,512]{1,0:T(8,128)(2,1)S(1)}, u32[]{:S(2)}, u32[]{:S(2)}) collective-permute-start(bf16[192,512]{1,0:T(8,128)(2,1)S(1)} %constant_dynamic-update-slice_fusion.refs_0_.refs_2_), channel_id=1, source_target_pairs={{0,8},{2,10},{4,12},{6,14},{8,0},{10,2},{12,4},{14,6},{16,24},{18,... | collective-permute-start | bytes 589832 | tf_op jit(solution)/shard_map/ppermute | solution.py:29
  40.6 6.3 %collective-permute-start.5 = (bf16[192,512]{1,0:T(8,128)(2,1)S(1)}, bf16[192,512]{1,0:T(8,128)(2,1)S(1)}, u32[]{:S(2)}, u32[]{:S(2)}) collective-permute-start(bf16[192,512]{1,0:T(8,128)(2,1)S(1)} %constant_dynamic-update-slice_fusion.refs_0_.refs_2_), channel_id=1, source_target_pairs={{0,12},{2,14},{4,0},{6,2},{8,4},{10,6},{12,8},{14,10},{16,28},{18,... | collective-permute-start | bytes 589832 | tf_op jit(solution)/shard_map/ppermute | solution.py:29
  42.6 6.3 %collective-permute-start.12 = (bf16[192,512]{1,0:T(8,128)(2,1)S(1)}, bf16[192,512]{1,0:T(8,128)(2,1)S(1)}, u32[]{:S(2)}, u32[]{:S(2)}) collective-permute-start(bf16[192,512]{1,0:T(8,128)(2,1)S(1)} %constant_dynamic-update-slice_fusion.4.refs_4_.refs_6_), channel_id=1, source_target_pairs={{0,2},{2,0},{4,6},{6,4},{8,10},{10,8},{12,14},{14,12},{16,18},{18,... | collective-permute-start | bytes 589832 | tf_op jit(solution)/shard_map/ppermute | solution.py:29
  45.0 8.0 %collective-permute-start.13 = (bf16[192,512]{1,0:T(8,128)(2,1)S(1)}, bf16[192,512]{1,0:T(8,128)(2,1)S(1)}, u32[]{:S(2)}, u32[]{:S(2)}) collective-permute-start(bf16[192,512]{1,0:T(8,128)(2,1)S(1)} %constant_dynamic-update-slice_fusion.4.refs_4_.refs_6_), channel_id=1, source_target_pairs={{0,18},{2,16},{4,22},{6,20},{8,26},{10,24},{12,30},{14,28},{16,2},... | collective-permute-start | bytes 589832 | tf_op jit(solution)/shard_map/ppermute | solution.py:29
  68.3 18.5 %collective-permute-start.16 = (bf16[192,512]{1,0:T(8,128)(2,1)S(1)}, bf16[192,512]{1,0:T(8,128)(2,1)S(1)}, u32[]{:S(2)}, u32[]{:S(2)}) collective-permute-start(bf16[192,512]{1,0:T(8,128)(2,1)S(1)} %get-tuple-element.47), channel_id=1, source_target_pairs={{0,16},{2,18},{4,20},{6,22},{8,24},{10,26},{12,28},{14,30},{16,0},... | collective-permute-start | bytes 589832 | tf_op jit(solution)/shard_map/ppermute | solution.py:29
  69.0 18.4 %collective-permute-start.17 = (bf16[192,512]{1,0:T(8,128)(2,1)S(1)}, bf16[192,512]{1,0:T(8,128)(2,1)S(1)}, u32[]{:S(2)}, u32[]{:S(2)}) collective-permute-start(bf16[192,512]{1,0:T(8,128)(2,1)S(1)} %get-tuple-element.48), channel_id=1, source_target_pairs={{0,2},{2,0},{4,6},{6,4},{8,10},{10,8},{12,14},{14,12},{16,18},{18,... | collective-permute-start | bytes 589832 | tf_op jit(solution)/shard_map/ppermute | solution.py:29
  70.3 17.2 %collective-permute-start.18 = (bf16[192,512]{1,0:T(8,128)(2,1)S(1)}, bf16[192,512]{1,0:T(8,128)(2,1)S(1)}, u32[]{:S(2)}, u32[]{:S(2)}) collective-permute-start(bf16[192,512]{1,0:T(8,128)(2,1)S(1)} %get-tuple-element.49), channel_id=1, source_target_pairs={{0,18},{2,16},{4,22},{6,20},{8,26},{10,24},{12,30},{14,28},{16,2},... | collective-permute-start | bytes 589832 | tf_op jit(solution)/shard_map/ppermute | solution.py:29
  82.9 8.6 %collective-permute-start.19 = (bf16[192,512]{1,0:T(8,128)(2,1)S(1)}, bf16[192,512]{1,0:T(8,128)(2,1)S(1)}, u32[]{:S(2)}, u32[]{:S(2)}) collective-permute-start(bf16[192,512]{1,0:T(8,128)(2,1)S(1)} %get-tuple-element.51), channel_id=1, source_target_pairs={{0,12},{2,14},{4,0},{6,2},{8,4},{10,6},{12,8},{14,10},{16,28},{18,... | collective-permute-start | bytes 589832 | tf_op jit(solution)/shard_map/ppermute | solution.py:29
  86.8 7.8 %collective-permute-start.21 = (bf16[192,512]{1,0:T(8,128)(2,1)S(1)}, bf16[192,512]{1,0:T(8,128)(2,1)S(1)}, u32[]{:S(2)}, u32[]{:S(2)}) collective-permute-start(bf16[192,512]{1,0:T(8,128)(2,1)S(1)} %get-tuple-element.53), channel_id=1, source_target_pairs={{0,4},{2,6},{4,8},{6,10},{8,12},{10,14},{12,0},{14,2},{16,20},{18,... | collective-permute-start | bytes 589832 | tf_op jit(solution)/shard_map/ppermute | solution.py:29
  96.2 8.4 %collective-permute-start.23 = (bf16[384,128]{1,0:T(8,128)(2,1)S(1)}, bf16[384,128]{1,0:T(8,128)(2,1)S(1)}, u32[]{:S(2)}, u32[]{:S(2)}) collective-permute-start(bf16[384,128]{1,0:T(8,128)(2,1)S(1)} %get-tuple-element.56), channel_id=1, source_target_pairs={{0,64},{2,66},{4,68},{6,70},{8,72},{10,74},{12,76},{14,78},{16,80}... | collective-permute-start | bytes 294920 | tf_op jit(solution)/shard_map/ppermute | solution.py:29
  99.5 6.2 %collective-permute-start.24 = (bf16[384,128]{1,0:T(8,128)(2,1)S(1)}, bf16[384,128]{1,0:T(8,128)(2,1)S(1)}, u32[]{:S(2)}, u32[]{:S(2)}) collective-permute-start(bf16[384,128]{1,0:T(8,128)(2,1)S(1)} %get-tuple-element.57), channel_id=1, source_target_pairs={{0,32},{2,34},{4,36},{6,38},{8,40},{10,42},{12,44},{14,46},{16,48}... | collective-permute-start | bytes 294920 | tf_op jit(solution)/shard_map/ppermute | solution.py:29
  107.9 14.5 %collective-permute-start.25 = (bf16[256,1536]{1,0:T(8,128)(2,1)S(1)}, bf16[256,1536]{1,0:T(8,128)(2,1)S(1)}, u32[]{:S(2)}, u32[]{:S(2)}) collective-permute-start(bf16[256,1536]{1,0:T(8,128)(2,1)S(1)} %shard_map.108.part), channel_id=1, source_target_pairs={{0,1},{1,0},{2,3},{3,2},{4,5},{5,4},{6,7},{7,6},{8,9},{9,8},{10,11... | collective-permute-start | bytes 2359304 | tf_op jit(solution)/shard_map/ppermute | solution.py:479
  132.9 9.8 %collective-permute-start.31 = (f32[32,192]{1,0:T(8,128)S(1)}, f32[32,192]{1,0:T(8,128)S(1)}, u32[]{:S(2)}, u32[]{:S(2)}) collective-permute-start(f32[32,192]{1,0:T(8,128)S(1)} %get-tuple-element.74), channel_id=1, source_target_pairs={{1,65},{3,67},{5,69},{7,71},{9,73},{11,75},{13,77},{15,79},{17,81}... | collective-permute-start | bytes 73736 | tf_op jit(solution)/shard_map/ppermute | solution.py:31
  136.5 6.3 %collective-permute-start.32 = (f32[32,192]{1,0:T(8,128)S(1)}, f32[32,192]{1,0:T(8,128)S(1)}, u32[]{:S(2)}, u32[]{:S(2)}) collective-permute-start(f32[32,192]{1,0:T(8,128)S(1)} %get-tuple-element.73), channel_id=1, source_target_pairs={{1,97},{3,99},{5,101},{7,103},{9,105},{11,107},{13,109},{15,111},{... | collective-permute-start | bytes 73736 | tf_op jit(solution)/shard_map/ppermute | solution.py:31
  140.2 6.8 %collective-permute-start.30 = (f32[32,192]{1,0:T(8,128)S(1)}, f32[32,192]{1,0:T(8,128)S(1)}, u32[]{:S(2)}, u32[]{:S(2)}) collective-permute-start(f32[32,192]{1,0:T(8,128)S(1)} %get-tuple-element.72), channel_id=1, source_target_pairs={{1,33},{3,35},{5,37},{7,39},{9,41},{11,43},{13,45},{15,47},{17,49}... | collective-permute-start | bytes 73736 | tf_op jit(solution)/shard_map/ppermute | solution.py:31
  152.2 7.3 %collective-permute-start.35 = (f32[32,24]{1,0:T(8,128)S(1)}, f32[32,24]{1,0:T(8,128)S(1)}, u32[]{:S(2)}, u32[]{:S(2)}) collective-permute-start(f32[32,24]{1,0:T(8,128)S(1)} %get-tuple-element.77), channel_id=1, source_target_pairs={{1,9},{3,11},{5,13},{7,15},{9,1},{11,3},{13,5},{15,7},{17,25},{19,... | collective-permute-start | bytes 9224 | tf_op jit(solution)/shard_map/ppermute | solution.py:31
  (22 other events, 257.2 us)

commit v3 on v2

--- a/solution.py
+++ b/solution.py
@@ -28,7 +28,8 @@
     if core is None:
         return lax.ppermute(a, axis, pairs)
     cores = lax.axis_size("mp")
-    return lax.ppermute(a, (axis, "mp"), [(i * cores + core, j * cores + core) for i, j in pairs])
+    steps = [(i * cores + c, (j if c == core else i) * cores + c) for i, j in pairs for c in range(cores)]
+    return lax.ppermute(a, (axis, "mp"), steps)
 
 
 def move_z4(a, s, core=None):
@@ -133,12 +134,12 @@
         o[...] = pay[lax.rem(idx[0] + s, 4)]
 
 
-def fill_pad(pad, left, own, right):
+def fill_pad(pad, left, own, right, place):
     reach = left.shape[0]
     rows = own.shape[0]
-    pad[16 - reach : 16] = left[...].astype(F32)
+    pad[16 - reach : 16] = jnp.where(place > 0, left[...].astype(F32), 0.0)
     pad[16 : 16 + rows] = own[...].astype(F32)
-    pad[16 + rows : 16 + rows + reach] = right[...].astype(F32)
+    pad[16 + rows : 16 + rows + reach] = jnp.where(place < TM - 1, right[...].astype(F32), 0.0)
 
 
 def conv_rows(pad, taps, out, rows, flip):
@@ -160,8 +161,8 @@
     lax.fori_loop(0, out.shape[1] // 128, chunk, 0)
 
 
-def send_kernel(idx, sharp, left, own, right, taps, qhat, wf, o0, o1, o2, o3, gres_o, pad, g_s, gres, *, hs):
-    fill_pad(pad, left, own, right)
+def send_kernel(idx, place, sharp, left, own, right, taps, qhat, wf, o0, o1, o2, o3, gres_o, pad, g_s, gres, *, hs):
+    fill_pad(pad, left, own, right, place[0])
     conv_rows(pad, taps, gres, own.shape[0], True)
     gres_o[...] = gres[...]
     gt = dotf(wf[...], gres[...].astype(BF16), 1, 1).astype(BF16)
@@ -173,12 +174,12 @@
 
 
 def tail_kernel(
-    core, part, other, x, factor, left, own, right, gres_hbm, res_o, sig_o, sums, first, last, pad, resf, gain, gres, sem,
+    core, place, part, other, x, factor, left, own, right, gres_hbm, res_o, sig_o, sums, first, last, pad, resf, gain, gres, sem,
     *, rows, taps, red,
 ):
     fetch = pltpu.make_async_copy(gres_hbm, gres, sem)
     fetch.start()
-    fill_pad(pad, left, own, right)
+    fill_pad(pad, left, own, right, place[0])
     reach = taps // 2
     total = part[0:rows].astype(F32) + other[0:rows].astype(F32)
     xf = x[...].astype(F32)
@@ -227,10 +228,10 @@
         sums[...] = jnp.zeros(sums.shape, F32)
 
 
-def out_kernel(core, left, own, right, taps, out, pad):
+def out_kernel(core, place, left, own, right, taps, out, pad):
     @pl.when(core[0] == 0)
     def _():
-        fill_pad(pad, left, own, right)
+        fill_pad(pad, left, own, right, place[0])
         conv_rows(pad, taps, out, own.shape[0], False)
 
     @pl.when(core[0] != 0)
@@ -378,9 +379,8 @@
 
 
 def rims(cells, head, tail, core=None):
-    ends = TM - 1
-    left = send(tail, "tm", [(i, i + 1) for i in range(ends)], core)
-    right = send(head, "tm", [(i + 1, i) for i in range(ends)], core)
+    left = send(tail, "tm", [(i, (i + 1) % TM) for i in range(TM)], core)
+    right = send(head, "tm", [((i + 1) % TM, i) for i in range(TM)], core)
     return left, cells, right
 
 
@@ -420,6 +420,7 @@
     reach = taps // 2
     t = lax.axis_index("tm")
     z4 = (t // 16).astype(jnp.int32).reshape(1)
+    place = t.astype(jnp.int32).reshape(1)
     x_in = input_signal[0]
     adj = mixture_adjoint[0]
     factor = standardize_factor[None]
@@ -446,9 +447,9 @@
         (piece,) * 4 + (shape((rows, width), F32),),
         scratch=[pad, pltpu.VMEM((4, 2 * hs, rows), BF16), pltpu.VMEM((rows, width), F32)],
         out_hbm=(4,),
-        smem=2,
+        smem=3,
         n_in=6,
-    )(z4, score_sharpening, *adj_rims, filter_taps, qhat, final_projection)
+    )(z4, place, score_sharpening, *adj_rims, filter_taps, qhat, final_projection)
     got_qg = [sent_qg[0]] + ordered(lambda s: move_z4(sent_qg[s], s), (2, 1, 3))
     kv0 = jnp.concatenate(got_kv, axis=1)
     qg0 = jnp.concatenate(got_qg, axis=1)
@@ -479,6 +480,7 @@
     other = lax.ppermute(part, "mp", [(0, 1), (1, 0)]) if mps > 1 else jnp.zeros_like(part)
     edge = shape((reach, width), BF16)
     core = lax.axis_index("mp").astype(jnp.int32)
+    core_at = core.reshape(1)
     red = mps - 1
     residual, signal_adjoint, sums, first, last = vcall(
         functools.partial(tail_kernel, rows=rows, taps=taps, red=red),
@@ -490,20 +492,20 @@
             pltpu.VMEM((rows, width), F32),
             pltpu.SemaphoreType.DMA(()),
         ],
-        smem=1,
+        smem=2,
         n_in=7,
         raw=1,
         out_hbm=(1,),
-    )(core.reshape(1), part, other, x_in, factor, *adj_rims, grad_res)
+    )(core_at, place, part, other, x_in, factor, *adj_rims, grad_res)
     res_rims = rims(residual, first, last, 0)
-    result = vcall(out_kernel, shape((rows, width), BF16), scratch=[pad], smem=1, n_in=4)(
-        core.reshape(1), *res_rims, filter_taps
+    result = vcall(out_kernel, shape((rows, width), BF16), scratch=[pad], smem=2, n_in=4)(
+        core_at, place, *res_rims, filter_taps
     )
     sums = scatter_sum(sums, batches, red)
     if mps > 1:
-        moved = lax.ppermute(result, "mp", [(0, 1)])
+        moved = lax.ppermute(result, "mp", [(0, 1), (1, 0)])
         result = jnp.where(core == 0, result, moved)
-        moved = lax.ppermute(sums, "mp", [(1, 0)])
+        moved = lax.ppermute(sums, "mp", [(0, 1), (1, 0)])
         sums = jnp.where(core == 1, sums, moved)
     return (result[None], signal_adjoint[None], sums[:taps], sums[taps])
 

time: 175 us -> 175 us (level)
  starting transfers between devices: 90.4 us -> 93.2 us
  waiting for transfers between devices: 45.5 us -> 42.8 us
    ppermute x13, starting transfers between devices: 30.8 us -> 34.9 us  [the longest x11 30.2 us: send(): return lax.ppermute(a, (axis, 'mp'), steps)]
    ppermute x25, waiting for transfers between devices: 30 us -> 27.8 us  [send(): return lax.ppermute(a, axis, pairs)]
    ppermute x25, starting transfers between devices: 47.1 us -> 45.2 us  [send(): return lax.ppermute(a, axis, pairs)]
  transfers between devices with their start and end apart: 39 -> 39, of which waited for: 19 -> 18; matrix products, arithmetic and copies ran while one was open for 1% -> 1% of each run, Pallas kernels for 9% -> 9%
where the time goes in v3:
time: 175 us
  starting transfers between devices  93.2 us (53%)
  waiting for transfers between devices  42.8 us (24%)
  Pallas kernels  33.7 us (19%)
  local copies, waits for them, and re-layouts  2.54 us (1%)
    ppermute x25, starting transfers between devices, send(): return lax.ppermute(a, axis, pairs)  45.2 us
    pallas_call x9, Pallas kernels, run(): return call(*args)  33.7 us
    ppermute x11, starting transfers between devices, send(): return lax.ppermute(a, (axis, 'mp'), steps)  30.2 us
    ppermute x25, waiting for transfers between devices, send(): return lax.ppermute(a, axis, pairs)  27.8 us
    ppermute x1, starting transfers between devices, step(): lax.ppermute(part, 'mp', [(0, 1), (1, 0)])  13.1 us
    ppermute x11, waiting for transfers between devices, send(): return lax.ppermute(a, (axis, 'mp'), steps)  12.9 us
    ppermute x1, starting transfers between devices, step(): moved = lax.ppermute(result, 'mp', [(0, 1), (1, 0)])  4.58 us
  transfers between devices with their start and end apart: 39, of which 18 were waited for; matrix products, arithmetic and copies ran while one was open for 1% of the time, Pallas kernels for 9%

profile of v3, /device:TPU:1, one launch (start us, length us, event | category | flops | bytes accessed | tf_op | source)
XLA Modules:
  0.0 174.6 jit_solution(3592403896623441211)
XLA Ops:
  4.4 3.9 %collective-permute-start = (bf16[192,128]{1,0:T(8,128)(2,1)S(1)}, bf16[192,128]{1,0:T(8,128)(2,1)S(1)}, u32[]{:S(2)}, u32[]{:S(2)}) collective-permute-start(bf16[192,128]{1,0:T(8,128)(2,1)S(1)} %get-tuple-element.36), channel_id=1, source_target_pairs={{0,32},{2,34},{4,36},{6,38},{8,40},{10,42},{12,44},{14,46},{16,48}... | collective-permute-start | bytes 147464 | tf_op jit(solution)/shard_map/ppermute | solution.py:29
  8.3 5.1 %collective-permute-start.1 = (bf16[192,128]{1,0:T(8,128)(2,1)S(1)}, bf16[192,128]{1,0:T(8,128)(2,1)S(1)}, u32[]{:S(2)}, u32[]{:S(2)}) collective-permute-start(bf16[192,128]{1,0:T(8,128)(2,1)S(1)} %get-tuple-element.37), channel_id=1, source_target_pairs={{0,64},{2,66},{4,68},{6,70},{8,72},{10,74},{12,76},{14,78},{16,80}... | collective-permute-start | bytes 147464 | tf_op jit(solution)/shard_map/ppermute | solution.py:29
  18.8 4.3 %collective-permute-start.7 = (bf16[15,1536]{1,0:T(8,128)(2,1)S(1)}, bf16[15,1536]{1,0:T(8,128)(2,1)S(1)}, u32[]{:S(2)}, u32[]{:S(2)}) collective-permute-start(bf16[15,1536]{1,0:T(8,128)(2,1)S(1)} %get-tuple-element.70), channel_id=1, source_target_pairs={{2,0},{4,2},{6,4},{8,6},{10,8},{12,10},{14,12},{16,14},{18,16},{20... | collective-permute-start | bytes 138248 | tf_op jit(solution)/shard_map/ppermute | solution.py:29
  24.5 5.1 %shard_map.103 = (bf16[192,128]{1,0:T(8,128)(2,1)S(1)}, bf16[192,128]{1,0:T(8,128)(2,1)S(1)}, bf16[192,128]{1,0:T(8,128)(2,1)S(1)}, bf16[192,128]{1,0:T(8,128)(2,1)S(1)}, f32[128,1536]{1,0:T(8,128)S(1)}) custom-call(s32[1]{0:T(128)} %bitcast.2.idx, s32[1]{0:T(128)} %bitcast.1.place, f32[4]{0:T(128)S(1)} %copy-done.6, ...), custom_call_target="tpu_custom_call" | custom-call | tf_op jit(solution)/shard_map/pallas_call | solution.py:88
  31.2 3.2 %collective-permute-start.10 = (bf16[192,128]{1,0:T(8,128)(2,1)S(1)}, bf16[192,128]{1,0:T(8,128)(2,1)S(1)}, u32[]{:S(2)}, u32[]{:S(2)}) collective-permute-start(bf16[192,128]{1,0:T(8,128)(2,1)S(1)} %get-tuple-element.43), channel_id=1, source_target_pairs={{0,96},{2,98},{4,100},{6,102},{8,104},{10,106},{12,108},{14,110},{... | collective-permute-start | bytes 147464 | tf_op jit(solution)/shard_map/ppermute | solution.py:29
  39.1 3.2 %collective-permute-start.12 = (bf16[192,512]{1,0:T(8,128)(2,1)S(1)}, bf16[192,512]{1,0:T(8,128)(2,1)S(1)}, u32[]{:S(2)}, u32[]{:S(2)}) collective-permute-start(bf16[192,512]{1,0:T(8,128)(2,1)S(1)} %constant_dynamic-update-slice_fusion.4.refs_4_.refs_6_), channel_id=1, source_target_pairs={{0,2},{2,0},{4,6},{6,4},{8,10},{10,8},{12,14},{14,12},{16,18},{18,... | collective-permute-start | bytes 589832 | tf_op jit(solution)/shard_map/ppermute | solution.py:29
  43.7 3.2 %collective-permute-done.12.refs_6_.refs_8_ = bf16[192,512]{1,0:T(8,128)(2,1)S(1)} collective-permute-done((bf16[192,512]{1,0:T(8,128)(2,1)S(1)}, bf16[192,512]{1,0:T(8,128)(2,1)S(1)}, u32[]{:S(2)}, u32[]{:S(2)}) %collective-permute-start.12) | collective-permute-done | bytes 196640 | tf_op jit(solution)/shard_map/ppermute | solution.py:29
  46.9 4.6 %collective-permute-done.13.refs_7_.refs_9_ = bf16[192,512]{1,0:T(8,128)(2,1)S(1)} collective-permute-done((bf16[192,512]{1,0:T(8,128)(2,1)S(1)}, bf16[192,512]{1,0:T(8,128)(2,1)S(1)}, u32[]{:S(2)}, u32[]{:S(2)}) %collective-permute-start.13) | collective-permute-done | bytes 196640 | tf_op jit(solution)/shard_map/ppermute | solution.py:29
  51.5 8.2 %shard_map.104 = (f32[4,2,512]{2,1,0:T(2,128)S(1)}, f32[4,288,512]{2,1,0:T(8,128)S(1)}) custom-call(bf16[192,512]{1,0:T(8,128)(2,1)S(1)} %constant_dynamic-update-slice_fusion.refs_0_.refs_2_, bf16[192,512]{1,0:T(8,128)(2,1)S(1)} %collective-permute-done.3.refs_1_.refs_3_, bf16[192,512]{1,0:T(8,128)(2,1)S(1)} %collective-permute-done.4.refs_2_.refs_4_, ...), custom_call_target="tpu_custom_call" | custom-call | tf_op jit(solution)/shard_map/pallas_call | solution.py:88
  62.6 4.0 %collective-permute-done.15.te1.refs_1_ = f32[4,2,512]{2,1,0:T(2,128)S(1)} collective-permute-done((f32[4,2,512]{2,1,0:T(2,128)S(1)}, f32[4,2,512]{2,1,0:T(2,128)S(1)}, u32[]{:S(2)}, u32[]{:S(2)}) %collective-permute-start.15) | collective-permute-done | bytes 16416 | tf_op jit(solution)/shard_map/ppermute | solution.py:29
  71.0 10.4 %shard_map.106 = (bf16[192,512]{1,0:T(8,128)(2,1)S(1)}, bf16[192,512]{1,0:T(8,128)(2,1)S(1)}, bf16[192,512]{1,0:T(8,128)(2,1)S(1)}, bf16[192,512]{1,0:T(8,128)(2,1)S(1)}) custom-call(f32[4,2,512]{2,1,0:T(2,128)S(1)} %maximum_add_fusion.te0.refs_0_, f32[4,2,512]{2,1,0:T(2,128)S(1)} %collective-permute-done.15.te1.refs_1_, ...), custom_call_target="tpu_custom_call" | custom-call | tf_op jit(solution)/shard_map/pallas_call | solution.py:88
  84.2 3.8 %collective-permute-done.19.refs_5_ = bf16[192,512]{1,0:T(8,128)(2,1)S(1)} collective-permute-done((bf16[192,512]{1,0:T(8,128)(2,1)S(1)}, bf16[192,512]{1,0:T(8,128)(2,1)S(1)}, u32[]{:S(2)}, u32[]{:S(2)}) %collective-permute-start.19) | collective-permute-done | bytes 196640 | tf_op jit(solution)/shard_map/ppermute | solution.py:29
  97.2 3.6 %collective-permute-done.23.b2 = bf16[384,128]{1,0:T(8,128)(2,1)S(1)} collective-permute-done((bf16[384,128]{1,0:T(8,128)(2,1)S(1)}, bf16[384,128]{1,0:T(8,128)(2,1)S(1)}, u32[]{:S(2)}, u32[]{:S(2)}) %collective-permute-start.23) | collective-permute-done | bytes 98336 | tf_op jit(solution)/shard_map/ppermute | solution.py:29
  103.9 13.1 %collective-permute-start.25 = (bf16[256,1536]{1,0:T(8,128)(2,1)S(1)}, bf16[256,1536]{1,0:T(8,128)(2,1)S(1)}, u32[]{:S(2)}, u32[]{:S(2)}) collective-permute-start(bf16[256,1536]{1,0:T(8,128)(2,1)S(1)} %shard_map.108.part), channel_id=1, source_target_pairs={{0,1},{1,0},{2,3},{3,2},{4,5},{5,4},{6,7},{7,6},{8,9},{9,8},{10,11... | collective-permute-start | bytes 2359304 | tf_op jit(solution)/shard_map/ppermute | solution.py:480
  118.9 4.7 %shard_map.109 = (bf16[128,1536]{1,0:T(8,128)(2,1)S(1)}, bf16[128,1536]{1,0:T(8,128)(2,1)}, f32[2,32,768]{2,1,0:T(8,128)S(1)}, bf16[15,1536]{1,0:T(8,128)(2,1)S(1)}, bf16[15,1536]{1,0:T(8,128)(2,1)S(1)}) custom-call(s32[1]{0:T(128)} %bitcast.core, s32[1]{0:T(128)} %bitcast.1.place, bf16[256,1536]{1,0:T(8,128)(2,1)S(1)} %shard_map.108.part, ...), custom_call_target="tpu_custom_call" | custom-call | tf_op jit(solution)/shard_map/pallas_call | solution.py:88
  123.6 3.3 %collective-permute-start.29 = (f32[32,768]{1,0:T(8,128)S(1)}, f32[32,768]{1,0:T(8,128)S(1)}, u32[]{:S(2)}, u32[]{:S(2)}) collective-permute-start(f32[32,768]{1,0:T(8,128)S(1)} %dynamic-slice_bitcast_fusion), channel_id=1, source_target_pairs={{0,0},{1,129},{128,128},{129,1},{2,2},{3,131},{130,130},{131,3},{4... | collective-permute-start | bytes 294920 | tf_op jit(solution)/shard_map/ppermute | solution.py:32
  129.1 5.0 %collective-permute-start.31 = (f32[32,192]{1,0:T(8,128)S(1)}, f32[32,192]{1,0:T(8,128)S(1)}, u32[]{:S(2)}, u32[]{:S(2)}) collective-permute-start(f32[32,192]{1,0:T(8,128)S(1)} %get-tuple-element.74), channel_id=1, source_target_pairs={{0,0},{1,65},{2,2},{3,67},{4,4},{5,69},{6,6},{7,71},{8,8},{9,73},{... | collective-permute-start | bytes 73736 | tf_op jit(solution)/shard_map/ppermute | solution.py:32
  137.1 3.1 %collective-permute-start.30 = (f32[32,192]{1,0:T(8,128)S(1)}, f32[32,192]{1,0:T(8,128)S(1)}, u32[]{:S(2)}, u32[]{:S(2)}) collective-permute-start(f32[32,192]{1,0:T(8,128)S(1)} %get-tuple-element.72), channel_id=1, source_target_pairs={{0,0},{1,33},{2,2},{3,35},{4,4},{5,37},{6,6},{7,39},{8,8},{9,41},{... | collective-permute-start | bytes 73736 | tf_op jit(solution)/shard_map/ppermute | solution.py:32
  140.3 3.6 %collective-permute-done.30 = f32[32,192]{1,0:T(8,128)S(1)} collective-permute-done((f32[32,192]{1,0:T(8,128)S(1)}, f32[32,192]{1,0:T(8,128)S(1)}, u32[]{:S(2)}, u32[]{:S(2)}) %collective-permute-start.30) | collective-permute-done | bytes 24608 | tf_op jit(solution)/shard_map/ppermute | solution.py:32
  144.0 3.9 %collective-permute-start.33 = (f32[32,96]{1,0:T(8,128)S(1)}, f32[32,96]{1,0:T(8,128)S(1)}, u32[]{:S(2)}, u32[]{:S(2)}) collective-permute-start(f32[32,96]{1,0:T(8,128)S(1)} %constant_dynamic-slice_fusion.4), channel_id=1, source_target_pairs={{0,0},{1,17},{2,2},{3,19},{4,4},{5,21},{6,6},{7,23},{8,8},{9,25},{... | collective-permute-start | bytes 36872 | tf_op jit(solution)/shard_map/ppermute | solution.py:32
  149.2 3.4 %collective-permute-start.35 = (f32[32,24]{1,0:T(8,128)S(1)}, f32[32,24]{1,0:T(8,128)S(1)}, u32[]{:S(2)}, u32[]{:S(2)}) collective-permute-start(f32[32,24]{1,0:T(8,128)S(1)} %get-tuple-element.77), channel_id=1, source_target_pairs={{0,0},{1,9},{2,2},{3,11},{4,4},{5,13},{6,6},{7,15},{8,8},{9,1},{10... | collective-permute-start | bytes 9224 | tf_op jit(solution)/shard_map/ppermute | solution.py:32
  152.6 3.3 %collective-permute-start.36 = (f32[32,24]{1,0:T(8,128)S(1)}, f32[32,24]{1,0:T(8,128)S(1)}, u32[]{:S(2)}, u32[]{:S(2)}) collective-permute-start(f32[32,24]{1,0:T(8,128)S(1)} %get-tuple-element.76), channel_id=1, source_target_pairs={{0,0},{1,13},{2,2},{3,15},{4,4},{5,1},{6,6},{7,3},{8,8},{9,5},{10,... | collective-permute-start | bytes 9224 | tf_op jit(solution)/shard_map/ppermute | solution.py:32
  157.9 3.6 %collective-permute-done.34 = f32[32,24]{1,0:T(8,128)S(1)} collective-permute-done((f32[32,24]{1,0:T(8,128)S(1)}, f32[32,24]{1,0:T(8,128)S(1)}, u32[]{:S(2)}, u32[]{:S(2)}) %collective-permute-start.34) | collective-permute-done | bytes 3104 | tf_op jit(solution)/shard_map/ppermute | solution.py:32
  167.9 4.6 %collective-permute-start.28 = (bf16[128,1536]{1,0:T(8,128)(2,1)S(1)}, bf16[128,1536]{1,0:T(8,128)(2,1)S(1)}, u32[]{:S(2)}, u32[]{:S(2)}) collective-permute-start(bf16[128,1536]{1,0:T(8,128)(2,1)S(1)} %shard_map.110), channel_id=1, source_target_pairs={{0,1},{1,0},{2,3},{3,2},{4,5},{5,4},{6,7},{7,6},{8,9},{9,8},{10,11... | collective-permute-start | bytes 1179656 | tf_op jit(solution)/shard_map/ppermute | solution.py:506
  (103 shorter events, 59.3 us)
Async XLA Ops:
  4.4 26.8 %collective-permute-start = (bf16[192,128]{1,0:T(8,128)(2,1)S(1)}, bf16[192,128]{1,0:T(8,128)(2,1)S(1)}, u32[]{:S(2)}, u32[]{:S(2)}) collective-permute-start(bf16[192,128]{1,0:T(8,128)(2,1)S(1)} %get-tuple-element.36), channel_id=1, source_target_pairs={{0,32},{2,34},{4,36},{6,38},{8,40},{10,42},{12,44},{14,46},{16,48}... | collective-permute-start | bytes 147464 | tf_op jit(solution)/shard_map/ppermute | solution.py:29
  8.3 26.1 %collective-permute-start.1 = (bf16[192,128]{1,0:T(8,128)(2,1)S(1)}, bf16[192,128]{1,0:T(8,128)(2,1)S(1)}, u32[]{:S(2)}, u32[]{:S(2)}) collective-permute-start(bf16[192,128]{1,0:T(8,128)(2,1)S(1)} %get-tuple-element.37), channel_id=1, source_target_pairs={{0,64},{2,66},{4,68},{6,70},{8,72},{10,74},{12,76},{14,78},{16,80}... | collective-permute-start | bytes 147464 | tf_op jit(solution)/shard_map/ppermute | solution.py:29
  13.4 21.1 %collective-permute-start.2 = (bf16[192,128]{1,0:T(8,128)(2,1)S(1)}, bf16[192,128]{1,0:T(8,128)(2,1)S(1)}, u32[]{:S(2)}, u32[]{:S(2)}) collective-permute-start(bf16[192,128]{1,0:T(8,128)(2,1)S(1)} %get-tuple-element.38), channel_id=1, source_target_pairs={{0,96},{2,98},{4,100},{6,102},{8,104},{10,106},{12,108},{14,110},{... | collective-permute-start | bytes 147464 | tf_op jit(solution)/shard_map/ppermute | solution.py:29
  15.8 8.7 %collective-permute-start.6 = (bf16[15,1536]{1,0:T(8,128)(2,1)S(1)}, bf16[15,1536]{1,0:T(8,128)(2,1)S(1)}, u32[]{:S(2)}, u32[]{:S(2)}) collective-permute-start(bf16[15,1536]{1,0:T(8,128)(2,1)S(1)} %get-tuple-element.71), channel_id=1, source_target_pairs={{0,2},{2,4},{4,6},{6,8},{8,10},{10,12},{12,14},{14,16},{16,18},{18... | collective-permute-start | bytes 138248 | tf_op jit(solution)/shard_map/ppermute | solution.py:29
  29.7 7.4 %collective-permute-start.8 = (bf16[192,128]{1,0:T(8,128)(2,1)S(1)}, bf16[192,128]{1,0:T(8,128)(2,1)S(1)}, u32[]{:S(2)}, u32[]{:S(2)}) collective-permute-start(bf16[192,128]{1,0:T(8,128)(2,1)S(1)} %get-tuple-element.41), channel_id=1, source_target_pairs={{0,32},{2,34},{4,36},{6,38},{8,40},{10,42},{12,44},{14,46},{16,48}... | collective-permute-start | bytes 147464 | tf_op jit(solution)/shard_map/ppermute | solution.py:29
  29.8 8.4 %collective-permute-start.9 = (bf16[192,128]{1,0:T(8,128)(2,1)S(1)}, bf16[192,128]{1,0:T(8,128)(2,1)S(1)}, u32[]{:S(2)}, u32[]{:S(2)}) collective-permute-start(bf16[192,128]{1,0:T(8,128)(2,1)S(1)} %get-tuple-element.42), channel_id=1, source_target_pairs={{0,64},{2,66},{4,68},{6,70},{8,72},{10,74},{12,76},{14,78},{16,80}... | collective-permute-start | bytes 147464 | tf_op jit(solution)/shard_map/ppermute | solution.py:29
  31.2 7.1 %collective-permute-start.10 = (bf16[192,128]{1,0:T(8,128)(2,1)S(1)}, bf16[192,128]{1,0:T(8,128)(2,1)S(1)}, u32[]{:S(2)}, u32[]{:S(2)}) collective-permute-start(bf16[192,128]{1,0:T(8,128)(2,1)S(1)} %get-tuple-element.43), channel_id=1, source_target_pairs={{0,96},{2,98},{4,100},{6,102},{8,104},{10,106},{12,108},{14,110},{... | collective-permute-start | bytes 147464 | tf_op jit(solution)/shard_map/ppermute | solution.py:29
  34.5 8.0 %collective-permute-start.3 = (bf16[192,512]{1,0:T(8,128)(2,1)S(1)}, bf16[192,512]{1,0:T(8,128)(2,1)S(1)}, u32[]{:S(2)}, u32[]{:S(2)}) collective-permute-start(bf16[192,512]{1,0:T(8,128)(2,1)S(1)} %constant_dynamic-update-slice_fusion.refs_0_.refs_2_), channel_id=1, source_target_pairs={{0,4},{2,6},{4,8},{6,10},{8,12},{10,14},{12,0},{14,2},{16,20},{18,... | collective-permute-start | bytes 589832 | tf_op jit(solution)/shard_map/ppermute | solution.py:29
  34.6 9.1 %collective-permute-start.4 = (bf16[192,512]{1,0:T(8,128)(2,1)S(1)}, bf16[192,512]{1,0:T(8,128)(2,1)S(1)}, u32[]{:S(2)}, u32[]{:S(2)}) collective-permute-start(bf16[192,512]{1,0:T(8,128)(2,1)S(1)} %constant_dynamic-update-slice_fusion.refs_0_.refs_2_), channel_id=1, source_target_pairs={{0,8},{2,10},{4,12},{6,14},{8,0},{10,2},{12,4},{14,6},{16,24},{18,... | collective-permute-start | bytes 589832 | tf_op jit(solution)/shard_map/ppermute | solution.py:29
  37.0 6.7 %collective-permute-start.5 = (bf16[192,512]{1,0:T(8,128)(2,1)S(1)}, bf16[192,512]{1,0:T(8,128)(2,1)S(1)}, u32[]{:S(2)}, u32[]{:S(2)}) collective-permute-start(bf16[192,512]{1,0:T(8,128)(2,1)S(1)} %constant_dynamic-update-slice_fusion.refs_0_.refs_2_), channel_id=1, source_target_pairs={{0,12},{2,14},{4,0},{6,2},{8,4},{10,6},{12,8},{14,10},{16,28},{18,... | collective-permute-start | bytes 589832 | tf_op jit(solution)/shard_map/ppermute | solution.py:29
  39.1 7.8 %collective-permute-start.12 = (bf16[192,512]{1,0:T(8,128)(2,1)S(1)}, bf16[192,512]{1,0:T(8,128)(2,1)S(1)}, u32[]{:S(2)}, u32[]{:S(2)}) collective-permute-start(bf16[192,512]{1,0:T(8,128)(2,1)S(1)} %constant_dynamic-update-slice_fusion.4.refs_4_.refs_6_), channel_id=1, source_target_pairs={{0,2},{2,0},{4,6},{6,4},{8,10},{10,8},{12,14},{14,12},{16,18},{18,... | collective-permute-start | bytes 589832 | tf_op jit(solution)/shard_map/ppermute | solution.py:29
  42.4 9.1 %collective-permute-start.13 = (bf16[192,512]{1,0:T(8,128)(2,1)S(1)}, bf16[192,512]{1,0:T(8,128)(2,1)S(1)}, u32[]{:S(2)}, u32[]{:S(2)}) collective-permute-start(bf16[192,512]{1,0:T(8,128)(2,1)S(1)} %constant_dynamic-update-slice_fusion.4.refs_4_.refs_6_), channel_id=1, source_target_pairs={{0,18},{2,16},{4,22},{6,20},{8,26},{10,24},{12,30},{14,28},{16,2},... | collective-permute-start | bytes 589832 | tf_op jit(solution)/shard_map/ppermute | solution.py:29
  66.8 17.4 %collective-permute-start.16 = (bf16[192,512]{1,0:T(8,128)(2,1)S(1)}, bf16[192,512]{1,0:T(8,128)(2,1)S(1)}, u32[]{:S(2)}, u32[]{:S(2)}) collective-permute-start(bf16[192,512]{1,0:T(8,128)(2,1)S(1)} %get-tuple-element.47), channel_id=1, source_target_pairs={{0,16},{2,18},{4,20},{6,22},{8,24},{10,26},{12,28},{14,30},{16,0},... | collective-permute-start | bytes 589832 | tf_op jit(solution)/shard_map/ppermute | solution.py:29
  66.9 17.3 %collective-permute-start.17 = (bf16[192,512]{1,0:T(8,128)(2,1)S(1)}, bf16[192,512]{1,0:T(8,128)(2,1)S(1)}, u32[]{:S(2)}, u32[]{:S(2)}) collective-permute-start(bf16[192,512]{1,0:T(8,128)(2,1)S(1)} %get-tuple-element.48), channel_id=1, source_target_pairs={{0,2},{2,0},{4,6},{6,4},{8,10},{10,8},{12,14},{14,12},{16,18},{18,... | collective-permute-start | bytes 589832 | tf_op jit(solution)/shard_map/ppermute | solution.py:29
  68.4 15.8 %collective-permute-start.18 = (bf16[192,512]{1,0:T(8,128)(2,1)S(1)}, bf16[192,512]{1,0:T(8,128)(2,1)S(1)}, u32[]{:S(2)}, u32[]{:S(2)}) collective-permute-start(bf16[192,512]{1,0:T(8,128)(2,1)S(1)} %get-tuple-element.49), channel_id=1, source_target_pairs={{0,18},{2,16},{4,22},{6,20},{8,26},{10,24},{12,30},{14,28},{16,2},... | collective-permute-start | bytes 589832 | tf_op jit(solution)/shard_map/ppermute | solution.py:29
  81.4 6.6 %collective-permute-start.19 = (bf16[192,512]{1,0:T(8,128)(2,1)S(1)}, bf16[192,512]{1,0:T(8,128)(2,1)S(1)}, u32[]{:S(2)}, u32[]{:S(2)}) collective-permute-start(bf16[192,512]{1,0:T(8,128)(2,1)S(1)} %get-tuple-element.51), channel_id=1, source_target_pairs={{0,12},{2,14},{4,0},{6,2},{8,4},{10,6},{12,8},{14,10},{16,28},{18,... | collective-permute-start | bytes 589832 | tf_op jit(solution)/shard_map/ppermute | solution.py:29
  84.2 7.2 %collective-permute-start.21 = (bf16[192,512]{1,0:T(8,128)(2,1)S(1)}, bf16[192,512]{1,0:T(8,128)(2,1)S(1)}, u32[]{:S(2)}, u32[]{:S(2)}) collective-permute-start(bf16[192,512]{1,0:T(8,128)(2,1)S(1)} %get-tuple-element.53), channel_id=1, source_target_pairs={{0,4},{2,6},{4,8},{6,10},{8,12},{10,14},{12,0},{14,2},{16,20},{18,... | collective-permute-start | bytes 589832 | tf_op jit(solution)/shard_map/ppermute | solution.py:29
  93.2 7.6 %collective-permute-start.23 = (bf16[384,128]{1,0:T(8,128)(2,1)S(1)}, bf16[384,128]{1,0:T(8,128)(2,1)S(1)}, u32[]{:S(2)}, u32[]{:S(2)}) collective-permute-start(bf16[384,128]{1,0:T(8,128)(2,1)S(1)} %get-tuple-element.56), channel_id=1, source_target_pairs={{0,64},{2,66},{4,68},{6,70},{8,72},{10,74},{12,76},{14,78},{16,80}... | collective-permute-start | bytes 294920 | tf_op jit(solution)/shard_map/ppermute | solution.py:29
  95.5 6.2 %collective-permute-start.24 = (bf16[384,128]{1,0:T(8,128)(2,1)S(1)}, bf16[384,128]{1,0:T(8,128)(2,1)S(1)}, u32[]{:S(2)}, u32[]{:S(2)}) collective-permute-start(bf16[384,128]{1,0:T(8,128)(2,1)S(1)} %get-tuple-element.57), channel_id=1, source_target_pairs={{0,32},{2,34},{4,36},{6,38},{8,40},{10,42},{12,44},{14,46},{16,48}... | collective-permute-start | bytes 294920 | tf_op jit(solution)/shard_map/ppermute | solution.py:29
  103.9 15.0 %collective-permute-start.25 = (bf16[256,1536]{1,0:T(8,128)(2,1)S(1)}, bf16[256,1536]{1,0:T(8,128)(2,1)S(1)}, u32[]{:S(2)}, u32[]{:S(2)}) collective-permute-start(bf16[256,1536]{1,0:T(8,128)(2,1)S(1)} %shard_map.108.part), channel_id=1, source_target_pairs={{0,1},{1,0},{2,3},{3,2},{4,5},{5,4},{6,7},{7,6},{8,9},{9,8},{10,11... | collective-permute-start | bytes 2359304 | tf_op jit(solution)/shard_map/ppermute | solution.py:480
  129.1 11.2 %collective-permute-start.31 = (f32[32,192]{1,0:T(8,128)S(1)}, f32[32,192]{1,0:T(8,128)S(1)}, u32[]{:S(2)}, u32[]{:S(2)}) collective-permute-start(f32[32,192]{1,0:T(8,128)S(1)} %get-tuple-element.74), channel_id=1, source_target_pairs={{0,0},{1,65},{2,2},{3,67},{4,4},{5,69},{6,6},{7,71},{8,8},{9,73},{... | collective-permute-start | bytes 73736 | tf_op jit(solution)/shard_map/ppermute | solution.py:32
  134.0 6.3 %collective-permute-start.32 = (f32[32,192]{1,0:T(8,128)S(1)}, f32[32,192]{1,0:T(8,128)S(1)}, u32[]{:S(2)}, u32[]{:S(2)}) collective-permute-start(f32[32,192]{1,0:T(8,128)S(1)} %get-tuple-element.73), channel_id=1, source_target_pairs={{0,0},{1,97},{2,2},{3,99},{4,4},{5,101},{6,6},{7,103},{8,8},{9,105... | collective-permute-start | bytes 73736 | tf_op jit(solution)/shard_map/ppermute | solution.py:32
  137.1 6.8 %collective-permute-start.30 = (f32[32,192]{1,0:T(8,128)S(1)}, f32[32,192]{1,0:T(8,128)S(1)}, u32[]{:S(2)}, u32[]{:S(2)}) collective-permute-start(f32[32,192]{1,0:T(8,128)S(1)} %get-tuple-element.72), channel_id=1, source_target_pairs={{0,0},{1,33},{2,2},{3,35},{4,4},{5,37},{6,6},{7,39},{8,8},{9,41},{... | collective-permute-start | bytes 73736 | tf_op jit(solution)/shard_map/ppermute | solution.py:32
  149.2 8.7 %collective-permute-start.35 = (f32[32,24]{1,0:T(8,128)S(1)}, f32[32,24]{1,0:T(8,128)S(1)}, u32[]{:S(2)}, u32[]{:S(2)}) collective-permute-start(f32[32,24]{1,0:T(8,128)S(1)} %get-tuple-element.77), channel_id=1, source_target_pairs={{0,0},{1,9},{2,2},{3,11},{4,4},{5,13},{6,6},{7,15},{8,8},{9,1},{10... | collective-permute-start | bytes 9224 | tf_op jit(solution)/shard_map/ppermute | solution.py:32
  (22 other events, 251.5 us)

commit v4 on v1

--- a/solution.py
+++ b/solution.py
@@ -89,7 +89,7 @@
 
 
 def front_kernel(
-    idx, sharp, factor, x_hbm, w_hbm, o0, o1, o2, o3, qpay, qhat_o, khat_o, rad_o, pay, x, w, sem, *, heads, hs
+    factor, x_hbm, w_hbm, pay, qhat_o, khat_o, rad_o, x, w, sem, *, heads, hs
 ):
     x_copy = pltpu.make_async_copy(x_hbm, x, sem.at[0])
     x_copy.start()
@@ -122,17 +122,14 @@
         rad_o[heads + h : heads + h + 1] = kr
         pay[h, 0:hs] = kh.astype(BF16)
         pay[h, hs : 2 * hs] = vt[lo:hi].astype(BF16)
-        qpay[h] = (qh * (sharp[h] / math.sqrt(hs))).astype(BF16)
-    for s, o in enumerate((o0, o1, o2, o3)):
-        o[...] = pay[lax.rem(idx[0] + s, 4)]
-
-
-def fill_pad(pad, left, own, right):
+
+
+def fill_pad(pad, left, own, right, place):
     reach = left.shape[0]
     rows = own.shape[0]
-    pad[16 - reach : 16] = left[...].astype(F32)
+    pad[16 - reach : 16] = jnp.where(place > 0, left[...].astype(F32), 0.0)
     pad[16 : 16 + rows] = own[...].astype(F32)
-    pad[16 + rows : 16 + rows + reach] = right[...].astype(F32)
+    pad[16 + rows : 16 + rows + reach] = jnp.where(place < TM - 1, right[...].astype(F32), 0.0)
 
 
 def conv_rows(pad, taps, out, rows, flip):
@@ -154,20 +151,27 @@
     lax.fori_loop(0, out.shape[1] // 128, chunk, 0)
 
 
-def send_kernel(idx, left, own, right, taps, qpay, wf, o0, o1, o2, o3, gres, pad, g_s, *, hs):
-    fill_pad(pad, left, own, right)
+def send_kernel(idx, place, sharp, left, own, right, taps, qhat, pay, wf, o0, o1, o2, o3, gres_o, pad, g_s, gres, *, hs):
+    fill_pad(pad, left, own, right, place[0])
     conv_rows(pad, taps, gres, own.shape[0], True)
+    gres_o[...] = gres[...]
     gt = dotf(wf[...], gres[...].astype(BF16), 1, 1).astype(BF16)
     for h in range(4):
-        g_s[h] = gt[h * hs : (h + 1) * hs]
+        g_s[h, 0:hs] = (qhat[h * hs : (h + 1) * hs] * (sharp[h] / math.sqrt(hs))).astype(BF16)
+        g_s[h, hs : 2 * hs] = gt[h * hs : (h + 1) * hs]
     for s, o in enumerate((o0, o1, o2, o3)):
         at = lax.rem(idx[0] + s, 4)
-        o[0:hs] = qpay[at]
-        o[hs : 2 * hs] = g_s[at]
-
-
-def tail_kernel(part, other, x, factor, left, own, right, gres, res_o, sig_o, sums, first, last, pad, resf, gain, *, rows, taps):
-    fill_pad(pad, left, own, right)
+        o[0 : 2 * hs] = pay[at]
+        o[2 * hs : 4 * hs] = g_s[at]
+
+
+def tail_kernel(
+    place, part, other, x, factor, left, own, right, gres_hbm, res_o, sig_o, sums, first, last, pad, resf, gain, gres, sem,
+    *, rows, taps,
+):
+    fetch = pltpu.make_async_copy(gres_hbm, gres, sem)
+    fetch.start()
+    fill_pad(pad, left, own, right, place[0])
     reach = taps // 2
     total = part[0:rows].astype(F32) + other[0:rows].astype(F32)
     xf = x[...].astype(F32)
@@ -187,6 +191,7 @@
     scaled = grad * f
     m1 = jnp.mean(scaled, axis=-1, keepdims=True)
     m2 = jnp.mean(prod * f, axis=-1, keepdims=True)
+    fetch.wait()
     sig_o[...] = (gres[...] + (scaled - m1 - unit * m2) * inv).astype(BF16)
     half = sums.shape[2] // 128
 
@@ -209,9 +214,16 @@
         lax.fori_loop(0, half, chunk, 0)
 
 
-def out_kernel(left, own, right, taps, out, pad):
-    fill_pad(pad, left, own, right)
+def out_kernel(place, left, own, right, taps, out, pad):
+    fill_pad(pad, left, own, right, place[0])
     conv_rows(pad, taps, out, own.shape[0], False)
+
+
+def pack_kernel(p0, p1, p2, p3, kv, qg):
+    half, lanes = kv.shape[0], p0.shape[1]
+    for s, p in enumerate((p0, p1, p2, p3)):
+        kv[:, s * lanes : (s + 1) * lanes] = p[0:half]
+        qg[:, s * lanes : (s + 1) * lanes] = p[half : 2 * half]
 
 
 def to_rows(a):
@@ -354,9 +366,8 @@
 
 
 def rims(cells, head, tail):
-    ends = TM - 1
-    left = lax.ppermute(tail, "tm", [(i, i + 1) for i in range(ends)])
-    right = lax.ppermute(head, "tm", [(i + 1, i) for i in range(ends)])
+    left = lax.ppermute(tail, "tm", [(i, (i + 1) % TM) for i in range(TM)])
+    right = lax.ppermute(head, "tm", [((i + 1) % TM, i) for i in range(TM)])
     return left, cells, right
 
 
@@ -396,37 +407,35 @@
     reach = taps // 2
     t = lax.axis_index("tm")
     z4 = (t // 16).astype(jnp.int32).reshape(1)
+    place = t.astype(jnp.int32).reshape(1)
     x_in = input_signal[0]
     adj = mixture_adjoint[0]
     factor = standardize_factor[None]
     shape = jax.ShapeDtypeStruct
     adj_rims = rims(adj, adj[:reach], adj[rows - reach :])
-    piece = shape((2 * hs, rows), BF16)
-    *sent_kv, qpay, qhat, khat, rad = vcall(
+    piece = shape((4 * hs, rows), BF16)
+    pay, qhat, khat, rad = vcall(
         functools.partial(front_kernel, heads=heads, hs=hs),
-        (piece,) * 4 + (shape((heads, hs, rows), BF16), shape((flat, rows), F32), shape((flat, rows), F32), shape((2 * heads, rows), F32)),
+        (shape((heads, 2 * hs, rows), BF16), shape((flat, rows), F32), shape((flat, rows), F32), shape((2 * heads, rows), F32)),
         scratch=[
-            pltpu.VMEM((heads, 2 * hs, rows), BF16),
             pltpu.VMEM((rows, width), BF16),
             pltpu.VMEM((3, width, flat), BF16),
             pltpu.SemaphoreType.DMA((4,)),
         ],
-        smem=2,
         n_in=1,
         raw=2,
-    )(z4, score_sharpening, factor, x_in, triple_projection)
-    got_kv = [sent_kv[0]] + ordered(lambda s: move_z4(sent_kv[s], s), (2, 1, 3))
+    )(factor, x_in, triple_projection)
     pad = pltpu.VMEM((rows + 32, width), F32)
-    *sent_qg, grad_res = vcall(
+    *sent, grad_res = vcall(
         functools.partial(send_kernel, hs=hs),
         (piece,) * 4 + (shape((rows, width), F32),),
-        scratch=[pad, pltpu.VMEM((4, hs, rows), BF16)],
-        smem=1,
-        n_in=6,
-    )(z4, *adj_rims, filter_taps, qpay, final_projection)
-    got_qg = [sent_qg[0]] + ordered(lambda s: move_z4(sent_qg[s], s), (2, 1, 3))
-    kv0 = jnp.concatenate(got_kv, axis=1)
-    qg0 = jnp.concatenate(got_qg, axis=1)
+        scratch=[pad, pltpu.VMEM((4, 2 * hs, rows), BF16), pltpu.VMEM((rows, width), F32)],
+        out_hbm=(4,),
+        smem=3,
+        n_in=7,
+    )(z4, place, score_sharpening, *adj_rims, filter_taps, qhat, pay, final_projection)
+    got = [sent[0]] + ordered(lambda s: move_z4(sent[s], s), (2, 1, 3))
+    kv0, qg0 = vcall(pack_kernel, (shape((2 * hs, 4 * rows), BF16),) * 2, n_in=4)(*got)
     kv = [kv0] + ordered(lambda s: move_x(kv0, s), (2, 1, 3))
     qg = [qg0] + ordered(lambda m: move_zy(qg0, m), (3, 2, 1))
     span = 4 * rows
@@ -456,14 +465,22 @@
     residual, signal_adjoint, sums, first, last = vcall(
         functools.partial(tail_kernel, rows=rows, taps=taps),
         (shape((rows, width), BF16), shape((rows, width), BF16), shape((2, taps + 1, width // 2), F32), edge, edge),
-        scratch=[pad, pltpu.VMEM((rows, width), F32), pltpu.VMEM((1, width), F32)],
-        n_in=8,
+        scratch=[
+            pad,
+            pltpu.VMEM((rows, width), F32),
+            pltpu.VMEM((1, width), F32),
+            pltpu.VMEM((rows, width), F32),
+            pltpu.SemaphoreType.DMA(()),
+        ],
+        smem=1,
+        n_in=7,
+        raw=1,
         out_hbm=(1,),
-    )(part, other, x_in, factor, *adj_rims, grad_res)
+    )(place, part, other, x_in, factor, *adj_rims, grad_res)
     res_rims = rims(residual, first, last)
-    sublayer_result = vcall(out_kernel, shape((rows, width), BF16), scratch=[pad], n_in=4, out_hbm=(0,))(*res_rims, filter_taps)
+    result = vcall(out_kernel, shape((rows, width), BF16), scratch=[pad], smem=1, n_in=4)(place, *res_rims, filter_taps)
     sums = scatter_sum(sums, batches)
-    return (sublayer_result[None], signal_adjoint[None], sums[:taps], sums[taps])
+    return (result[None], signal_adjoint[None], sums[:taps], sums[taps])
 
 
 def solution(mesh):

time: 174 us -> 161 us (0.925)
  starting transfers between devices: 75.1 us -> 69.9 us
  local copies, waits for them, and re-layouts: 7.77 us -> 4 us
  waiting for transfers between devices: 51.4 us -> 48 us
    ppermute x4, starting transfers between devices: 15.6 us -> 8.06 us  [the longest x2 7.03 us: rims(): left = lax.ppermute(tail, 'tm', [(i, (i + 1) % TM) for i in range(TM)])]
    ppermute x12 -> x9, starting transfers between devices: 31.1 us -> 24.5 us  [move_z4(): return lax.ppermute(a, 'tm', pairs)]
    ppermute x10, starting transfers between devices: 17.7 us -> 23.3 us  [move_zy(): return lax.ppermute(a, 'tm', pairs)]
    unnamed x39 -> x16, local copies, waits for them, and re-layouts: 6.03 us -> 1.46 us
    ppermute x4, waiting for transfers between devices: 12 us -> 8.28 us  [the longest x2 8.27 us: rims(): right = lax.ppermute(head, 'tm', [((i + 1) % TM, i) for i in range(TM)])]
    ppermute x12 -> x9, waiting for transfers between devices: 11.3 us -> 14.8 us  [move_z4(): return lax.ppermute(a, 'tm', pairs)]
    ppermute x9, starting transfers between devices: 10.6 us -> 13.6 us  [move_x(): return lax.ppermute(a, 'tm', pairs)]
    ppermute x10, waiting for transfers between devices: 14.1 us -> 11.5 us  [move_zy(): return lax.ppermute(a, 'tm', pairs)]
  transfers between devices with their start and end apart: 37 -> 34, of which waited for: 20 -> 19; matrix products, arithmetic and copies ran while one was open for 0% -> 1% of each run, Pallas kernels for 11% -> 11%
where the time goes in v4:
time: 161 us
  starting transfers between devices  69.9 us (43%)
  waiting for transfers between devices  48 us (30%)
  Pallas kernels  37.6 us (23%)
  local copies, waits for them, and re-layouts  4 us (2%)
    pallas_call x10, Pallas kernels, run(): return call(*args)  37.6 us
    ppermute x9, starting transfers between devices, move_z4(): return lax.ppermute(a, 'tm', pairs)  24.5 us
    ppermute x10, starting transfers between devices, move_zy(): return lax.ppermute(a, 'tm', pairs)  23.3 us
    ppermute x9, waiting for transfers between devices, move_z4(): return lax.ppermute(a, 'tm', pairs)  14.8 us
    ppermute x9, starting transfers between devices, move_x(): return lax.ppermute(a, 'tm', pairs)  13.6 us
    ppermute x10, waiting for transfers between devices, move_zy(): return lax.ppermute(a, 'tm', pairs)  11.5 us
    ppermute x2, waiting for transfers between devices, rims(): right = lax.ppermute(head, 'tm', [((i + 1) % TM, i) for i in range(TM)])  8.27 us
    ppermute x2, starting transfers between devices, rims(): left = lax.ppermute(tail, 'tm', [(i, (i + 1) % TM) for i in range(TM)])  7.03 us
  transfers between devices with their start and end apart: 34, of which 19 were waited for; matrix products, arithmetic and copies ran while one was open for 1% of the time, Pallas kernels for 11%

profile of v4, /device:TPU:30, one launch (start us, length us, event | category | flops | bytes accessed | tf_op | source)
XLA Modules:
  0.0 160.7 jit_solution(14308792269229300301)
XLA Ops:
  5.9 2.8 %shard_map.102 = (bf16[4,192,128]{2,1,0:T(8,128)(2,1)S(1)}, f32[384,128]{1,0:T(8,128)S(1)}, f32[384,128]{1,0:T(8,128)S(1)}, f32[8,128]{1,0:T(8,128)S(1)}) custom-call(f32[1,1536]{1,0:T(1,128)S(1)} %broadcast_in_dim.9.factor, bf16[128,1536]{1,0:T(8,128)(2,1)} %bitcast.20, bf16[3,1536,384]{2,1,0:T(8,128)(2,1)} %w.1), custom_call_target="tpu_custom_call" | custom-call | tf_op jit(solution)/shard_map/pallas_call | solution.py:80
  8.8 4.0 %collective-permute-done.1.right = bf16[15,1536]{1,0:T(8,128)(2,1)S(1)} collective-permute-done((bf16[15,1536]{1,0:T(8,128)(2,1)S(1)}, bf16[15,1536]{1,0:T(8,128)(2,1)S(1)}, u32[]{:S(2)}, u32[]{:S(2)}) %collective-permute-start.1) | collective-permute-done | bytes 46112 | tf_op jit(solution)/shard_map/ppermute | solution.py:370
  12.8 5.1 %shard_map.103 = (bf16[384,128]{1,0:T(8,128)(2,1)S(1)}, bf16[384,128]{1,0:T(8,128)(2,1)S(1)}, bf16[384,128]{1,0:T(8,128)(2,1)S(1)}, bf16[384,128]{1,0:T(8,128)(2,1)S(1)}, f32[128,1536]{1,0:T(8,128)S(1)}) custom-call(s32[1]{0:T(128)} %bitcast.1.idx, s32[1]{0:T(128)} %bitcast.place, f32[4]{0:T(128)S(1)} %copy-done.6, ...), custom_call_target="tpu_custom_call" | custom-call | tf_op jit(solution)/shard_map/pallas_call | solution.py:80
  18.0 3.3 %collective-permute-start.2 = (bf16[384,128]{1,0:T(8,128)(2,1)S(1)}, bf16[384,128]{1,0:T(8,128)(2,1)S(1)}, u32[]{:S(2)}, u32[]{:S(2)}) collective-permute-start(bf16[384,128]{1,0:T(8,128)(2,1)S(1)} %get-tuple-element.37), channel_id=1, source_target_pairs={{0,32},{2,34},{4,36},{6,38},{8,40},{10,42},{12,44},{14,46},{16,48}... | collective-permute-start | bytes 294920 | tf_op jit(solution)/shard_map/ppermute | solution.py:32
  21.3 4.5 %collective-permute-start.3 = (bf16[384,128]{1,0:T(8,128)(2,1)S(1)}, bf16[384,128]{1,0:T(8,128)(2,1)S(1)}, u32[]{:S(2)}, u32[]{:S(2)}) collective-permute-start(bf16[384,128]{1,0:T(8,128)(2,1)S(1)} %get-tuple-element.38), channel_id=1, source_target_pairs={{0,64},{2,66},{4,68},{6,70},{8,72},{10,74},{12,76},{14,78},{16,80}... | collective-permute-start | bytes 294920 | tf_op jit(solution)/shard_map/ppermute | solution.py:32
  25.8 2.7 %collective-permute-start.4 = (bf16[384,128]{1,0:T(8,128)(2,1)S(1)}, bf16[384,128]{1,0:T(8,128)(2,1)S(1)}, u32[]{:S(2)}, u32[]{:S(2)}) collective-permute-start(bf16[384,128]{1,0:T(8,128)(2,1)S(1)} %get-tuple-element.39), channel_id=1, source_target_pairs={{0,96},{2,98},{4,100},{6,102},{8,104},{10,106},{12,108},{14,110},{... | collective-permute-start | bytes 294920 | tf_op jit(solution)/shard_map/ppermute | solution.py:32
  28.5 3.8 %collective-permute-done.3.p2 = bf16[384,128]{1,0:T(8,128)(2,1)S(1)} collective-permute-done((bf16[384,128]{1,0:T(8,128)(2,1)S(1)}, bf16[384,128]{1,0:T(8,128)(2,1)S(1)}, u32[]{:S(2)}, u32[]{:S(2)}) %collective-permute-start.3) | collective-permute-done | bytes 98336 | tf_op jit(solution)/shard_map/ppermute | solution.py:32
  35.9 3.2 %collective-permute-start.8 = (bf16[192,512]{1,0:T(8,128)(2,1)S(1)}, bf16[192,512]{1,0:T(8,128)(2,1)S(1)}, u32[]{:S(2)}, u32[]{:S(2)}) collective-permute-start(bf16[192,512]{1,0:T(8,128)(2,1)S(1)} %get-tuple-element.41.refs_4_.refs_6_), channel_id=1, source_target_pairs={{0,16},{2,18},{4,20},{6,22},{8,24},{10,26},{12,28},{14,30},{16,0},... | collective-permute-start | bytes 589832 | tf_op jit(solution)/shard_map/ppermute | solution.py:48
  43.2 6.0 %collective-permute-done.9.refs_6_.refs_8_ = bf16[192,512]{1,0:T(8,128)(2,1)S(1)} collective-permute-done((bf16[192,512]{1,0:T(8,128)(2,1)S(1)}, bf16[192,512]{1,0:T(8,128)(2,1)S(1)}, u32[]{:S(2)}, u32[]{:S(2)}) %collective-permute-start.9) | collective-permute-done | bytes 196640 | tf_op jit(solution)/shard_map/ppermute | solution.py:48
  49.2 8.2 %shard_map.105 = (f32[4,2,512]{2,1,0:T(2,128)S(1)}, f32[4,288,512]{2,1,0:T(8,128)S(1)}) custom-call(bf16[192,512]{1,0:T(8,128)(2,1)S(1)} %get-tuple-element.40.refs_0_.refs_2_, bf16[192,512]{1,0:T(8,128)(2,1)S(1)} %collective-permute-done.5.refs_1_.refs_3_, bf16[192,512]{1,0:T(8,128)(2,1)S(1)} %collective-permute-done.6.refs_2_.refs_4_, ...), custom_call_target="tpu_custom_call" | custom-call | tf_op jit(solution)/shard_map/pallas_call | solution.py:80
  61.4 4.0 %collective-permute-start.12 = (f32[4,2,512]{2,1,0:T(2,128)S(1)}, f32[4,2,512]{2,1,0:T(2,128)S(1)}, u32[]{:S(2)}, u32[]{:S(2)}) collective-permute-start(f32[4,2,512]{2,1,0:T(2,128)S(1)} %maximum_add_fusion.te0.refs_0_), channel_id=1, source_target_pairs={{0,2},{2,0},{4,6},{6,4},{8,10},{10,8},{12,14},{14,12},{16,18},{18,... | collective-permute-start | bytes 49160 | tf_op jit(solution)/shard_map/ppermute | solution.py:48
  72.4 10.4 %shard_map.107 = (bf16[192,512]{1,0:T(8,128)(2,1)S(1)}, bf16[192,512]{1,0:T(8,128)(2,1)S(1)}, bf16[192,512]{1,0:T(8,128)(2,1)S(1)}, bf16[192,512]{1,0:T(8,128)(2,1)S(1)}) custom-call(f32[4,2,512]{2,1,0:T(2,128)S(1)} %maximum_add_fusion.te0.refs_0_, f32[4,2,512]{2,1,0:T(2,128)S(1)} %collective-permute-done.12.te1.refs_1_, ...), custom_call_target="tpu_custom_call" | custom-call | tf_op jit(solution)/shard_map/pallas_call | solution.py:80
  84.5 3.7 %collective-permute-start.17 = (bf16[192,512]{1,0:T(8,128)(2,1)S(1)}, bf16[192,512]{1,0:T(8,128)(2,1)S(1)}, u32[]{:S(2)}, u32[]{:S(2)}) collective-permute-start(bf16[192,512]{1,0:T(8,128)(2,1)S(1)} %get-tuple-element.50), channel_id=1, source_target_pairs={{0,8},{2,10},{4,12},{6,14},{8,0},{10,2},{12,4},{14,6},{16,24},{18,... | collective-permute-start | bytes 589832 | tf_op jit(solution)/shard_map/ppermute | solution.py:40
  90.5 3.5 %collective-permute-done.17.refs_6_ = bf16[192,512]{1,0:T(8,128)(2,1)S(1)} collective-permute-done((bf16[192,512]{1,0:T(8,128)(2,1)S(1)}, bf16[192,512]{1,0:T(8,128)(2,1)S(1)}, u32[]{:S(2)}, u32[]{:S(2)}) %collective-permute-start.17) | collective-permute-done | bytes 196640 | tf_op jit(solution)/shard_map/ppermute | solution.py:40
  94.2 3.9 %collective-permute-start.19 = (bf16[384,128]{1,0:T(8,128)(2,1)S(1)}, bf16[384,128]{1,0:T(8,128)(2,1)S(1)}, u32[]{:S(2)}, u32[]{:S(2)}) collective-permute-start(bf16[384,128]{1,0:T(8,128)(2,1)S(1)} %get-tuple-element.53), channel_id=1, source_target_pairs={{0,96},{2,98},{4,100},{6,102},{8,104},{10,106},{12,108},{14,110},{... | collective-permute-start | bytes 294920 | tf_op jit(solution)/shard_map/ppermute | solution.py:32
  98.1 2.6 %collective-permute-start.20 = (bf16[384,128]{1,0:T(8,128)(2,1)S(1)}, bf16[384,128]{1,0:T(8,128)(2,1)S(1)}, u32[]{:S(2)}, u32[]{:S(2)}) collective-permute-start(bf16[384,128]{1,0:T(8,128)(2,1)S(1)} %get-tuple-element.54), channel_id=1, source_target_pairs={{0,64},{2,66},{4,68},{6,70},{8,72},{10,74},{12,76},{14,78},{16,80}... | collective-permute-start | bytes 294920 | tf_op jit(solution)/shard_map/ppermute | solution.py:32
  102.0 4.8 %collective-permute-done.20.b2 = bf16[384,128]{1,0:T(8,128)(2,1)S(1)} collective-permute-done((bf16[384,128]{1,0:T(8,128)(2,1)S(1)}, bf16[384,128]{1,0:T(8,128)(2,1)S(1)}, u32[]{:S(2)}, u32[]{:S(2)}) %collective-permute-start.20) | collective-permute-done | bytes 98336 | tf_op jit(solution)/shard_map/ppermute | solution.py:32
  112.6 4.5 %shard_map.110 = (bf16[128,1536]{1,0:T(8,128)(2,1)S(1)}, bf16[128,1536]{1,0:T(8,128)(2,1)}, f32[2,32,768]{2,1,0:T(8,128)S(1)}, bf16[15,1536]{1,0:T(8,128)(2,1)S(1)}, bf16[15,1536]{1,0:T(8,128)(2,1)S(1)}) custom-call(s32[1]{0:T(128)} %bitcast.place, bf16[256,1536]{1,0:T(8,128)(2,1)S(1)} %shard_map.109.part, ...), custom_call_target="tpu_custom_call" | custom-call | tf_op jit(solution)/shard_map/pallas_call | solution.py:80
  117.2 4.8 %collective-permute-done.25 = f32[32,768]{1,0:T(8,128)S(1)} collective-permute-done((f32[32,768]{1,0:T(8,128)S(1)}, f32[32,768]{1,0:T(8,128)S(1)}, u32[]{:S(2)}, u32[]{:S(2)}) %collective-permute-start.25) | collective-permute-done | bytes 98336 | tf_op jit(solution)/shard_map/ppermute | solution.py:385
  122.1 3.2 %collective-permute-start.27 = (f32[32,192]{1,0:T(8,128)S(1)}, f32[32,192]{1,0:T(8,128)S(1)}, u32[]{:S(2)}, u32[]{:S(2)}) collective-permute-start(f32[32,192]{1,0:T(8,128)S(1)} %get-tuple-element.72), channel_id=1, source_target_pairs={{0,64},{2,66},{4,68},{6,70},{8,72},{10,74},{12,76},{14,78},{16,80}... | collective-permute-start | bytes 73736 | tf_op jit(solution)/shard_map/ppermute | solution.py:32
  141.6 4.5 %collective-permute-start.23 = (bf16[15,1536]{1,0:T(8,128)(2,1)S(1)}, bf16[15,1536]{1,0:T(8,128)(2,1)S(1)}, u32[]{:S(2)}, u32[]{:S(2)}) collective-permute-start(bf16[15,1536]{1,0:T(8,128)(2,1)S(1)} %get-tuple-element.59), channel_id=1, source_target_pairs={{0,2},{2,4},{4,6},{6,8},{8,10},{10,12},{12,14},{14,16},{16,18},{18... | collective-permute-start | bytes 138248 | tf_op jit(solution)/shard_map/ppermute | solution.py:369
  146.2 4.2 %collective-permute-start.33 = (f32[32,12]{1,0:T(8,128)S(1)}, f32[32,12]{1,0:T(8,128)S(1)}, u32[]{:S(2)}, u32[]{:S(2)}) collective-permute-start(f32[32,12]{1,0:T(8,128)S(1)} %constant_dynamic-slice_fusion), channel_id=1, source_target_pairs={{0,2},{2,0},{4,6},{6,4},{8,10},{10,8},{12,14},{14,12},{16,18},{18,... | collective-permute-start | bytes 4616 | tf_op jit(solution)/shard_map/ppermute | solution.py:48
  150.4 4.3 %collective-permute-done.24.right = bf16[15,1536]{1,0:T(8,128)(2,1)S(1)} collective-permute-done((bf16[15,1536]{1,0:T(8,128)(2,1)S(1)}, bf16[15,1536]{1,0:T(8,128)(2,1)S(1)}, u32[]{:S(2)}, u32[]{:S(2)}) %collective-permute-start.24) | collective-permute-done | bytes 46112 | tf_op jit(solution)/shard_map/ppermute | solution.py:370
  154.7 4.1 %shard_map.111 = bf16[128,1536]{1,0:T(8,128)(2,1)S(1)} custom-call(s32[1]{0:T(128)} %bitcast.place, bf16[15,1536]{1,0:T(8,128)(2,1)S(1)} %collective-permute-done.23.left, bf16[128,1536]{1,0:T(8,128)(2,1)S(1)} %get-tuple-element.60.own, bf16[15,1536]{1,0:T(8,128)(2,1)S(1)} %collective-permute-done.24.right, f32[31,1536]{1,0:T(8,128)S(1)} %copy-done.5), custom_call_target="tpu_custom_call" | custom-call | tf_op jit(solution)/shard_map/pallas_call | solution.py:80
  (85 shorter events, 53.9 us)
Async XLA Ops:
  1.6 7.2 %collective-permute-start = (bf16[15,1536]{1,0:T(8,128)(2,1)S(1)}, bf16[15,1536]{1,0:T(8,128)(2,1)S(1)}, u32[]{:S(2)}, u32[]{:S(2)}) collective-permute-start(bf16[15,1536]{1,0:T(8,128)(2,1)S(1)} %get-tuple-element.69), channel_id=1, source_target_pairs={{0,2},{2,4},{4,6},{6,8},{8,10},{10,12},{12,14},{14,16},{16,18},{18... | collective-permute-start | bytes 138248 | tf_op jit(solution)/shard_map/ppermute | solution.py:369
  4.2 8.6 %collective-permute-start.1 = (bf16[15,1536]{1,0:T(8,128)(2,1)S(1)}, bf16[15,1536]{1,0:T(8,128)(2,1)S(1)}, u32[]{:S(2)}, u32[]{:S(2)}) collective-permute-start(bf16[15,1536]{1,0:T(8,128)(2,1)S(1)} %get-tuple-element.68), channel_id=1, source_target_pairs={{2,0},{4,2},{6,4},{8,6},{10,8},{12,10},{14,12},{16,14},{18,16},{20... | collective-permute-start | bytes 138248 | tf_op jit(solution)/shard_map/ppermute | solution.py:370
  18.0 10.5 %collective-permute-start.2 = (bf16[384,128]{1,0:T(8,128)(2,1)S(1)}, bf16[384,128]{1,0:T(8,128)(2,1)S(1)}, u32[]{:S(2)}, u32[]{:S(2)}) collective-permute-start(bf16[384,128]{1,0:T(8,128)(2,1)S(1)} %get-tuple-element.37), channel_id=1, source_target_pairs={{0,32},{2,34},{4,36},{6,38},{8,40},{10,42},{12,44},{14,46},{16,48}... | collective-permute-start | bytes 294920 | tf_op jit(solution)/shard_map/ppermute | solution.py:32
  21.3 10.9 %collective-permute-start.3 = (bf16[384,128]{1,0:T(8,128)(2,1)S(1)}, bf16[384,128]{1,0:T(8,128)(2,1)S(1)}, u32[]{:S(2)}, u32[]{:S(2)}) collective-permute-start(bf16[384,128]{1,0:T(8,128)(2,1)S(1)} %get-tuple-element.38), channel_id=1, source_target_pairs={{0,64},{2,66},{4,68},{6,70},{8,72},{10,74},{12,76},{14,78},{16,80}... | collective-permute-start | bytes 294920 | tf_op jit(solution)/shard_map/ppermute | solution.py:32
  25.8 7.9 %collective-permute-start.4 = (bf16[384,128]{1,0:T(8,128)(2,1)S(1)}, bf16[384,128]{1,0:T(8,128)(2,1)S(1)}, u32[]{:S(2)}, u32[]{:S(2)}) collective-permute-start(bf16[384,128]{1,0:T(8,128)(2,1)S(1)} %get-tuple-element.39), channel_id=1, source_target_pairs={{0,96},{2,98},{4,100},{6,102},{8,104},{10,106},{12,108},{14,110},{... | collective-permute-start | bytes 294920 | tf_op jit(solution)/shard_map/ppermute | solution.py:32
  33.9 8.2 %collective-permute-start.6 = (bf16[192,512]{1,0:T(8,128)(2,1)S(1)}, bf16[192,512]{1,0:T(8,128)(2,1)S(1)}, u32[]{:S(2)}, u32[]{:S(2)}) collective-permute-start(bf16[192,512]{1,0:T(8,128)(2,1)S(1)} %get-tuple-element.40.refs_0_.refs_2_), channel_id=1, source_target_pairs={{0,8},{2,10},{4,12},{6,14},{8,0},{10,2},{12,4},{14,6},{16,24},{18,... | collective-permute-start | bytes 589832 | tf_op jit(solution)/shard_map/ppermute | solution.py:40
  35.0 8.2 %collective-permute-start.7 = (bf16[192,512]{1,0:T(8,128)(2,1)S(1)}, bf16[192,512]{1,0:T(8,128)(2,1)S(1)}, u32[]{:S(2)}, u32[]{:S(2)}) collective-permute-start(bf16[192,512]{1,0:T(8,128)(2,1)S(1)} %get-tuple-element.40.refs_0_.refs_2_), channel_id=1, source_target_pairs={{0,12},{2,14},{4,0},{6,2},{8,4},{10,6},{12,8},{14,10},{16,28},{18,... | collective-permute-start | bytes 589832 | tf_op jit(solution)/shard_map/ppermute | solution.py:40
  35.9 7.4 %collective-permute-start.8 = (bf16[192,512]{1,0:T(8,128)(2,1)S(1)}, bf16[192,512]{1,0:T(8,128)(2,1)S(1)}, u32[]{:S(2)}, u32[]{:S(2)}) collective-permute-start(bf16[192,512]{1,0:T(8,128)(2,1)S(1)} %get-tuple-element.41.refs_4_.refs_6_), channel_id=1, source_target_pairs={{0,16},{2,18},{4,20},{6,22},{8,24},{10,26},{12,28},{14,30},{16,0},... | collective-permute-start | bytes 589832 | tf_op jit(solution)/shard_map/ppermute | solution.py:48
  39.1 10.1 %collective-permute-start.9 = (bf16[192,512]{1,0:T(8,128)(2,1)S(1)}, bf16[192,512]{1,0:T(8,128)(2,1)S(1)}, u32[]{:S(2)}, u32[]{:S(2)}) collective-permute-start(bf16[192,512]{1,0:T(8,128)(2,1)S(1)} %get-tuple-element.41.refs_4_.refs_6_), channel_id=1, source_target_pairs={{0,2},{2,0},{4,6},{6,4},{8,10},{10,8},{12,14},{14,12},{16,18},{18,... | collective-permute-start | bytes 589832 | tf_op jit(solution)/shard_map/ppermute | solution.py:48
  39.5 9.7 %collective-permute-start.10 = (bf16[192,512]{1,0:T(8,128)(2,1)S(1)}, bf16[192,512]{1,0:T(8,128)(2,1)S(1)}, u32[]{:S(2)}, u32[]{:S(2)}) collective-permute-start(bf16[192,512]{1,0:T(8,128)(2,1)S(1)} %get-tuple-element.41.refs_4_.refs_6_), channel_id=1, source_target_pairs={{0,18},{2,16},{4,22},{6,20},{8,26},{10,24},{12,30},{14,28},{16,2},... | collective-permute-start | bytes 589832 | tf_op jit(solution)/shard_map/ppermute | solution.py:48
  67.4 20.8 %collective-permute-start.13 = (bf16[192,512]{1,0:T(8,128)(2,1)S(1)}, bf16[192,512]{1,0:T(8,128)(2,1)S(1)}, u32[]{:S(2)}, u32[]{:S(2)}) collective-permute-start(bf16[192,512]{1,0:T(8,128)(2,1)S(1)} %get-tuple-element.45), channel_id=1, source_target_pairs={{0,16},{2,18},{4,20},{6,22},{8,24},{10,26},{12,28},{14,30},{16,0},... | collective-permute-start | bytes 589832 | tf_op jit(solution)/shard_map/ppermute | solution.py:48
  68.6 20.5 %collective-permute-start.14 = (bf16[192,512]{1,0:T(8,128)(2,1)S(1)}, bf16[192,512]{1,0:T(8,128)(2,1)S(1)}, u32[]{:S(2)}, u32[]{:S(2)}) collective-permute-start(bf16[192,512]{1,0:T(8,128)(2,1)S(1)} %get-tuple-element.46), channel_id=1, source_target_pairs={{0,2},{2,0},{4,6},{6,4},{8,10},{10,8},{12,14},{14,12},{16,18},{18,... | collective-permute-start | bytes 589832 | tf_op jit(solution)/shard_map/ppermute | solution.py:48
  71.1 18.1 %collective-permute-start.15 = (bf16[192,512]{1,0:T(8,128)(2,1)S(1)}, bf16[192,512]{1,0:T(8,128)(2,1)S(1)}, u32[]{:S(2)}, u32[]{:S(2)}) collective-permute-start(bf16[192,512]{1,0:T(8,128)(2,1)S(1)} %get-tuple-element.47), channel_id=1, source_target_pairs={{0,18},{2,16},{4,22},{6,20},{8,26},{10,24},{12,30},{14,28},{16,2},... | collective-permute-start | bytes 589832 | tf_op jit(solution)/shard_map/ppermute | solution.py:48
  82.8 7.7 %collective-permute-start.16 = (bf16[192,512]{1,0:T(8,128)(2,1)S(1)}, bf16[192,512]{1,0:T(8,128)(2,1)S(1)}, u32[]{:S(2)}, u32[]{:S(2)}) collective-permute-start(bf16[192,512]{1,0:T(8,128)(2,1)S(1)} %get-tuple-element.49), channel_id=1, source_target_pairs={{0,12},{2,14},{4,0},{6,2},{8,4},{10,6},{12,8},{14,10},{16,28},{18,... | collective-permute-start | bytes 589832 | tf_op jit(solution)/shard_map/ppermute | solution.py:40
  84.5 9.4 %collective-permute-start.17 = (bf16[192,512]{1,0:T(8,128)(2,1)S(1)}, bf16[192,512]{1,0:T(8,128)(2,1)S(1)}, u32[]{:S(2)}, u32[]{:S(2)}) collective-permute-start(bf16[192,512]{1,0:T(8,128)(2,1)S(1)} %get-tuple-element.50), channel_id=1, source_target_pairs={{0,8},{2,10},{4,12},{6,14},{8,0},{10,2},{12,4},{14,6},{16,24},{18,... | collective-permute-start | bytes 589832 | tf_op jit(solution)/shard_map/ppermute | solution.py:40
  94.2 7.8 %collective-permute-start.19 = (bf16[384,128]{1,0:T(8,128)(2,1)S(1)}, bf16[384,128]{1,0:T(8,128)(2,1)S(1)}, u32[]{:S(2)}, u32[]{:S(2)}) collective-permute-start(bf16[384,128]{1,0:T(8,128)(2,1)S(1)} %get-tuple-element.53), channel_id=1, source_target_pairs={{0,96},{2,98},{4,100},{6,102},{8,104},{10,106},{12,108},{14,110},{... | collective-permute-start | bytes 294920 | tf_op jit(solution)/shard_map/ppermute | solution.py:32
  98.1 8.8 %collective-permute-start.20 = (bf16[384,128]{1,0:T(8,128)(2,1)S(1)}, bf16[384,128]{1,0:T(8,128)(2,1)S(1)}, u32[]{:S(2)}, u32[]{:S(2)}) collective-permute-start(bf16[384,128]{1,0:T(8,128)(2,1)S(1)} %get-tuple-element.54), channel_id=1, source_target_pairs={{0,64},{2,66},{4,68},{6,70},{8,72},{10,74},{12,76},{14,78},{16,80}... | collective-permute-start | bytes 294920 | tf_op jit(solution)/shard_map/ppermute | solution.py:32
  100.7 7.2 %collective-permute-start.21 = (bf16[384,128]{1,0:T(8,128)(2,1)S(1)}, bf16[384,128]{1,0:T(8,128)(2,1)S(1)}, u32[]{:S(2)}, u32[]{:S(2)}) collective-permute-start(bf16[384,128]{1,0:T(8,128)(2,1)S(1)} %get-tuple-element.55), channel_id=1, source_target_pairs={{0,32},{2,34},{4,36},{6,38},{8,40},{10,42},{12,44},{14,46},{16,48}... | collective-permute-start | bytes 294920 | tf_op jit(solution)/shard_map/ppermute | solution.py:32
  122.1 7.9 %collective-permute-start.27 = (f32[32,192]{1,0:T(8,128)S(1)}, f32[32,192]{1,0:T(8,128)S(1)}, u32[]{:S(2)}, u32[]{:S(2)}) collective-permute-start(f32[32,192]{1,0:T(8,128)S(1)} %get-tuple-element.72), channel_id=1, source_target_pairs={{0,64},{2,66},{4,68},{6,70},{8,72},{10,74},{12,76},{14,78},{16,80}... | collective-permute-start | bytes 73736 | tf_op jit(solution)/shard_map/ppermute | solution.py:32
  136.4 9.7 %collective-permute-start.31 = (f32[32,24]{1,0:T(8,128)S(1)}, f32[32,24]{1,0:T(8,128)S(1)}, u32[]{:S(2)}, u32[]{:S(2)}) collective-permute-start(f32[32,24]{1,0:T(8,128)S(1)} %get-tuple-element.75), channel_id=1, source_target_pairs={{0,8},{2,10},{4,12},{6,14},{8,0},{10,2},{12,4},{14,6},{16,24},{18,... | collective-permute-start | bytes 9224 | tf_op jit(solution)/shard_map/ppermute | solution.py:40
  138.4 7.7 %collective-permute-start.32 = (f32[32,24]{1,0:T(8,128)S(1)}, f32[32,24]{1,0:T(8,128)S(1)}, u32[]{:S(2)}, u32[]{:S(2)}) collective-permute-start(f32[32,24]{1,0:T(8,128)S(1)} %get-tuple-element.74), channel_id=1, source_target_pairs={{0,12},{2,14},{4,0},{6,2},{8,4},{10,6},{12,8},{14,10},{16,28},{18,... | collective-permute-start | bytes 9224 | tf_op jit(solution)/shard_map/ppermute | solution.py:40
  141.6 8.8 %collective-permute-start.23 = (bf16[15,1536]{1,0:T(8,128)(2,1)S(1)}, bf16[15,1536]{1,0:T(8,128)(2,1)S(1)}, u32[]{:S(2)}, u32[]{:S(2)}) collective-permute-start(bf16[15,1536]{1,0:T(8,128)(2,1)S(1)} %get-tuple-element.59), channel_id=1, source_target_pairs={{0,2},{2,4},{4,6},{6,8},{8,10},{10,12},{12,14},{14,16},{16,18},{18... | collective-permute-start | bytes 138248 | tf_op jit(solution)/shard_map/ppermute | solution.py:369
  146.1 8.6 %collective-permute-start.24 = (bf16[15,1536]{1,0:T(8,128)(2,1)S(1)}, bf16[15,1536]{1,0:T(8,128)(2,1)S(1)}, u32[]{:S(2)}, u32[]{:S(2)}) collective-permute-start(bf16[15,1536]{1,0:T(8,128)(2,1)S(1)} %get-tuple-element.61), channel_id=1, source_target_pairs={{2,0},{4,2},{6,4},{8,6},{10,8},{12,10},{14,12},{16,14},{18,16},{20... | collective-permute-start | bytes 138248 | tf_op jit(solution)/shard_map/ppermute | solution.py:370
  146.2 13.2 %collective-permute-start.33 = (f32[32,12]{1,0:T(8,128)S(1)}, f32[32,12]{1,0:T(8,128)S(1)}, u32[]{:S(2)}, u32[]{:S(2)}) collective-permute-start(f32[32,12]{1,0:T(8,128)S(1)} %constant_dynamic-slice_fusion), channel_id=1, source_target_pairs={{0,2},{2,0},{4,6},{6,4},{8,10},{10,8},{12,14},{14,12},{16,18},{18,... | collective-permute-start | bytes 4616 | tf_op jit(solution)/shard_map/ppermute | solution.py:48
  (17 other events, 209.9 us)

commit v5 on v4

--- a/solution.py
+++ b/solution.py
@@ -233,8 +233,9 @@
 def rows_kernel(*refs, hs):
     kv = refs[0:4]
     qg = refs[4:8]
-    te, acc = refs[8:10]
-    kn, vn, qgs = refs[10:]
+    te = refs[8]
+    out = refs[9:13]
+    kn, vn, qgs, acc = refs[13:]
     span = kv[0].shape[1]
     for r in range(4):
         kn[r] = to_rows(kv[r][0:hs])
@@ -255,37 +256,33 @@
             exp = exp + jnp.sum(wp.reshape(span // 8, 8, span), axis=0)
             low = low + dotf(kv[r][...], w.astype(BF16))
             high = high + dotf(kv[r][0:hs], wp.astype(BF16))
-        acc[j, 0 : 2 * hs] = low
-        acc[j, 2 * hs : 3 * hs] = high
-        te[j, 0:1] = jnp.sum(tot, axis=0, keepdims=True)
-        te[j, 1:2] = jnp.sum(exp, axis=0, keepdims=True)
+        tot = jnp.sum(tot, axis=0, keepdims=True)
+        exp = jnp.sum(exp, axis=0, keepdims=True)
+        te[j, 0:1] = tot
+        te[j, 1:2] = exp
+        acc[j, 0:hs] = low[hs : 2 * hs].astype(BF16)
+        acc[j, hs : 2 * hs] = (high - (exp / tot) * low[0:hs]).astype(BF16)
+        acc[j, 2 * hs : 3 * hs] = low[0:hs].astype(BF16)
         return 0
 
     lax.fori_loop(0, 4, over_q, 0)
-
-
-def norm_kernel(te0, te1, acc, *rows, hs):
     for r in range(4):
-        t = te0[r] + te1[r ^ 2]
-        inv = 1.0 / t[0:1]
-        delta = t[1:2] * inv
-        rows[r][0:hs] = (acc[r, hs : 2 * hs] * inv).astype(BF16)
-        rows[r][hs : 2 * hs] = ((acc[r, 2 * hs : 3 * hs] - delta * acc[r, 0:hs]) * inv).astype(BF16)
+        out[r][...] = acc[r]
 
 
 def cols_kernel(*refs, hs):
-    te = refs[0:2]
-    kv = refs[2:6]
-    qg = refs[6:10]
-    cols = refs[10:14]
-    kn, vn, qn, gn, inv, dlt, colacc = refs[14:]
+    te = refs[0:4]
+    kv = refs[4:8]
+    qg = refs[8:12]
+    cols = refs[12:16]
+    kn, vn, qn, gn, inv, dlt, colacc = refs[16:]
     span = kv[0].shape[1]
     for r in range(4):
         kn[r] = to_rows(kv[r][0:hs])
         vn[r] = to_rows(kv[r][hs : 2 * hs])
         qn[r] = to_rows(qg[r][0:hs])
         gn[r] = to_rows(qg[r][hs : 2 * hs])
-        t = te[0][r] + te[1][r ^ 2]
+        t = (te[0][r] + te[1][r ^ 1]) + (te[2][r ^ 2] + te[3][r ^ 3])
         one = 1.0 / t[0:1]
         inv[r] = one
         dlt[r] = t[1:2] * one
@@ -313,8 +310,8 @@
     nat = pltpu.VMEM((4, span, hs), BF16)
     return vcall(
         functools.partial(rows_kernel, hs=hs),
-        (jax.ShapeDtypeStruct((4, 2, span), F32), jax.ShapeDtypeStruct((4, 3 * hs, span), F32)),
-        scratch=[nat, nat, pltpu.VMEM((4, 2 * hs, span), BF16)],
+        (jax.ShapeDtypeStruct((4, 2, span), F32),) + (jax.ShapeDtypeStruct((3 * hs, span), BF16),) * 4,
+        scratch=[nat, nat, pltpu.VMEM((4, 2 * hs, span), BF16), pltpu.VMEM((4, 3 * hs, span), BF16)],
         n_in=8,
     )(*kv, *qg)
 
@@ -326,22 +323,35 @@
         functools.partial(cols_kernel, hs=hs),
         tuple(jax.ShapeDtypeStruct((2 * hs, span), BF16) for _ in range(4)),
         scratch=[nat, nat, nat, nat, row, row, pltpu.VMEM((4, 2 * hs, span), BF16)],
-        n_in=10,
+        n_in=12,
     )(*te, *kv, *qg)
 
 
 def sum_kernel(*refs, hs):
-    row = refs[0][...].astype(F32)
-    col = refs[4][...].astype(F32)
-    for i in range(1, 4):
-        row = row + refs[i][...].astype(F32)
-        col = col + refs[4 + i][...].astype(F32)
-    row = row.astype(BF16)
+    te = refs[0:4]
+    row = refs[4:8]
+    out = refs[12:16]
+    each = [te[m][m] for m in range(4)]
+    total = (each[0] + each[1]) + (each[2] + each[3])
+    inv = 1.0 / total[0:1]
+    delta = total[1:2] * inv
+    att = jnp.zeros((hs, inv.shape[1]), F32)
+    grad = jnp.zeros((hs, inv.shape[1]), F32)
+    col = jnp.zeros((2 * hs, inv.shape[1]), F32)
+    for m in range(4):
+        att = att + row[m][0:hs].astype(F32)
+        shift = each[m][1:2] / each[m][0:1] - delta
+        grad = grad + (row[m][hs : 2 * hs].astype(F32) + shift * row[m][2 * hs : 3 * hs].astype(F32))
+        col = col + refs[8 + m][...].astype(F32)
+    att = (att * inv).astype(BF16)
+    grad = (grad * inv).astype(BF16)
     col = col.astype(BF16)
-    lanes = row.shape[1] // 4
+    lanes = inv.shape[1] // 4
     for s in range(4):
-        refs[8 + s][0 : 2 * hs] = row[:, s * lanes : (s + 1) * lanes]
-        refs[8 + s][2 * hs : 4 * hs] = col[:, s * lanes : (s + 1) * lanes]
+        part = slice(s * lanes, (s + 1) * lanes)
+        out[s][0:hs] = att[:, part]
+        out[s][hs : 2 * hs] = grad[:, part]
+        out[s][2 * hs : 4 * hs] = col[:, part]
 
 
 def back_kernel(idx, sharp, b0, b1, b2, b3, qhat, khat, rad, wf, w, out, home, att, qgr, kgr, vgr, *, heads, hs):
@@ -439,19 +449,16 @@
     kv = [kv0] + ordered(lambda s: move_x(kv0, s), (2, 1, 3))
     qg = [qg0] + ordered(lambda m: move_zy(qg0, m), (3, 2, 1))
     span = 4 * rows
-    te0, acc = run_rows(kv, qg, hs, span)
-    te1 = move_zy(te0, 1)
-    te1 = te0 + jnp.stack([te1[r ^ 1] for r in range(4)])
-    te = [te1, move_zy(te1, 2)]
-    rowp = vcall(functools.partial(norm_kernel, hs=hs), (shape((2 * hs, span), BF16),) * 4, n_in=3)(*te, acc)
+    te0, *rowp = run_rows(kv, qg, hs, span)
+    te = [te0] + ordered(lambda m: move_zy(te0, m), (3, 2, 1))
     row = [rowp[0]] + ordered(lambda m: move_zy(rowp[m], m), (3, 2, 1))
     colp = run_cols(te, kv, qg, hs, span)
     col = [colp[0]] + ordered(lambda s: move_x(colp[s], -s), (2, 1, 3))
     home = vcall(
         functools.partial(sum_kernel, hs=hs),
         tuple(shape((4 * hs, rows), BF16) for _ in range(4)),
-        n_in=8,
-    )(*row, *col)
+        n_in=12,
+    )(*te, *row, *col)
     back = [home[0]] + ordered(lambda s: move_z4(home[s], -s), (2, 1, 3))
     part = vcall(
         functools.partial(back_kernel, heads=heads, hs=hs),

time: 161 us -> 162 us (level)
    ppermute x9, starting transfers between devices: 13.6 us -> 15.9 us  [move_x(): return lax.ppermute(a, 'tm', pairs)]
    ppermute x2, starting transfers between devices: 7.03 us -> 5.3 us  [rims(): left = lax.ppermute(tail, 'tm', [(i, (i + 1) % TM) for i in range(TM)])]
    ppermute x10 -> x11, waiting for transfers between devices: 11.5 us -> 12.5 us  [move_zy(): return lax.ppermute(a, 'tm', pairs)]
    ppermute x10 -> x11, starting transfers between devices: 23.3 us -> 22.8 us  [move_zy(): return lax.ppermute(a, 'tm', pairs)]
    pallas_call x10 -> x9, Pallas kernels: 37.6 us -> 37.8 us  [run(): return call(*args)]
  transfers between devices with their start and end apart: 34 -> 35, of which waited for: 19 -> 20; matrix products, arithmetic and copies ran while one was open for 1% -> 1% of each run, Pallas kernels for 11% -> 4%
where the time goes in v5:
time: 162 us
  starting transfers between devices  71 us (44%)
  waiting for transfers between devices  48.2 us (30%)
  Pallas kernels  37.8 us (23%)
  local copies, waits for them, and re-layouts  4 us (2%)
    pallas_call x9, Pallas kernels, run(): return call(*args)  37.8 us
    ppermute x9, starting transfers between devices, move_z4(): return lax.ppermute(a, 'tm', pairs)  24.7 us
    ppermute x11, starting transfers between devices, move_zy(): return lax.ppermute(a, 'tm', pairs)  22.8 us
    ppermute x9, starting transfers between devices, move_x(): return lax.ppermute(a, 'tm', pairs)  15.9 us
    ppermute x9, waiting for transfers between devices, move_z4(): return lax.ppermute(a, 'tm', pairs)  14.9 us
    ppermute x11, waiting for transfers between devices, move_zy(): return lax.ppermute(a, 'tm', pairs)  12.5 us
    ppermute x2, waiting for transfers between devices, rims(): right = lax.ppermute(head, 'tm', [((i + 1) % TM, i) for i in range(TM)])  7.79 us
    ppermute x9, waiting for transfers between devices, move_x(): return lax.ppermute(a, 'tm', pairs)  6.04 us
  transfers between devices with their start and end apart: 35, of which 20 were waited for; matrix products, arithmetic and copies ran while one was open for 1% of the time, Pallas kernels for 4%

profile of v5, /device:TPU:30, one launch (start us, length us, event | category | flops | bytes accessed | tf_op | source)
XLA Modules:
  0.0 162.2 jit_solution(17789216844097835633)
XLA Ops:
  5.9 2.8 %shard_map.102 = (bf16[4,192,128]{2,1,0:T(8,128)(2,1)S(1)}, f32[384,128]{1,0:T(8,128)S(1)}, f32[384,128]{1,0:T(8,128)S(1)}, f32[8,128]{1,0:T(8,128)S(1)}) custom-call(f32[1,1536]{1,0:T(1,128)S(1)} %broadcast_in_dim.9.factor, bf16[128,1536]{1,0:T(8,128)(2,1)} %bitcast.20, bf16[3,1536,384]{2,1,0:T(8,128)(2,1)} %w.1), custom_call_target="tpu_custom_call" | custom-call | tf_op jit(solution)/shard_map/pallas_call | solution.py:80
  8.8 4.0 %collective-permute-done.1.right = bf16[15,1536]{1,0:T(8,128)(2,1)S(1)} collective-permute-done((bf16[15,1536]{1,0:T(8,128)(2,1)S(1)}, bf16[15,1536]{1,0:T(8,128)(2,1)S(1)}, u32[]{:S(2)}, u32[]{:S(2)}) %collective-permute-start.1) | collective-permute-done | bytes 46112 | tf_op jit(solution)/shard_map/ppermute | solution.py:380
  12.9 5.1 %shard_map.103 = (bf16[384,128]{1,0:T(8,128)(2,1)S(1)}, bf16[384,128]{1,0:T(8,128)(2,1)S(1)}, bf16[384,128]{1,0:T(8,128)(2,1)S(1)}, bf16[384,128]{1,0:T(8,128)(2,1)S(1)}, f32[128,1536]{1,0:T(8,128)S(1)}) custom-call(s32[1]{0:T(128)} %bitcast.1.idx, s32[1]{0:T(128)} %bitcast.place, f32[4]{0:T(128)S(1)} %copy-done.6, ...), custom_call_target="tpu_custom_call" | custom-call | tf_op jit(solution)/shard_map/pallas_call | solution.py:80
  18.0 3.4 %collective-permute-start.2 = (bf16[384,128]{1,0:T(8,128)(2,1)S(1)}, bf16[384,128]{1,0:T(8,128)(2,1)S(1)}, u32[]{:S(2)}, u32[]{:S(2)}) collective-permute-start(bf16[384,128]{1,0:T(8,128)(2,1)S(1)} %get-tuple-element.36), channel_id=1, source_target_pairs={{0,32},{2,34},{4,36},{6,38},{8,40},{10,42},{12,44},{14,46},{16,48}... | collective-permute-start | bytes 294920 | tf_op jit(solution)/shard_map/ppermute | solution.py:32
  21.3 4.5 %collective-permute-start.3 = (bf16[384,128]{1,0:T(8,128)(2,1)S(1)}, bf16[384,128]{1,0:T(8,128)(2,1)S(1)}, u32[]{:S(2)}, u32[]{:S(2)}) collective-permute-start(bf16[384,128]{1,0:T(8,128)(2,1)S(1)} %get-tuple-element.37), channel_id=1, source_target_pairs={{0,64},{2,66},{4,68},{6,70},{8,72},{10,74},{12,76},{14,78},{16,80}... | collective-permute-start | bytes 294920 | tf_op jit(solution)/shard_map/ppermute | solution.py:32
  25.8 2.7 %collective-permute-start.4 = (bf16[384,128]{1,0:T(8,128)(2,1)S(1)}, bf16[384,128]{1,0:T(8,128)(2,1)S(1)}, u32[]{:S(2)}, u32[]{:S(2)}) collective-permute-start(bf16[384,128]{1,0:T(8,128)(2,1)S(1)} %get-tuple-element.38), channel_id=1, source_target_pairs={{0,96},{2,98},{4,100},{6,102},{8,104},{10,106},{12,108},{14,110},{... | collective-permute-start | bytes 294920 | tf_op jit(solution)/shard_map/ppermute | solution.py:32
  28.5 3.8 %collective-permute-done.3.p2 = bf16[384,128]{1,0:T(8,128)(2,1)S(1)} collective-permute-done((bf16[384,128]{1,0:T(8,128)(2,1)S(1)}, bf16[384,128]{1,0:T(8,128)(2,1)S(1)}, u32[]{:S(2)}, u32[]{:S(2)}) %collective-permute-start.3) | collective-permute-done | bytes 98336 | tf_op jit(solution)/shard_map/ppermute | solution.py:32
  35.9 3.2 %collective-permute-start.8 = (bf16[192,512]{1,0:T(8,128)(2,1)S(1)}, bf16[192,512]{1,0:T(8,128)(2,1)S(1)}, u32[]{:S(2)}, u32[]{:S(2)}) collective-permute-start(bf16[192,512]{1,0:T(8,128)(2,1)S(1)} %get-tuple-element.40.refs_4_.refs_8_), channel_id=1, source_target_pairs={{0,16},{2,18},{4,20},{6,22},{8,24},{10,26},{12,28},{14,30},{16,0},... | collective-permute-start | bytes 589832 | tf_op jit(solution)/shard_map/ppermute | solution.py:48
  43.3 6.0 %collective-permute-done.9.refs_6_.refs_10_ = bf16[192,512]{1,0:T(8,128)(2,1)S(1)} collective-permute-done((bf16[192,512]{1,0:T(8,128)(2,1)S(1)}, bf16[192,512]{1,0:T(8,128)(2,1)S(1)}, u32[]{:S(2)}, u32[]{:S(2)}) %collective-permute-start.9) | collective-permute-done | bytes 196640 | tf_op jit(solution)/shard_map/ppermute | solution.py:48
  49.2 8.5 %shard_map.105 = (f32[4,2,512]{2,1,0:T(2,128)S(1)}, bf16[288,512]{1,0:T(8,128)(2,1)S(1)}, bf16[288,512]{1,0:T(8,128)(2,1)S(1)}, bf16[288,512]{1,0:T(8,128)(2,1)S(1)}, bf16[288,512]{1,0:T(8,128)(2,1)S(1)}) custom-call(bf16[192,512]{1,0:T(8,128)(2,1)S(1)} %get-tuple-element.39.refs_0_.refs_4_, bf16[192,512]{1,0:T(8,128)(2,1)S(1)} %collective-permute-done.5.refs_1_.refs_5_, ...), custom_call_target="tpu_custom_call" | custom-call | tf_op jit(solution)/shard_map/pallas_call | solution.py:80
  64.9 3.3 %collective-permute-done.13.refs_3_ = f32[4,2,512]{2,1,0:T(2,128)S(1)} collective-permute-done((f32[4,2,512]{2,1,0:T(2,128)S(1)}, f32[4,2,512]{2,1,0:T(2,128)S(1)}, u32[]{:S(2)}, u32[]{:S(2)}) %collective-permute-start.13) | collective-permute-done | bytes 16416 | tf_op jit(solution)/shard_map/ppermute | solution.py:48
  68.2 10.4 %shard_map.106 = (bf16[192,512]{1,0:T(8,128)(2,1)S(1)}, bf16[192,512]{1,0:T(8,128)(2,1)S(1)}, bf16[192,512]{1,0:T(8,128)(2,1)S(1)}, bf16[192,512]{1,0:T(8,128)(2,1)S(1)}) custom-call(f32[4,2,512]{2,1,0:T(2,128)S(1)} %get-tuple-element.41.refs_0_, f32[4,2,512]{2,1,0:T(2,128)S(1)} %collective-permute-done.11.refs_1_, ...), custom_call_target="tpu_custom_call" | custom-call | tf_op jit(solution)/shard_map/pallas_call | solution.py:80
  83.8 5.2 %collective-permute-start.18 = (bf16[192,512]{1,0:T(8,128)(2,1)S(1)}, bf16[192,512]{1,0:T(8,128)(2,1)S(1)}, u32[]{:S(2)}, u32[]{:S(2)}) collective-permute-start(bf16[192,512]{1,0:T(8,128)(2,1)S(1)} %get-tuple-element.48), channel_id=1, source_target_pairs={{0,8},{2,10},{4,12},{6,14},{8,0},{10,2},{12,4},{14,6},{16,24},{18,... | collective-permute-start | bytes 589832 | tf_op jit(solution)/shard_map/ppermute | solution.py:40
  95.0 3.9 %collective-permute-start.20 = (bf16[384,128]{1,0:T(8,128)(2,1)S(1)}, bf16[384,128]{1,0:T(8,128)(2,1)S(1)}, u32[]{:S(2)}, u32[]{:S(2)}) collective-permute-start(bf16[384,128]{1,0:T(8,128)(2,1)S(1)} %get-tuple-element.51), channel_id=1, source_target_pairs={{0,96},{2,98},{4,100},{6,102},{8,104},{10,106},{12,108},{14,110},{... | collective-permute-start | bytes 294920 | tf_op jit(solution)/shard_map/ppermute | solution.py:32
  103.7 3.8 %collective-permute-done.21.b2 = bf16[384,128]{1,0:T(8,128)(2,1)S(1)} collective-permute-done((bf16[384,128]{1,0:T(8,128)(2,1)S(1)}, bf16[384,128]{1,0:T(8,128)(2,1)S(1)}, u32[]{:S(2)}, u32[]{:S(2)}) %collective-permute-start.21) | collective-permute-done | bytes 98336 | tf_op jit(solution)/shard_map/ppermute | solution.py:32
  113.3 4.5 %shard_map.109 = (bf16[128,1536]{1,0:T(8,128)(2,1)S(1)}, bf16[128,1536]{1,0:T(8,128)(2,1)}, f32[2,32,768]{2,1,0:T(8,128)S(1)}, bf16[15,1536]{1,0:T(8,128)(2,1)S(1)}, bf16[15,1536]{1,0:T(8,128)(2,1)S(1)}) custom-call(s32[1]{0:T(128)} %bitcast.place, bf16[256,1536]{1,0:T(8,128)(2,1)S(1)} %shard_map.108.part, ...), custom_call_target="tpu_custom_call" | custom-call | tf_op jit(solution)/shard_map/pallas_call | solution.py:80
  118.0 4.8 %collective-permute-done.26 = f32[32,768]{1,0:T(8,128)S(1)} collective-permute-done((f32[32,768]{1,0:T(8,128)S(1)}, f32[32,768]{1,0:T(8,128)S(1)}, u32[]{:S(2)}, u32[]{:S(2)}) %collective-permute-start.26) | collective-permute-done | bytes 98336 | tf_op jit(solution)/shard_map/ppermute | solution.py:395
  122.9 3.5 %collective-permute-start.28 = (f32[32,192]{1,0:T(8,128)S(1)}, f32[32,192]{1,0:T(8,128)S(1)}, u32[]{:S(2)}, u32[]{:S(2)}) collective-permute-start(f32[32,192]{1,0:T(8,128)S(1)} %get-tuple-element.70), channel_id=1, source_target_pairs={{0,64},{2,66},{4,68},{6,70},{8,72},{10,74},{12,76},{14,78},{16,80}... | collective-permute-start | bytes 73736 | tf_op jit(solution)/shard_map/ppermute | solution.py:32
  137.6 4.0 %collective-permute-start.32 = (f32[32,24]{1,0:T(8,128)S(1)}, f32[32,24]{1,0:T(8,128)S(1)}, u32[]{:S(2)}, u32[]{:S(2)}) collective-permute-start(f32[32,24]{1,0:T(8,128)S(1)} %get-tuple-element.73), channel_id=1, source_target_pairs={{0,8},{2,10},{4,12},{6,14},{8,0},{10,2},{12,4},{14,6},{16,24},{18,... | collective-permute-start | bytes 9224 | tf_op jit(solution)/shard_map/ppermute | solution.py:40
  141.8 3.1 %collective-permute-start.31 = (f32[32,24]{1,0:T(8,128)S(1)}, f32[32,24]{1,0:T(8,128)S(1)}, u32[]{:S(2)}, u32[]{:S(2)}) collective-permute-start(f32[32,24]{1,0:T(8,128)S(1)} %get-tuple-element.71), channel_id=1, source_target_pairs={{0,4},{2,6},{4,8},{6,10},{8,12},{10,14},{12,0},{14,2},{16,20},{18,... | collective-permute-start | bytes 9224 | tf_op jit(solution)/shard_map/ppermute | solution.py:40
  144.8 2.7 %collective-permute-start.24 = (bf16[15,1536]{1,0:T(8,128)(2,1)S(1)}, bf16[15,1536]{1,0:T(8,128)(2,1)S(1)}, u32[]{:S(2)}, u32[]{:S(2)}) collective-permute-start(bf16[15,1536]{1,0:T(8,128)(2,1)S(1)} %get-tuple-element.57), channel_id=1, source_target_pairs={{0,2},{2,4},{4,6},{6,8},{8,10},{10,12},{12,14},{14,16},{16,18},{18... | collective-permute-start | bytes 138248 | tf_op jit(solution)/shard_map/ppermute | solution.py:379
  148.5 3.8 %collective-permute-start.34 = (f32[32,12]{1,0:T(8,128)S(1)}, f32[32,12]{1,0:T(8,128)S(1)}, u32[]{:S(2)}, u32[]{:S(2)}) collective-permute-start(f32[32,12]{1,0:T(8,128)S(1)} %constant_dynamic-slice_fusion), channel_id=1, source_target_pairs={{0,2},{2,0},{4,6},{6,4},{8,10},{10,8},{12,14},{14,12},{16,18},{18,... | collective-permute-start | bytes 4616 | tf_op jit(solution)/shard_map/ppermute | solution.py:48
  152.4 3.8 %collective-permute-done.25.right = bf16[15,1536]{1,0:T(8,128)(2,1)S(1)} collective-permute-done((bf16[15,1536]{1,0:T(8,128)(2,1)S(1)}, bf16[15,1536]{1,0:T(8,128)(2,1)S(1)}, u32[]{:S(2)}, u32[]{:S(2)}) %collective-permute-start.25) | collective-permute-done | bytes 46112 | tf_op jit(solution)/shard_map/ppermute | solution.py:380
  156.1 4.1 %shard_map.110 = bf16[128,1536]{1,0:T(8,128)(2,1)S(1)} custom-call(s32[1]{0:T(128)} %bitcast.place, bf16[15,1536]{1,0:T(8,128)(2,1)S(1)} %collective-permute-done.24.left, bf16[128,1536]{1,0:T(8,128)(2,1)S(1)} %get-tuple-element.58.own, bf16[15,1536]{1,0:T(8,128)(2,1)S(1)} %collective-permute-done.25.right, f32[31,1536]{1,0:T(8,128)S(1)} %copy-done.5), custom_call_target="tpu_custom_call" | custom-call | tf_op jit(solution)/shard_map/pallas_call | solution.py:80
  (84 shorter events, 56.6 us)
Async XLA Ops:
  1.6 7.2 %collective-permute-start = (bf16[15,1536]{1,0:T(8,128)(2,1)S(1)}, bf16[15,1536]{1,0:T(8,128)(2,1)S(1)}, u32[]{:S(2)}, u32[]{:S(2)}) collective-permute-start(bf16[15,1536]{1,0:T(8,128)(2,1)S(1)} %get-tuple-element.67), channel_id=1, source_target_pairs={{0,2},{2,4},{4,6},{6,8},{8,10},{10,12},{12,14},{14,16},{16,18},{18... | collective-permute-start | bytes 138248 | tf_op jit(solution)/shard_map/ppermute | solution.py:379
  4.2 8.6 %collective-permute-start.1 = (bf16[15,1536]{1,0:T(8,128)(2,1)S(1)}, bf16[15,1536]{1,0:T(8,128)(2,1)S(1)}, u32[]{:S(2)}, u32[]{:S(2)}) collective-permute-start(bf16[15,1536]{1,0:T(8,128)(2,1)S(1)} %get-tuple-element.66), channel_id=1, source_target_pairs={{2,0},{4,2},{6,4},{8,6},{10,8},{12,10},{14,12},{16,14},{18,16},{20... | collective-permute-start | bytes 138248 | tf_op jit(solution)/shard_map/ppermute | solution.py:380
  18.0 10.5 %collective-permute-start.2 = (bf16[384,128]{1,0:T(8,128)(2,1)S(1)}, bf16[384,128]{1,0:T(8,128)(2,1)S(1)}, u32[]{:S(2)}, u32[]{:S(2)}) collective-permute-start(bf16[384,128]{1,0:T(8,128)(2,1)S(1)} %get-tuple-element.36), channel_id=1, source_target_pairs={{0,32},{2,34},{4,36},{6,38},{8,40},{10,42},{12,44},{14,46},{16,48}... | collective-permute-start | bytes 294920 | tf_op jit(solution)/shard_map/ppermute | solution.py:32
  21.3 10.9 %collective-permute-start.3 = (bf16[384,128]{1,0:T(8,128)(2,1)S(1)}, bf16[384,128]{1,0:T(8,128)(2,1)S(1)}, u32[]{:S(2)}, u32[]{:S(2)}) collective-permute-start(bf16[384,128]{1,0:T(8,128)(2,1)S(1)} %get-tuple-element.37), channel_id=1, source_target_pairs={{0,64},{2,66},{4,68},{6,70},{8,72},{10,74},{12,76},{14,78},{16,80}... | collective-permute-start | bytes 294920 | tf_op jit(solution)/shard_map/ppermute | solution.py:32
  25.8 7.9 %collective-permute-start.4 = (bf16[384,128]{1,0:T(8,128)(2,1)S(1)}, bf16[384,128]{1,0:T(8,128)(2,1)S(1)}, u32[]{:S(2)}, u32[]{:S(2)}) collective-permute-start(bf16[384,128]{1,0:T(8,128)(2,1)S(1)} %get-tuple-element.38), channel_id=1, source_target_pairs={{0,96},{2,98},{4,100},{6,102},{8,104},{10,106},{12,108},{14,110},{... | collective-permute-start | bytes 294920 | tf_op jit(solution)/shard_map/ppermute | solution.py:32
  33.9 8.2 %collective-permute-start.6 = (bf16[192,512]{1,0:T(8,128)(2,1)S(1)}, bf16[192,512]{1,0:T(8,128)(2,1)S(1)}, u32[]{:S(2)}, u32[]{:S(2)}) collective-permute-start(bf16[192,512]{1,0:T(8,128)(2,1)S(1)} %get-tuple-element.39.refs_0_.refs_4_), channel_id=1, source_target_pairs={{0,8},{2,10},{4,12},{6,14},{8,0},{10,2},{12,4},{14,6},{16,24},{18,... | collective-permute-start | bytes 589832 | tf_op jit(solution)/shard_map/ppermute | solution.py:40
  35.0 8.2 %collective-permute-start.7 = (bf16[192,512]{1,0:T(8,128)(2,1)S(1)}, bf16[192,512]{1,0:T(8,128)(2,1)S(1)}, u32[]{:S(2)}, u32[]{:S(2)}) collective-permute-start(bf16[192,512]{1,0:T(8,128)(2,1)S(1)} %get-tuple-element.39.refs_0_.refs_4_), channel_id=1, source_target_pairs={{0,12},{2,14},{4,0},{6,2},{8,4},{10,6},{12,8},{14,10},{16,28},{18,... | collective-permute-start | bytes 589832 | tf_op jit(solution)/shard_map/ppermute | solution.py:40
  35.9 7.4 %collective-permute-start.8 = (bf16[192,512]{1,0:T(8,128)(2,1)S(1)}, bf16[192,512]{1,0:T(8,128)(2,1)S(1)}, u32[]{:S(2)}, u32[]{:S(2)}) collective-permute-start(bf16[192,512]{1,0:T(8,128)(2,1)S(1)} %get-tuple-element.40.refs_4_.refs_8_), channel_id=1, source_target_pairs={{0,16},{2,18},{4,20},{6,22},{8,24},{10,26},{12,28},{14,30},{16,0},... | collective-permute-start | bytes 589832 | tf_op jit(solution)/shard_map/ppermute | solution.py:48
  39.1 10.1 %collective-permute-start.9 = (bf16[192,512]{1,0:T(8,128)(2,1)S(1)}, bf16[192,512]{1,0:T(8,128)(2,1)S(1)}, u32[]{:S(2)}, u32[]{:S(2)}) collective-permute-start(bf16[192,512]{1,0:T(8,128)(2,1)S(1)} %get-tuple-element.40.refs_4_.refs_8_), channel_id=1, source_target_pairs={{0,2},{2,0},{4,6},{6,4},{8,10},{10,8},{12,14},{14,12},{16,18},{18,... | collective-permute-start | bytes 589832 | tf_op jit(solution)/shard_map/ppermute | solution.py:48
  39.5 9.7 %collective-permute-start.10 = (bf16[192,512]{1,0:T(8,128)(2,1)S(1)}, bf16[192,512]{1,0:T(8,128)(2,1)S(1)}, u32[]{:S(2)}, u32[]{:S(2)}) collective-permute-start(bf16[192,512]{1,0:T(8,128)(2,1)S(1)} %get-tuple-element.40.refs_4_.refs_8_), channel_id=1, source_target_pairs={{0,18},{2,16},{4,22},{6,20},{8,26},{10,24},{12,30},{14,28},{16,2},... | collective-permute-start | bytes 589832 | tf_op jit(solution)/shard_map/ppermute | solution.py:48
  78.6 10.4 %collective-permute-start.17 = (bf16[192,512]{1,0:T(8,128)(2,1)S(1)}, bf16[192,512]{1,0:T(8,128)(2,1)S(1)}, u32[]{:S(2)}, u32[]{:S(2)}) collective-permute-start(bf16[192,512]{1,0:T(8,128)(2,1)S(1)} %get-tuple-element.47), channel_id=1, source_target_pairs={{0,12},{2,14},{4,0},{6,2},{8,4},{10,6},{12,8},{14,10},{16,28},{18,... | collective-permute-start | bytes 589832 | tf_op jit(solution)/shard_map/ppermute | solution.py:40
  78.8 15.9 %collective-permute-start.14 = (bf16[288,512]{1,0:T(8,128)(2,1)S(1)}, bf16[288,512]{1,0:T(8,128)(2,1)S(1)}, u32[]{:S(2)}, u32[]{:S(2)}) collective-permute-start(bf16[288,512]{1,0:T(8,128)(2,1)S(1)} %get-tuple-element.43), channel_id=1, source_target_pairs={{0,16},{2,18},{4,20},{6,22},{8,24},{10,26},{12,28},{14,30},{16,0},... | collective-permute-start | bytes 884744 | tf_op jit(solution)/shard_map/ppermute | solution.py:48
  80.7 13.9 %collective-permute-start.15 = (bf16[288,512]{1,0:T(8,128)(2,1)S(1)}, bf16[288,512]{1,0:T(8,128)(2,1)S(1)}, u32[]{:S(2)}, u32[]{:S(2)}) collective-permute-start(bf16[288,512]{1,0:T(8,128)(2,1)S(1)} %get-tuple-element.44), channel_id=1, source_target_pairs={{0,2},{2,0},{4,6},{6,4},{8,10},{10,8},{12,14},{14,12},{16,18},{18,... | collective-permute-start | bytes 884744 | tf_op jit(solution)/shard_map/ppermute | solution.py:48
  82.1 12.6 %collective-permute-start.16 = (bf16[288,512]{1,0:T(8,128)(2,1)S(1)}, bf16[288,512]{1,0:T(8,128)(2,1)S(1)}, u32[]{:S(2)}, u32[]{:S(2)}) collective-permute-start(bf16[288,512]{1,0:T(8,128)(2,1)S(1)} %get-tuple-element.45), channel_id=1, source_target_pairs={{0,18},{2,16},{4,22},{6,20},{8,26},{10,24},{12,30},{14,28},{16,2},... | collective-permute-start | bytes 884744 | tf_op jit(solution)/shard_map/ppermute | solution.py:48
  83.8 8.8 %collective-permute-start.18 = (bf16[192,512]{1,0:T(8,128)(2,1)S(1)}, bf16[192,512]{1,0:T(8,128)(2,1)S(1)}, u32[]{:S(2)}, u32[]{:S(2)}) collective-permute-start(bf16[192,512]{1,0:T(8,128)(2,1)S(1)} %get-tuple-element.48), channel_id=1, source_target_pairs={{0,8},{2,10},{4,12},{6,14},{8,0},{10,2},{12,4},{14,6},{16,24},{18,... | collective-permute-start | bytes 589832 | tf_op jit(solution)/shard_map/ppermute | solution.py:40
  95.0 8.8 %collective-permute-start.20 = (bf16[384,128]{1,0:T(8,128)(2,1)S(1)}, bf16[384,128]{1,0:T(8,128)(2,1)S(1)}, u32[]{:S(2)}, u32[]{:S(2)}) collective-permute-start(bf16[384,128]{1,0:T(8,128)(2,1)S(1)} %get-tuple-element.51), channel_id=1, source_target_pairs={{0,96},{2,98},{4,100},{6,102},{8,104},{10,106},{12,108},{14,110},{... | collective-permute-start | bytes 294920 | tf_op jit(solution)/shard_map/ppermute | solution.py:32
  98.9 8.6 %collective-permute-start.21 = (bf16[384,128]{1,0:T(8,128)(2,1)S(1)}, bf16[384,128]{1,0:T(8,128)(2,1)S(1)}, u32[]{:S(2)}, u32[]{:S(2)}) collective-permute-start(bf16[384,128]{1,0:T(8,128)(2,1)S(1)} %get-tuple-element.52), channel_id=1, source_target_pairs={{0,64},{2,66},{4,68},{6,70},{8,72},{10,74},{12,76},{14,78},{16,80}... | collective-permute-start | bytes 294920 | tf_op jit(solution)/shard_map/ppermute | solution.py:32
  101.5 7.1 %collective-permute-start.22 = (bf16[384,128]{1,0:T(8,128)(2,1)S(1)}, bf16[384,128]{1,0:T(8,128)(2,1)S(1)}, u32[]{:S(2)}, u32[]{:S(2)}) collective-permute-start(bf16[384,128]{1,0:T(8,128)(2,1)S(1)} %get-tuple-element.53), channel_id=1, source_target_pairs={{0,32},{2,34},{4,36},{6,38},{8,40},{10,42},{12,44},{14,46},{16,48}... | collective-permute-start | bytes 294920 | tf_op jit(solution)/shard_map/ppermute | solution.py:32
  122.9 7.9 %collective-permute-start.28 = (f32[32,192]{1,0:T(8,128)S(1)}, f32[32,192]{1,0:T(8,128)S(1)}, u32[]{:S(2)}, u32[]{:S(2)}) collective-permute-start(f32[32,192]{1,0:T(8,128)S(1)} %get-tuple-element.70), channel_id=1, source_target_pairs={{0,64},{2,66},{4,68},{6,70},{8,72},{10,74},{12,76},{14,78},{16,80}... | collective-permute-start | bytes 73736 | tf_op jit(solution)/shard_map/ppermute | solution.py:32
  137.6 10.8 %collective-permute-start.32 = (f32[32,24]{1,0:T(8,128)S(1)}, f32[32,24]{1,0:T(8,128)S(1)}, u32[]{:S(2)}, u32[]{:S(2)}) collective-permute-start(f32[32,24]{1,0:T(8,128)S(1)} %get-tuple-element.73), channel_id=1, source_target_pairs={{0,8},{2,10},{4,12},{6,14},{8,0},{10,2},{12,4},{14,6},{16,24},{18,... | collective-permute-start | bytes 9224 | tf_op jit(solution)/shard_map/ppermute | solution.py:40
  141.6 6.8 %collective-permute-start.33 = (f32[32,24]{1,0:T(8,128)S(1)}, f32[32,24]{1,0:T(8,128)S(1)}, u32[]{:S(2)}, u32[]{:S(2)}) collective-permute-start(f32[32,24]{1,0:T(8,128)S(1)} %get-tuple-element.72), channel_id=1, source_target_pairs={{0,12},{2,14},{4,0},{6,2},{8,4},{10,6},{12,8},{14,10},{16,28},{18,... | collective-permute-start | bytes 9224 | tf_op jit(solution)/shard_map/ppermute | solution.py:40
  144.8 7.5 %collective-permute-start.24 = (bf16[15,1536]{1,0:T(8,128)(2,1)S(1)}, bf16[15,1536]{1,0:T(8,128)(2,1)S(1)}, u32[]{:S(2)}, u32[]{:S(2)}) collective-permute-start(bf16[15,1536]{1,0:T(8,128)(2,1)S(1)} %get-tuple-element.57), channel_id=1, source_target_pairs={{0,2},{2,4},{4,6},{6,8},{8,10},{10,12},{12,14},{14,16},{16,18},{18... | collective-permute-start | bytes 138248 | tf_op jit(solution)/shard_map/ppermute | solution.py:379
  147.5 8.6 %collective-permute-start.25 = (bf16[15,1536]{1,0:T(8,128)(2,1)S(1)}, bf16[15,1536]{1,0:T(8,128)(2,1)S(1)}, u32[]{:S(2)}, u32[]{:S(2)}) collective-permute-start(bf16[15,1536]{1,0:T(8,128)(2,1)S(1)} %get-tuple-element.59), channel_id=1, source_target_pairs={{2,0},{4,2},{6,4},{8,6},{10,8},{12,10},{14,12},{16,14},{18,16},{20... | collective-permute-start | bytes 138248 | tf_op jit(solution)/shard_map/ppermute | solution.py:380
  148.5 12.4 %collective-permute-start.34 = (f32[32,12]{1,0:T(8,128)S(1)}, f32[32,12]{1,0:T(8,128)S(1)}, u32[]{:S(2)}, u32[]{:S(2)}) collective-permute-start(f32[32,12]{1,0:T(8,128)S(1)} %constant_dynamic-slice_fusion), channel_id=1, source_target_pairs={{0,2},{2,0},{4,6},{6,4},{8,10},{10,8},{12,14},{14,12},{16,18},{18,... | collective-permute-start | bytes 4616 | tf_op jit(solution)/shard_map/ppermute | solution.py:48
  (18 other events, 311.8 us)

commit v6 on v5

--- a/solution.py
+++ b/solution.py
@@ -272,14 +272,16 @@
 
 def cols_kernel(*refs, hs):
     te = refs[0:4]
-    kv = refs[4:8]
-    qg = refs[8:12]
-    cols = refs[12:16]
-    kn, vn, qn, gn, inv, dlt, colacc = refs[16:]
+    qg = refs[4:8]
+    count = (len(refs) - 15) // 2
+    kv = refs[8 : 8 + count]
+    cols = refs[8 + count : 8 + 2 * count]
+    kn, vn, qn, gn, inv, dlt, colacc = refs[8 + 2 * count :]
     span = kv[0].shape[1]
-    for r in range(4):
+    for r in range(count):
         kn[r] = to_rows(kv[r][0:hs])
         vn[r] = to_rows(kv[r][hs : 2 * hs])
+    for r in range(4):
         qn[r] = to_rows(qg[r][0:hs])
         gn[r] = to_rows(qg[r][hs : 2 * hs])
         t = (te[0][r] + te[1][r ^ 1]) + (te[2][r ^ 2] + te[3][r ^ 3])
@@ -301,8 +303,8 @@
         colacc[b, hs : 2 * hs] = gv.T.astype(BF16)
         return 0
 
-    lax.fori_loop(0, 4, over_k, 0)
-    for r in range(4):
+    lax.fori_loop(0, count, over_k, 0)
+    for r in range(count):
         cols[r][...] = colacc[r]
 
 
@@ -321,10 +323,10 @@
     row = pltpu.VMEM((4, 1, span), F32)
     return vcall(
         functools.partial(cols_kernel, hs=hs),
-        tuple(jax.ShapeDtypeStruct((2 * hs, span), BF16) for _ in range(4)),
+        tuple(jax.ShapeDtypeStruct((2 * hs, span), BF16) for _ in kv),
         scratch=[nat, nat, nat, nat, row, row, pltpu.VMEM((4, 2 * hs, span), BF16)],
-        n_in=12,
-    )(*te, *kv, *qg)
+        n_in=8 + len(kv),
+    )(*te, *qg, *kv)
 
 
 def sum_kernel(*refs, hs):
@@ -446,14 +448,15 @@
     )(z4, place, score_sharpening, *adj_rims, filter_taps, qhat, pay, final_projection)
     got = [sent[0]] + ordered(lambda s: move_z4(sent[s], s), (2, 1, 3))
     kv0, qg0 = vcall(pack_kernel, (shape((2 * hs, 4 * rows), BF16),) * 2, n_in=4)(*got)
+    qg = [qg0] + ordered(lambda m: move_zy(qg0, m), (3, 2, 1))
     kv = [kv0] + ordered(lambda s: move_x(kv0, s), (2, 1, 3))
-    qg = [qg0] + ordered(lambda m: move_zy(qg0, m), (3, 2, 1))
     span = 4 * rows
     te0, *rowp = run_rows(kv, qg, hs, span)
     te = [te0] + ordered(lambda m: move_zy(te0, m), (3, 2, 1))
     row = [rowp[0]] + ordered(lambda m: move_zy(rowp[m], m), (3, 2, 1))
-    colp = run_cols(te, kv, qg, hs, span)
-    col = [colp[0]] + ordered(lambda s: move_x(colp[s], -s), (2, 1, 3))
+    away = run_cols(te, kv[1:], qg, hs, span)
+    back = ordered(lambda s: move_x(away[s - 1], -s), (2, 1, 3))
+    col = list(run_cols(te, kv[:1], qg, hs, span)) + back
     home = vcall(
         functools.partial(sum_kernel, hs=hs),
         tuple(shape((4 * hs, rows), BF16) for _ in range(4)),

time: 162 us -> 160 us (0.988)
  the two profiles are of different devices: /device:TPU:30 before, /device:TPU:126 now
where the time goes in v6:
time: 160 us
  waiting for transfers between devices  58.1 us (36%)
  starting transfers between devices  57.7 us (36%)
  Pallas kernels  38 us (24%)
  local copies, waits for them, and re-layouts  4.88 us (3%)
    pallas_call x10, Pallas kernels, run(): return call(*args)  38 us
    ppermute x9, starting transfers between devices, move_z4(): return lax.ppermute(a, 'tm', pairs)  18.8 us
    ppermute x9, waiting for transfers between devices, move_z4(): return lax.ppermute(a, 'tm', pairs)  16.8 us
    ppermute x9, starting transfers between devices, move_x(): return lax.ppermute(a, 'tm', pairs)  15.9 us
    ppermute x11, starting transfers between devices, move_zy(): return lax.ppermute(a, 'tm', pairs)  15.5 us
    ppermute x2, waiting for transfers between devices, rims(): right = lax.ppermute(head, 'tm', [((i + 1) % TM, i) for i in range(TM)])  13.7 us
    ppermute x11, waiting for transfers between devices, move_zy(): return lax.ppermute(a, 'tm', pairs)  12.9 us
    ppermute x9, waiting for transfers between devices, move_x(): return lax.ppermute(a, 'tm', pairs)  7.22 us
  transfers between devices with their start and end apart: 35, of which 21 were waited for; matrix products, arithmetic and copies ran while one was open for 1% of the time, Pallas kernels for 6%

profile of v6, /device:TPU:126, one launch (start us, length us, event | category | flops | bytes accessed | tf_op | source)
XLA Modules:
  0.0 160.1 jit_solution(14723283121766094363)
XLA Ops:
  1.6 3.8 %collective-permute-start = (bf16[15,1536]{1,0:T(8,128)(2,1)S(1)}, bf16[15,1536]{1,0:T(8,128)(2,1)S(1)}, u32[]{:S(2)}, u32[]{:S(2)}) collective-permute-start(bf16[15,1536]{1,0:T(8,128)(2,1)S(1)} %get-tuple-element.65), channel_id=1, source_target_pairs={{0,2},{2,4},{4,6},{6,8},{8,10},{10,12},{12,14},{14,16},{16,18},{18... | collective-permute-start | bytes 138248 | tf_op jit(solution)/shard_map/ppermute | solution.py:381
  9.0 6.2 %collective-permute-done.1.right = bf16[15,1536]{1,0:T(8,128)(2,1)S(1)} collective-permute-done((bf16[15,1536]{1,0:T(8,128)(2,1)S(1)}, bf16[15,1536]{1,0:T(8,128)(2,1)S(1)}, u32[]{:S(2)}, u32[]{:S(2)}) %collective-permute-start.1) | collective-permute-done | bytes 46112 | tf_op jit(solution)/shard_map/ppermute | solution.py:382
  15.3 5.1 %shard_map.103 = (bf16[384,128]{1,0:T(8,128)(2,1)S(1)}, bf16[384,128]{1,0:T(8,128)(2,1)S(1)}, bf16[384,128]{1,0:T(8,128)(2,1)S(1)}, bf16[384,128]{1,0:T(8,128)(2,1)S(1)}, f32[128,1536]{1,0:T(8,128)S(1)}) custom-call(s32[1]{0:T(128)} %bitcast.1.idx, s32[1]{0:T(128)} %bitcast.place, f32[4]{0:T(128)S(1)} %copy-done.6, ...), custom_call_target="tpu_custom_call" | custom-call | tf_op jit(solution)/shard_map/pallas_call | solution.py:80
  22.1 2.9 %collective-permute-start.4 = (bf16[384,128]{1,0:T(8,128)(2,1)S(1)}, bf16[384,128]{1,0:T(8,128)(2,1)S(1)}, u32[]{:S(2)}, u32[]{:S(2)}) collective-permute-start(bf16[384,128]{1,0:T(8,128)(2,1)S(1)} %get-tuple-element.37), channel_id=1, source_target_pairs={{0,96},{2,98},{4,100},{6,102},{8,104},{10,106},{12,108},{14,110},{... | collective-permute-start | bytes 294920 | tf_op jit(solution)/shard_map/ppermute | solution.py:32
  25.1 4.3 %collective-permute-done.2.p1 = bf16[384,128]{1,0:T(8,128)(2,1)S(1)} collective-permute-done((bf16[384,128]{1,0:T(8,128)(2,1)S(1)}, bf16[384,128]{1,0:T(8,128)(2,1)S(1)}, u32[]{:S(2)}, u32[]{:S(2)}) %collective-permute-start.2) | collective-permute-done | bytes 98336 | tf_op jit(solution)/shard_map/ppermute | solution.py:32
  29.3 3.8 %collective-permute-done.3.p2 = bf16[384,128]{1,0:T(8,128)(2,1)S(1)} collective-permute-done((bf16[384,128]{1,0:T(8,128)(2,1)S(1)}, bf16[384,128]{1,0:T(8,128)(2,1)S(1)}, u32[]{:S(2)}, u32[]{:S(2)}) %collective-permute-start.3) | collective-permute-done | bytes 98336 | tf_op jit(solution)/shard_map/ppermute | solution.py:32
  37.6 4.5 %collective-permute-done.5.refs_1_.refs_8_ = bf16[192,512]{1,0:T(8,128)(2,1)S(1)} collective-permute-done((bf16[192,512]{1,0:T(8,128)(2,1)S(1)}, bf16[192,512]{1,0:T(8,128)(2,1)S(1)}, u32[]{:S(2)}, u32[]{:S(2)}) %collective-permute-start.5) | collective-permute-done | bytes 196640 | tf_op jit(solution)/shard_map/ppermute | solution.py:40
  45.7 4.4 %collective-permute-done.10.refs_7_ = bf16[192,512]{1,0:T(8,128)(2,1)S(1)} collective-permute-done((bf16[192,512]{1,0:T(8,128)(2,1)S(1)}, bf16[192,512]{1,0:T(8,128)(2,1)S(1)}, u32[]{:S(2)}, u32[]{:S(2)}) %collective-permute-start.10) | collective-permute-done | bytes 196640 | tf_op jit(solution)/shard_map/ppermute | solution.py:48
  50.1 8.4 %shard_map.105 = (f32[4,2,512]{2,1,0:T(2,128)S(1)}, bf16[288,512]{1,0:T(8,128)(2,1)S(1)}, bf16[288,512]{1,0:T(8,128)(2,1)S(1)}, bf16[288,512]{1,0:T(8,128)(2,1)S(1)}, bf16[288,512]{1,0:T(8,128)(2,1)S(1)}) custom-call(bf16[192,512]{1,0:T(8,128)(2,1)S(1)} %get-tuple-element.38.refs_0_.refs_8_, bf16[192,512]{1,0:T(8,128)(2,1)S(1)} %collective-permute-done.5.refs_1_.refs_8_, ...), custom_call_target="tpu_custom_call" | custom-call | tf_op jit(solution)/shard_map/pallas_call | solution.py:80
  58.8 3.7 %collective-permute-start.12 = (f32[4,2,512]{2,1,0:T(2,128)S(1)}, f32[4,2,512]{2,1,0:T(2,128)S(1)}, u32[]{:S(2)}, u32[]{:S(2)}) collective-permute-start(f32[4,2,512]{2,1,0:T(2,128)S(1)} %get-tuple-element.40.refs_0_), channel_id=1, source_target_pairs={{0,2},{2,0},{4,6},{6,4},{8,10},{10,8},{12,14},{14,12},{16,18},{18,... | collective-permute-start | bytes 49160 | tf_op jit(solution)/shard_map/ppermute | solution.py:48
  64.2 4.4 %collective-permute-done.13.refs_3_ = f32[4,2,512]{2,1,0:T(2,128)S(1)} collective-permute-done((f32[4,2,512]{2,1,0:T(2,128)S(1)}, f32[4,2,512]{2,1,0:T(2,128)S(1)}, u32[]{:S(2)}, u32[]{:S(2)}) %collective-permute-start.13) | collective-permute-done | bytes 16416 | tf_op jit(solution)/shard_map/ppermute | solution.py:48
  68.6 7.9 %shard_map.107 = (bf16[192,512]{1,0:T(8,128)(2,1)S(1)}, bf16[192,512]{1,0:T(8,128)(2,1)S(1)}, bf16[192,512]{1,0:T(8,128)(2,1)S(1)}) custom-call(f32[4,2,512]{2,1,0:T(2,128)S(1)} %get-tuple-element.40.refs_0_, f32[4,2,512]{2,1,0:T(2,128)S(1)} %collective-permute-done.11.refs_1_, f32[4,2,512]{2,1,0:T(2,128)S(1)} %collective-permute-done.12.refs_2_, ...), custom_call_target="tpu_custom_call" | custom-call | tf_op jit(solution)/shard_map/pallas_call | solution.py:80
  78.5 3.1 %collective-permute-start.16 = (bf16[288,512]{1,0:T(8,128)(2,1)S(1)}, bf16[288,512]{1,0:T(8,128)(2,1)S(1)}, u32[]{:S(2)}, u32[]{:S(2)}) collective-permute-start(bf16[288,512]{1,0:T(8,128)(2,1)S(1)} %get-tuple-element.44), channel_id=1, source_target_pairs={{0,18},{2,16},{4,22},{6,20},{8,26},{10,24},{12,30},{14,28},{16,2},... | collective-permute-start | bytes 884744 | tf_op jit(solution)/shard_map/ppermute | solution.py:48
  81.7 5.1 %collective-permute-start.18 = (bf16[192,512]{1,0:T(8,128)(2,1)S(1)}, bf16[192,512]{1,0:T(8,128)(2,1)S(1)}, u32[]{:S(2)}, u32[]{:S(2)}) collective-permute-start(bf16[192,512]{1,0:T(8,128)(2,1)S(1)} %get-tuple-element.46), channel_id=1, source_target_pairs={{0,8},{2,10},{4,12},{6,14},{8,0},{10,2},{12,4},{14,6},{16,24},{18,... | collective-permute-start | bytes 589832 | tf_op jit(solution)/shard_map/ppermute | solution.py:40
  92.9 4.8 %collective-permute-start.21 = (bf16[384,128]{1,0:T(8,128)(2,1)S(1)}, bf16[384,128]{1,0:T(8,128)(2,1)S(1)}, u32[]{:S(2)}, u32[]{:S(2)}) collective-permute-start(bf16[384,128]{1,0:T(8,128)(2,1)S(1)} %get-tuple-element.50), channel_id=1, source_target_pairs={{0,64},{2,66},{4,68},{6,70},{8,72},{10,74},{12,76},{14,78},{16,80}... | collective-permute-start | bytes 294920 | tf_op jit(solution)/shard_map/ppermute | solution.py:32
  109.5 4.5 %shard_map.110 = (bf16[128,1536]{1,0:T(8,128)(2,1)S(1)}, bf16[128,1536]{1,0:T(8,128)(2,1)}, f32[2,32,768]{2,1,0:T(8,128)S(1)}, bf16[15,1536]{1,0:T(8,128)(2,1)S(1)}, bf16[15,1536]{1,0:T(8,128)(2,1)S(1)}) custom-call(s32[1]{0:T(128)} %bitcast.place, bf16[256,1536]{1,0:T(8,128)(2,1)S(1)} %shard_map.109.part, ...), custom_call_target="tpu_custom_call" | custom-call | tf_op jit(solution)/shard_map/pallas_call | solution.py:80
  114.1 4.8 %collective-permute-done.26 = f32[32,768]{1,0:T(8,128)S(1)} collective-permute-done((f32[32,768]{1,0:T(8,128)S(1)}, f32[32,768]{1,0:T(8,128)S(1)}, u32[]{:S(2)}, u32[]{:S(2)}) %collective-permute-start.26) | collective-permute-done | bytes 98336 | tf_op jit(solution)/shard_map/ppermute | solution.py:397
  119.0 3.2 %collective-permute-start.28 = (f32[32,192]{1,0:T(8,128)S(1)}, f32[32,192]{1,0:T(8,128)S(1)}, u32[]{:S(2)}, u32[]{:S(2)}) collective-permute-start(f32[32,192]{1,0:T(8,128)S(1)} %get-tuple-element.68), channel_id=1, source_target_pairs={{0,64},{2,66},{4,68},{6,70},{8,72},{10,74},{12,76},{14,78},{16,80}... | collective-permute-start | bytes 73736 | tf_op jit(solution)/shard_map/ppermute | solution.py:32
  129.7 3.6 %collective-permute-done.30 = f32[32,96]{1,0:T(8,128)S(1)} collective-permute-done((f32[32,96]{1,0:T(8,128)S(1)}, f32[32,96]{1,0:T(8,128)S(1)}, u32[]{:S(2)}, u32[]{:S(2)}) %collective-permute-start.30) | collective-permute-done | bytes 12320 | tf_op jit(solution)/shard_map/ppermute | solution.py:48
  133.5 4.2 %collective-permute-start.32 = (f32[32,24]{1,0:T(8,128)S(1)}, f32[32,24]{1,0:T(8,128)S(1)}, u32[]{:S(2)}, u32[]{:S(2)}) collective-permute-start(f32[32,24]{1,0:T(8,128)S(1)} %get-tuple-element.71), channel_id=1, source_target_pairs={{0,8},{2,10},{4,12},{6,14},{8,0},{10,2},{12,4},{14,6},{16,24},{18,... | collective-permute-start | bytes 9224 | tf_op jit(solution)/shard_map/ppermute | solution.py:40
  137.8 3.2 %collective-permute-start.31 = (f32[32,24]{1,0:T(8,128)S(1)}, f32[32,24]{1,0:T(8,128)S(1)}, u32[]{:S(2)}, u32[]{:S(2)}) collective-permute-start(f32[32,24]{1,0:T(8,128)S(1)} %get-tuple-element.69), channel_id=1, source_target_pairs={{0,4},{2,6},{4,8},{6,10},{8,12},{10,14},{12,0},{14,2},{16,20},{18,... | collective-permute-start | bytes 9224 | tf_op jit(solution)/shard_map/ppermute | solution.py:40
  141.0 3.2 %collective-permute-start.24 = (bf16[15,1536]{1,0:T(8,128)(2,1)S(1)}, bf16[15,1536]{1,0:T(8,128)(2,1)S(1)}, u32[]{:S(2)}, u32[]{:S(2)}) collective-permute-start(bf16[15,1536]{1,0:T(8,128)(2,1)S(1)} %get-tuple-element.55), channel_id=1, source_target_pairs={{0,2},{2,4},{4,6},{6,8},{8,10},{10,12},{12,14},{14,16},{16,18},{18... | collective-permute-start | bytes 138248 | tf_op jit(solution)/shard_map/ppermute | solution.py:381
  146.6 7.4 %collective-permute-done.25.right = bf16[15,1536]{1,0:T(8,128)(2,1)S(1)} collective-permute-done((bf16[15,1536]{1,0:T(8,128)(2,1)S(1)}, bf16[15,1536]{1,0:T(8,128)(2,1)S(1)}, u32[]{:S(2)}, u32[]{:S(2)}) %collective-permute-start.25) | collective-permute-done | bytes 46112 | tf_op jit(solution)/shard_map/ppermute | solution.py:382
  154.0 4.1 %shard_map.111 = bf16[128,1536]{1,0:T(8,128)(2,1)S(1)} custom-call(s32[1]{0:T(128)} %bitcast.place, bf16[15,1536]{1,0:T(8,128)(2,1)S(1)} %collective-permute-done.24.left, bf16[128,1536]{1,0:T(8,128)(2,1)S(1)} %get-tuple-element.56.own, bf16[15,1536]{1,0:T(8,128)(2,1)S(1)} %collective-permute-done.25.right, f32[31,1536]{1,0:T(8,128)S(1)} %copy-done.5), custom_call_target="tpu_custom_call" | custom-call | tf_op jit(solution)/shard_map/pallas_call | solution.py:80
  (85 shorter events, 48.6 us)
Async XLA Ops:
  1.6 7.4 %collective-permute-start = (bf16[15,1536]{1,0:T(8,128)(2,1)S(1)}, bf16[15,1536]{1,0:T(8,128)(2,1)S(1)}, u32[]{:S(2)}, u32[]{:S(2)}) collective-permute-start(bf16[15,1536]{1,0:T(8,128)(2,1)S(1)} %get-tuple-element.65), channel_id=1, source_target_pairs={{0,2},{2,4},{4,6},{6,8},{8,10},{10,12},{12,14},{14,16},{16,18},{18... | collective-permute-start | bytes 138248 | tf_op jit(solution)/shard_map/ppermute | solution.py:381
  5.4 9.8 %collective-permute-start.1 = (bf16[15,1536]{1,0:T(8,128)(2,1)S(1)}, bf16[15,1536]{1,0:T(8,128)(2,1)S(1)}, u32[]{:S(2)}, u32[]{:S(2)}) collective-permute-start(bf16[15,1536]{1,0:T(8,128)(2,1)S(1)} %get-tuple-element.64), channel_id=1, source_target_pairs={{2,0},{4,2},{6,4},{8,6},{10,8},{12,10},{14,12},{16,14},{18,16},{20... | collective-permute-start | bytes 138248 | tf_op jit(solution)/shard_map/ppermute | solution.py:382
  21.3 8.1 %collective-permute-start.2 = (bf16[384,128]{1,0:T(8,128)(2,1)S(1)}, bf16[384,128]{1,0:T(8,128)(2,1)S(1)}, u32[]{:S(2)}, u32[]{:S(2)}) collective-permute-start(bf16[384,128]{1,0:T(8,128)(2,1)S(1)} %get-tuple-element.35), channel_id=1, source_target_pairs={{0,32},{2,34},{4,36},{6,38},{8,40},{10,42},{12,44},{14,46},{16,48}... | collective-permute-start | bytes 294920 | tf_op jit(solution)/shard_map/ppermute | solution.py:32
  21.5 11.6 %collective-permute-start.3 = (bf16[384,128]{1,0:T(8,128)(2,1)S(1)}, bf16[384,128]{1,0:T(8,128)(2,1)S(1)}, u32[]{:S(2)}, u32[]{:S(2)}) collective-permute-start(bf16[384,128]{1,0:T(8,128)(2,1)S(1)} %get-tuple-element.36), channel_id=1, source_target_pairs={{0,64},{2,66},{4,68},{6,70},{8,72},{10,74},{12,76},{14,78},{16,80}... | collective-permute-start | bytes 294920 | tf_op jit(solution)/shard_map/ppermute | solution.py:32
  22.1 12.0 %collective-permute-start.4 = (bf16[384,128]{1,0:T(8,128)(2,1)S(1)}, bf16[384,128]{1,0:T(8,128)(2,1)S(1)}, u32[]{:S(2)}, u32[]{:S(2)}) collective-permute-start(bf16[384,128]{1,0:T(8,128)(2,1)S(1)} %get-tuple-element.37), channel_id=1, source_target_pairs={{0,96},{2,98},{4,100},{6,102},{8,104},{10,106},{12,108},{14,110},{... | collective-permute-start | bytes 294920 | tf_op jit(solution)/shard_map/ppermute | solution.py:32
  34.2 7.8 %collective-permute-start.5 = (bf16[192,512]{1,0:T(8,128)(2,1)S(1)}, bf16[192,512]{1,0:T(8,128)(2,1)S(1)}, u32[]{:S(2)}, u32[]{:S(2)}) collective-permute-start(bf16[192,512]{1,0:T(8,128)(2,1)S(1)} %get-tuple-element.38.refs_0_.refs_8_), channel_id=1, source_target_pairs={{0,4},{2,6},{4,8},{6,10},{8,12},{10,14},{12,0},{14,2},{16,20},{18,... | collective-permute-start | bytes 589832 | tf_op jit(solution)/shard_map/ppermute | solution.py:40
  34.3 10.3 %collective-permute-start.6 = (bf16[192,512]{1,0:T(8,128)(2,1)S(1)}, bf16[192,512]{1,0:T(8,128)(2,1)S(1)}, u32[]{:S(2)}, u32[]{:S(2)}) collective-permute-start(bf16[192,512]{1,0:T(8,128)(2,1)S(1)} %get-tuple-element.38.refs_0_.refs_8_), channel_id=1, source_target_pairs={{0,8},{2,10},{4,12},{6,14},{8,0},{10,2},{12,4},{14,6},{16,24},{18,... | collective-permute-start | bytes 589832 | tf_op jit(solution)/shard_map/ppermute | solution.py:40
  34.4 11.3 %collective-permute-start.7 = (bf16[192,512]{1,0:T(8,128)(2,1)S(1)}, bf16[192,512]{1,0:T(8,128)(2,1)S(1)}, u32[]{:S(2)}, u32[]{:S(2)}) collective-permute-start(bf16[192,512]{1,0:T(8,128)(2,1)S(1)} %get-tuple-element.38.refs_0_.refs_8_), channel_id=1, source_target_pairs={{0,12},{2,14},{4,0},{6,2},{8,4},{10,6},{12,8},{14,10},{16,28},{18,... | collective-permute-start | bytes 589832 | tf_op jit(solution)/shard_map/ppermute | solution.py:40
  36.4 9.4 %collective-permute-start.8 = (bf16[192,512]{1,0:T(8,128)(2,1)S(1)}, bf16[192,512]{1,0:T(8,128)(2,1)S(1)}, u32[]{:S(2)}, u32[]{:S(2)}) collective-permute-start(bf16[192,512]{1,0:T(8,128)(2,1)S(1)} %get-tuple-element.39.refs_4_), channel_id=1, source_target_pairs={{0,16},{2,18},{4,20},{6,22},{8,24},{10,26},{12,28},{14,30},{16,0},... | collective-permute-start | bytes 589832 | tf_op jit(solution)/shard_map/ppermute | solution.py:48
  36.4 9.4 %collective-permute-start.9 = (bf16[192,512]{1,0:T(8,128)(2,1)S(1)}, bf16[192,512]{1,0:T(8,128)(2,1)S(1)}, u32[]{:S(2)}, u32[]{:S(2)}) collective-permute-start(bf16[192,512]{1,0:T(8,128)(2,1)S(1)} %get-tuple-element.39.refs_4_), channel_id=1, source_target_pairs={{0,2},{2,0},{4,6},{6,4},{8,10},{10,8},{12,14},{14,12},{16,18},{18,... | collective-permute-start | bytes 589832 | tf_op jit(solution)/shard_map/ppermute | solution.py:48
  42.0 8.1 %collective-permute-start.10 = (bf16[192,512]{1,0:T(8,128)(2,1)S(1)}, bf16[192,512]{1,0:T(8,128)(2,1)S(1)}, u32[]{:S(2)}, u32[]{:S(2)}) collective-permute-start(bf16[192,512]{1,0:T(8,128)(2,1)S(1)} %get-tuple-element.39.refs_4_), channel_id=1, source_target_pairs={{0,18},{2,16},{4,22},{6,20},{8,26},{10,24},{12,30},{14,28},{16,2},... | collective-permute-start | bytes 589832 | tf_op jit(solution)/shard_map/ppermute | solution.py:48
  76.5 10.2 %collective-permute-start.17 = (bf16[192,512]{1,0:T(8,128)(2,1)S(1)}, bf16[192,512]{1,0:T(8,128)(2,1)S(1)}, u32[]{:S(2)}, u32[]{:S(2)}) collective-permute-start(bf16[192,512]{1,0:T(8,128)(2,1)S(1)} %get-tuple-element.45), channel_id=1, source_target_pairs={{0,12},{2,14},{4,0},{6,2},{8,4},{10,6},{12,8},{14,10},{16,28},{18,... | collective-permute-start | bytes 589832 | tf_op jit(solution)/shard_map/ppermute | solution.py:40
  76.6 15.8 %collective-permute-start.14 = (bf16[288,512]{1,0:T(8,128)(2,1)S(1)}, bf16[288,512]{1,0:T(8,128)(2,1)S(1)}, u32[]{:S(2)}, u32[]{:S(2)}) collective-permute-start(bf16[288,512]{1,0:T(8,128)(2,1)S(1)} %get-tuple-element.42), channel_id=1, source_target_pairs={{0,16},{2,18},{4,20},{6,22},{8,24},{10,26},{12,28},{14,30},{16,0},... | collective-permute-start | bytes 884744 | tf_op jit(solution)/shard_map/ppermute | solution.py:48
  76.8 15.6 %collective-permute-start.15 = (bf16[288,512]{1,0:T(8,128)(2,1)S(1)}, bf16[288,512]{1,0:T(8,128)(2,1)S(1)}, u32[]{:S(2)}, u32[]{:S(2)}) collective-permute-start(bf16[288,512]{1,0:T(8,128)(2,1)S(1)} %get-tuple-element.43), channel_id=1, source_target_pairs={{0,2},{2,0},{4,6},{6,4},{8,10},{10,8},{12,14},{14,12},{16,18},{18,... | collective-permute-start | bytes 884744 | tf_op jit(solution)/shard_map/ppermute | solution.py:48
  78.5 13.9 %collective-permute-start.16 = (bf16[288,512]{1,0:T(8,128)(2,1)S(1)}, bf16[288,512]{1,0:T(8,128)(2,1)S(1)}, u32[]{:S(2)}, u32[]{:S(2)}) collective-permute-start(bf16[288,512]{1,0:T(8,128)(2,1)S(1)} %get-tuple-element.44), channel_id=1, source_target_pairs={{0,18},{2,16},{4,22},{6,20},{8,26},{10,24},{12,30},{14,28},{16,2},... | collective-permute-start | bytes 884744 | tf_op jit(solution)/shard_map/ppermute | solution.py:48
  81.7 9.1 %collective-permute-start.18 = (bf16[192,512]{1,0:T(8,128)(2,1)S(1)}, bf16[192,512]{1,0:T(8,128)(2,1)S(1)}, u32[]{:S(2)}, u32[]{:S(2)}) collective-permute-start(bf16[192,512]{1,0:T(8,128)(2,1)S(1)} %get-tuple-element.46), channel_id=1, source_target_pairs={{0,8},{2,10},{4,12},{6,14},{8,0},{10,2},{12,4},{14,6},{16,24},{18,... | collective-permute-start | bytes 589832 | tf_op jit(solution)/shard_map/ppermute | solution.py:40
  92.7 7.7 %collective-permute-start.20 = (bf16[384,128]{1,0:T(8,128)(2,1)S(1)}, bf16[384,128]{1,0:T(8,128)(2,1)S(1)}, u32[]{:S(2)}, u32[]{:S(2)}) collective-permute-start(bf16[384,128]{1,0:T(8,128)(2,1)S(1)} %get-tuple-element.49), channel_id=1, source_target_pairs={{0,96},{2,98},{4,100},{6,102},{8,104},{10,106},{12,108},{14,110},{... | collective-permute-start | bytes 294920 | tf_op jit(solution)/shard_map/ppermute | solution.py:32
  92.9 9.6 %collective-permute-start.21 = (bf16[384,128]{1,0:T(8,128)(2,1)S(1)}, bf16[384,128]{1,0:T(8,128)(2,1)S(1)}, u32[]{:S(2)}, u32[]{:S(2)}) collective-permute-start(bf16[384,128]{1,0:T(8,128)(2,1)S(1)} %get-tuple-element.50), channel_id=1, source_target_pairs={{0,64},{2,66},{4,68},{6,70},{8,72},{10,74},{12,76},{14,78},{16,80}... | collective-permute-start | bytes 294920 | tf_op jit(solution)/shard_map/ppermute | solution.py:32
  97.7 7.3 %collective-permute-start.22 = (bf16[384,128]{1,0:T(8,128)(2,1)S(1)}, bf16[384,128]{1,0:T(8,128)(2,1)S(1)}, u32[]{:S(2)}, u32[]{:S(2)}) collective-permute-start(bf16[384,128]{1,0:T(8,128)(2,1)S(1)} %get-tuple-element.51), channel_id=1, source_target_pairs={{0,32},{2,34},{4,36},{6,38},{8,40},{10,42},{12,44},{14,46},{16,48}... | collective-permute-start | bytes 294920 | tf_op jit(solution)/shard_map/ppermute | solution.py:32
  119.0 8.1 %collective-permute-start.28 = (f32[32,192]{1,0:T(8,128)S(1)}, f32[32,192]{1,0:T(8,128)S(1)}, u32[]{:S(2)}, u32[]{:S(2)}) collective-permute-start(f32[32,192]{1,0:T(8,128)S(1)} %get-tuple-element.68), channel_id=1, source_target_pairs={{0,64},{2,66},{4,68},{6,70},{8,72},{10,74},{12,76},{14,78},{16,80}... | collective-permute-start | bytes 73736 | tf_op jit(solution)/shard_map/ppermute | solution.py:32
  133.5 11.0 %collective-permute-start.32 = (f32[32,24]{1,0:T(8,128)S(1)}, f32[32,24]{1,0:T(8,128)S(1)}, u32[]{:S(2)}, u32[]{:S(2)}) collective-permute-start(f32[32,24]{1,0:T(8,128)S(1)} %get-tuple-element.71), channel_id=1, source_target_pairs={{0,8},{2,10},{4,12},{6,14},{8,0},{10,2},{12,4},{14,6},{16,24},{18,... | collective-permute-start | bytes 9224 | tf_op jit(solution)/shard_map/ppermute | solution.py:40
  137.7 6.8 %collective-permute-start.33 = (f32[32,24]{1,0:T(8,128)S(1)}, f32[32,24]{1,0:T(8,128)S(1)}, u32[]{:S(2)}, u32[]{:S(2)}) collective-permute-start(f32[32,24]{1,0:T(8,128)S(1)} %get-tuple-element.70), channel_id=1, source_target_pairs={{0,12},{2,14},{4,0},{6,2},{8,4},{10,6},{12,8},{14,10},{16,28},{18,... | collective-permute-start | bytes 9224 | tf_op jit(solution)/shard_map/ppermute | solution.py:40
  144.2 9.8 %collective-permute-start.25 = (bf16[15,1536]{1,0:T(8,128)(2,1)S(1)}, bf16[15,1536]{1,0:T(8,128)(2,1)S(1)}, u32[]{:S(2)}, u32[]{:S(2)}) collective-permute-start(bf16[15,1536]{1,0:T(8,128)(2,1)S(1)} %get-tuple-element.57), channel_id=1, source_target_pairs={{2,0},{4,2},{6,4},{8,6},{10,8},{12,10},{14,12},{16,14},{18,16},{20... | collective-permute-start | bytes 138248 | tf_op jit(solution)/shard_map/ppermute | solution.py:382
  144.7 14.2 %collective-permute-start.34 = (f32[32,12]{1,0:T(8,128)S(1)}, f32[32,12]{1,0:T(8,128)S(1)}, u32[]{:S(2)}, u32[]{:S(2)}) collective-permute-start(f32[32,12]{1,0:T(8,128)S(1)} %constant_dynamic-slice_fusion), channel_id=1, source_target_pairs={{0,2},{2,0},{4,6},{6,4},{8,10},{10,8},{12,14},{14,12},{16,18},{18,... | collective-permute-start | bytes 4616 | tf_op jit(solution)/shard_map/ppermute | solution.py:48
  (18 other events, 216.6 us)

commit v7 on v5

--- a/solution.py
+++ b/solution.py
@@ -53,19 +53,25 @@
     return [got[s] for s in (1, 2, 3)]
 
 
-def vcall(kernel, out_shape, scratch=(), smem=0, n_in=0, raw=0, out_hbm=()):
+def vcall(kernel, out_shape, scratch=(), smem=0, n_in=0, raw=0, out_hbm=(), out_raw=()):
     space = [pl.BlockSpec(memory_space=pltpu.SMEM)] * smem
     space += [pl.BlockSpec(memory_space=pltpu.VMEM)] * n_in
     space += [pl.BlockSpec(memory_space=pltpu.HBM if not INTERPRET else pl.ANY)] * raw
     flat, tree = jax.tree.flatten(out_shape)
     held = flat
     if not INTERPRET:
-        held = [o if i in out_hbm else pltpu.VMEM(o.shape, o.dtype) for i, o in enumerate(flat)]
+        held = [o if i in out_hbm else (pltpu.HBM if i in out_raw else pltpu.VMEM)(o.shape, o.dtype) for i, o in enumerate(flat)]
     call = pl.pallas_call(
         kernel,
         out_shape=jax.tree.unflatten(tree, held),
         in_specs=space,
-        out_specs=jax.tree.unflatten(tree, [pl.BlockSpec(memory_space=pltpu.VMEM)] * len(flat)),
+        out_specs=jax.tree.unflatten(
+            tree,
+            [
+                pl.BlockSpec(memory_space=pltpu.VMEM if i not in out_raw else pl.ANY if INTERPRET else pltpu.HBM)
+                for i in range(len(flat))
+            ],
+        ),
         scratch_shapes=list(scratch),
         compiler_params=pltpu.CompilerParams(vmem_limit_bytes=LIMIT),
         interpret=INTERPRET,
@@ -88,20 +94,27 @@
     return lax.dot_general(a, b, (((ca,), (cb,)), ((), ())), preferred_element_type=F32)
 
 
+def one_row(a):
+    return jnp.concatenate([a[i : i + 1] for i in range(a.shape[0])], axis=1)
+
+
 def front_kernel(
-    factor, x_hbm, w_hbm, pay, qhat_o, khat_o, rad_o, x, w, sem, *, heads, hs
+    factor_hbm, x_hbm, w_hbm, pay, qhat_o, khat_o, rad_o, factor, x, w, sem, *, heads, hs
 ):
     x_copy = pltpu.make_async_copy(x_hbm, x, sem.at[0])
     x_copy.start()
+    f_copy = pltpu.make_async_copy(factor_hbm, factor, sem.at[4])
+    f_copy.start()
     copies = [pltpu.make_async_copy(w_hbm.at[i], w.at[i], sem.at[1 + i]) for i in range(3)]
     for i in (1, 2, 0):
         copies[i].start()
     x_copy.wait()
+    f_copy.wait()
     xf = x[...].astype(F32)
     centred = xf - jnp.mean(xf, axis=-1, keepdims=True)
     var = jnp.mean(centred * centred, axis=-1, keepdims=True)
     unit = centred * (1.0 / jnp.sqrt(var + 1e-05))
-    normed = (unit * factor[...]).astype(BF16)
+    normed = (unit * one_row(factor)).astype(BF16)
     copies[1].wait()
     kt = dotf(normed, w[1]).T
     copies[2].wait()
@@ -151,10 +164,11 @@
     lax.fori_loop(0, out.shape[1] // 128, chunk, 0)
 
 
-def send_kernel(idx, place, sharp, left, own, right, taps, qhat, pay, wf, o0, o1, o2, o3, gres_o, pad, g_s, gres, *, hs):
+def send_kernel(idx, place, sharp, left, own, right, taps, qhat, pay, wf, o0, o1, o2, o3, gres_o, pad, g_s, gres, sem, *, hs):
     fill_pad(pad, left, own, right, place[0])
     conv_rows(pad, taps, gres, own.shape[0], True)
-    gres_o[...] = gres[...]
+    out = pltpu.make_async_copy(gres, gres_o, sem)
+    out.start()
     gt = dotf(wf[...], gres[...].astype(BF16), 1, 1).astype(BF16)
     for h in range(4):
         g_s[h, 0:hs] = (qhat[h * hs : (h + 1) * hs] * (sharp[h] / math.sqrt(hs))).astype(BF16)
@@ -163,6 +177,7 @@
         at = lax.rem(idx[0] + s, 4)
         o[0 : 2 * hs] = pay[at]
         o[2 * hs : 4 * hs] = g_s[at]
+    out.wait()
 
 
 def tail_kernel(
@@ -187,7 +202,7 @@
     grad = part[rows : 2 * rows].astype(F32) + other[rows : 2 * rows].astype(F32)
     prod = grad * unit
     gain[...] = jnp.sum(prod, axis=0, keepdims=True)
-    f = factor[...]
+    f = one_row(factor)
     scaled = grad * f
     m1 = jnp.mean(scaled, axis=-1, keepdims=True)
     m2 = jnp.mean(prod * f, axis=-1, keepdims=True)
@@ -420,7 +435,7 @@
     place = t.astype(jnp.int32).reshape(1)
     x_in = input_signal[0]
     adj = mixture_adjoint[0]
-    factor = standardize_factor[None]
+    factor = standardize_factor.reshape(-1, 128)
     shape = jax.ShapeDtypeStruct
     adj_rims = rims(adj, adj[:reach], adj[rows - reach :])
     piece = shape((4 * hs, rows), BF16)
@@ -428,26 +443,26 @@
         functools.partial(front_kernel, heads=heads, hs=hs),
         (shape((heads, 2 * hs, rows), BF16), shape((flat, rows), F32), shape((flat, rows), F32), shape((2 * heads, rows), F32)),
         scratch=[
+            pltpu.VMEM(factor.shape, F32),
             pltpu.VMEM((rows, width), BF16),
             pltpu.VMEM((3, width, flat), BF16),
-            pltpu.SemaphoreType.DMA((4,)),
+            pltpu.SemaphoreType.DMA((5,)),
         ],
-        n_in=1,
-        raw=2,
+        raw=3,
     )(factor, x_in, triple_projection)
     pad = pltpu.VMEM((rows + 32, width), F32)
     *sent, grad_res = vcall(
         functools.partial(send_kernel, hs=hs),
         (piece,) * 4 + (shape((rows, width), F32),),
-        scratch=[pad, pltpu.VMEM((4, 2 * hs, rows), BF16), pltpu.VMEM((rows, width), F32)],
-        out_hbm=(4,),
+        scratch=[pad, pltpu.VMEM((4, 2 * hs, rows), BF16), pltpu.VMEM((rows, width), F32), pltpu.SemaphoreType.DMA(())],
+        out_raw=(4,),
         smem=3,
         n_in=7,
     )(z4, place, score_sharpening, *adj_rims, filter_taps, qhat, pay, final_projection)
     got = [sent[0]] + ordered(lambda s: move_z4(sent[s], s), (2, 1, 3))
     kv0, qg0 = vcall(pack_kernel, (shape((2 * hs, 4 * rows), BF16),) * 2, n_in=4)(*got)
+    qg = [qg0] + ordered(lambda m: move_zy(qg0, m), (3, 2, 1))
     kv = [kv0] + ordered(lambda s: move_x(kv0, s), (2, 1, 3))
-    qg = [qg0] + ordered(lambda m: move_zy(qg0, m), (3, 2, 1))
     span = 4 * rows
     te0, *rowp = run_rows(kv, qg, hs, span)
     te = [te0] + ordered(lambda m: move_zy(te0, m), (3, 2, 1))

time: 162 us -> 163 us (level)
  waiting for transfers between devices: 48.2 us -> 50.9 us
  starting transfers between devices: 71 us -> 68.6 us
  transfers between devices with their start and end apart: 35 -> 35, of which waited for: 20 -> 18; matrix products, arithmetic and copies ran while one was open for 1% -> 1% of each run, Pallas kernels for 4% -> 4%
where the time goes in v7:
time: 163 us
  starting transfers between devices  68.6 us (42%)
  waiting for transfers between devices  50.9 us (31%)
  Pallas kernels  38.4 us (24%)
  local copies, waits for them, and re-layouts  3.3 us (2%)
    pallas_call x9, Pallas kernels, run(): return call(*args)  38.4 us
    ppermute x9, starting transfers between devices, move_z4(): return lax.ppermute(a, 'tm', pairs)  24.2 us
    ppermute x11, starting transfers between devices, move_zy(): return lax.ppermute(a, 'tm', pairs)  21.4 us
    ppermute x9, waiting for transfers between devices, move_z4(): return lax.ppermute(a, 'tm', pairs)  16.2 us
    ppermute x9, starting transfers between devices, move_x(): return lax.ppermute(a, 'tm', pairs)  15.5 us
    ppermute x11, waiting for transfers between devices, move_zy(): return lax.ppermute(a, 'tm', pairs)  11.5 us
    ppermute x2, waiting for transfers between devices, rims(): right = lax.ppermute(head, 'tm', [((i + 1) % TM, i) for i in range(TM)])  8.94 us
    ppermute x9, waiting for transfers between devices, move_x(): return lax.ppermute(a, 'tm', pairs)  7.31 us
  transfers between devices with their start and end apart: 35, of which 18 were waited for; matrix products, arithmetic and copies ran while one was open for 1% of the time, Pallas kernels for 4%

profile of v7, /device:TPU:30, one launch (start us, length us, event | category | flops | bytes accessed | tf_op | source)
XLA Modules:
  0.0 162.6 jit_solution(11045171030907927953)
XLA Ops:
  5.2 2.9 %shard_map.102 = (bf16[4,192,128]{2,1,0:T(8,128)(2,1)S(1)}, f32[384,128]{1,0:T(8,128)S(1)}, f32[384,128]{1,0:T(8,128)S(1)}, f32[8,128]{1,0:T(8,128)S(1)}) custom-call(f32[12,128]{1,0:T(8,128)} %bitcast.23, bf16[128,1536]{1,0:T(8,128)(2,1)} %bitcast.21, bf16[3,1536,384]{2,1,0:T(8,128)(2,1)} %w.1), custom_call_target="tpu_custom_call" | custom-call | tf_op jit(solution)/shard_map/pallas_call | solution.py:86
  8.1 4.7 %collective-permute-done.1.right = bf16[15,1536]{1,0:T(8,128)(2,1)S(1)} collective-permute-done((bf16[15,1536]{1,0:T(8,128)(2,1)S(1)}, bf16[15,1536]{1,0:T(8,128)(2,1)S(1)}, u32[]{:S(2)}, u32[]{:S(2)}) %collective-permute-start.1) | collective-permute-done | bytes 46112 | tf_op jit(solution)/shard_map/ppermute | solution.py:395
  12.9 5.9 %shard_map.103 = (bf16[384,128]{1,0:T(8,128)(2,1)S(1)}, bf16[384,128]{1,0:T(8,128)(2,1)S(1)}, bf16[384,128]{1,0:T(8,128)(2,1)S(1)}, bf16[384,128]{1,0:T(8,128)(2,1)S(1)}, f32[128,1536]{1,0:T(8,128)}) custom-call(s32[1]{0:T(128)} %bitcast.1.idx, s32[1]{0:T(128)} %bitcast.place, f32[4]{0:T(128)S(1)} %copy-done.6, ...), custom_call_target="tpu_custom_call" | custom-call | tf_op jit(solution)/shard_map/pallas_call | solution.py:86
  18.7 3.3 %collective-permute-start.2 = (bf16[384,128]{1,0:T(8,128)(2,1)S(1)}, bf16[384,128]{1,0:T(8,128)(2,1)S(1)}, u32[]{:S(2)}, u32[]{:S(2)}) collective-permute-start(bf16[384,128]{1,0:T(8,128)(2,1)S(1)} %get-tuple-element.36), channel_id=1, source_target_pairs={{0,32},{2,34},{4,36},{6,38},{8,40},{10,42},{12,44},{14,46},{16,48}... | collective-permute-start | bytes 294920 | tf_op jit(solution)/shard_map/ppermute | solution.py:32
  22.1 4.5 %collective-permute-start.3 = (bf16[384,128]{1,0:T(8,128)(2,1)S(1)}, bf16[384,128]{1,0:T(8,128)(2,1)S(1)}, u32[]{:S(2)}, u32[]{:S(2)}) collective-permute-start(bf16[384,128]{1,0:T(8,128)(2,1)S(1)} %get-tuple-element.37), channel_id=1, source_target_pairs={{0,64},{2,66},{4,68},{6,70},{8,72},{10,74},{12,76},{14,78},{16,80}... | collective-permute-start | bytes 294920 | tf_op jit(solution)/shard_map/ppermute | solution.py:32
  26.6 2.7 %collective-permute-start.4 = (bf16[384,128]{1,0:T(8,128)(2,1)S(1)}, bf16[384,128]{1,0:T(8,128)(2,1)S(1)}, u32[]{:S(2)}, u32[]{:S(2)}) collective-permute-start(bf16[384,128]{1,0:T(8,128)(2,1)S(1)} %get-tuple-element.38), channel_id=1, source_target_pairs={{0,96},{2,98},{4,100},{6,102},{8,104},{10,106},{12,108},{14,110},{... | collective-permute-start | bytes 294920 | tf_op jit(solution)/shard_map/ppermute | solution.py:32
  29.3 3.8 %collective-permute-done.3.p2 = bf16[384,128]{1,0:T(8,128)(2,1)S(1)} collective-permute-done((bf16[384,128]{1,0:T(8,128)(2,1)S(1)}, bf16[384,128]{1,0:T(8,128)(2,1)S(1)}, u32[]{:S(2)}, u32[]{:S(2)}) %collective-permute-start.3) | collective-permute-done | bytes 98336 | tf_op jit(solution)/shard_map/ppermute | solution.py:32
  37.2 2.7 %collective-permute-start.8 = (bf16[192,512]{1,0:T(8,128)(2,1)S(1)}, bf16[192,512]{1,0:T(8,128)(2,1)S(1)}, u32[]{:S(2)}, u32[]{:S(2)}) collective-permute-start(bf16[192,512]{1,0:T(8,128)(2,1)S(1)} %get-tuple-element.40.refs_4_.refs_8_), channel_id=1, source_target_pairs={{0,16},{2,18},{4,20},{6,22},{8,24},{10,26},{12,28},{14,30},{16,0},... | collective-permute-start | bytes 589832 | tf_op jit(solution)/shard_map/ppermute | solution.py:48
  44.6 5.0 %collective-permute-done.9.refs_6_.refs_10_ = bf16[192,512]{1,0:T(8,128)(2,1)S(1)} collective-permute-done((bf16[192,512]{1,0:T(8,128)(2,1)S(1)}, bf16[192,512]{1,0:T(8,128)(2,1)S(1)}, u32[]{:S(2)}, u32[]{:S(2)}) %collective-permute-start.9) | collective-permute-done | bytes 196640 | tf_op jit(solution)/shard_map/ppermute | solution.py:48
  49.5 8.3 %shard_map.105 = (f32[4,2,512]{2,1,0:T(2,128)S(1)}, bf16[288,512]{1,0:T(8,128)(2,1)S(1)}, bf16[288,512]{1,0:T(8,128)(2,1)S(1)}, bf16[288,512]{1,0:T(8,128)(2,1)S(1)}, bf16[288,512]{1,0:T(8,128)(2,1)S(1)}) custom-call(bf16[192,512]{1,0:T(8,128)(2,1)S(1)} %get-tuple-element.39.refs_0_.refs_4_, bf16[192,512]{1,0:T(8,128)(2,1)S(1)} %collective-permute-done.5.refs_1_.refs_5_, ...), custom_call_target="tpu_custom_call" | custom-call | tf_op jit(solution)/shard_map/pallas_call | solution.py:86
  65.5 3.0 %collective-permute-done.13.refs_3_ = f32[4,2,512]{2,1,0:T(2,128)S(1)} collective-permute-done((f32[4,2,512]{2,1,0:T(2,128)S(1)}, f32[4,2,512]{2,1,0:T(2,128)S(1)}, u32[]{:S(2)}, u32[]{:S(2)}) %collective-permute-start.13) | collective-permute-done | bytes 16416 | tf_op jit(solution)/shard_map/ppermute | solution.py:48
  68.4 10.4 %shard_map.106 = (bf16[192,512]{1,0:T(8,128)(2,1)S(1)}, bf16[192,512]{1,0:T(8,128)(2,1)S(1)}, bf16[192,512]{1,0:T(8,128)(2,1)S(1)}, bf16[192,512]{1,0:T(8,128)(2,1)S(1)}) custom-call(f32[4,2,512]{2,1,0:T(2,128)S(1)} %get-tuple-element.41.refs_0_, f32[4,2,512]{2,1,0:T(2,128)S(1)} %collective-permute-done.11.refs_1_, ...), custom_call_target="tpu_custom_call" | custom-call | tf_op jit(solution)/shard_map/pallas_call | solution.py:86
  84.0 5.2 %collective-permute-start.18 = (bf16[192,512]{1,0:T(8,128)(2,1)S(1)}, bf16[192,512]{1,0:T(8,128)(2,1)S(1)}, u32[]{:S(2)}, u32[]{:S(2)}) collective-permute-start(bf16[192,512]{1,0:T(8,128)(2,1)S(1)} %get-tuple-element.48), channel_id=1, source_target_pairs={{0,8},{2,10},{4,12},{6,14},{8,0},{10,2},{12,4},{14,6},{16,24},{18,... | collective-permute-start | bytes 589832 | tf_op jit(solution)/shard_map/ppermute | solution.py:40
  90.2 2.7 %collective-permute-done.18.refs_10_ = bf16[192,512]{1,0:T(8,128)(2,1)S(1)} collective-permute-done((bf16[192,512]{1,0:T(8,128)(2,1)S(1)}, bf16[192,512]{1,0:T(8,128)(2,1)S(1)}, u32[]{:S(2)}, u32[]{:S(2)}) %collective-permute-start.18) | collective-permute-done | bytes 196640 | tf_op jit(solution)/shard_map/ppermute | solution.py:40
  95.2 3.8 %collective-permute-start.20 = (bf16[384,128]{1,0:T(8,128)(2,1)S(1)}, bf16[384,128]{1,0:T(8,128)(2,1)S(1)}, u32[]{:S(2)}, u32[]{:S(2)}) collective-permute-start(bf16[384,128]{1,0:T(8,128)(2,1)S(1)} %get-tuple-element.51), channel_id=1, source_target_pairs={{0,96},{2,98},{4,100},{6,102},{8,104},{10,106},{12,108},{14,110},{... | collective-permute-start | bytes 294920 | tf_op jit(solution)/shard_map/ppermute | solution.py:32
  102.9 6.2 %collective-permute-done.21.b2 = bf16[384,128]{1,0:T(8,128)(2,1)S(1)} collective-permute-done((bf16[384,128]{1,0:T(8,128)(2,1)S(1)}, bf16[384,128]{1,0:T(8,128)(2,1)S(1)}, u32[]{:S(2)}, u32[]{:S(2)}) %collective-permute-start.21) | collective-permute-done | bytes 98336 | tf_op jit(solution)/shard_map/ppermute | solution.py:32
  113.8 4.5 %shard_map.109 = (bf16[128,1536]{1,0:T(8,128)(2,1)S(1)}, bf16[128,1536]{1,0:T(8,128)(2,1)}, f32[2,32,768]{2,1,0:T(8,128)S(1)}, bf16[15,1536]{1,0:T(8,128)(2,1)S(1)}, bf16[15,1536]{1,0:T(8,128)(2,1)S(1)}) custom-call(s32[1]{0:T(128)} %bitcast.place, bf16[256,1536]{1,0:T(8,128)(2,1)S(1)} %shard_map.108.part, ...), custom_call_target="tpu_custom_call" | custom-call | tf_op jit(solution)/shard_map/pallas_call | solution.py:86
  118.4 4.8 %collective-permute-done.26 = f32[32,768]{1,0:T(8,128)S(1)} collective-permute-done((f32[32,768]{1,0:T(8,128)S(1)}, f32[32,768]{1,0:T(8,128)S(1)}, u32[]{:S(2)}, u32[]{:S(2)}) %collective-permute-start.26) | collective-permute-done | bytes 98336 | tf_op jit(solution)/shard_map/ppermute | solution.py:410
  123.3 3.0 %collective-permute-start.28 = (f32[32,192]{1,0:T(8,128)S(1)}, f32[32,192]{1,0:T(8,128)S(1)}, u32[]{:S(2)}, u32[]{:S(2)}) collective-permute-start(f32[32,192]{1,0:T(8,128)S(1)} %get-tuple-element.70), channel_id=1, source_target_pairs={{0,64},{2,66},{4,68},{6,70},{8,72},{10,74},{12,76},{14,78},{16,80}... | collective-permute-start | bytes 73736 | tf_op jit(solution)/shard_map/ppermute | solution.py:32
  138.0 3.9 %collective-permute-start.32 = (f32[32,24]{1,0:T(8,128)S(1)}, f32[32,24]{1,0:T(8,128)S(1)}, u32[]{:S(2)}, u32[]{:S(2)}) collective-permute-start(f32[32,24]{1,0:T(8,128)S(1)} %get-tuple-element.73), channel_id=1, source_target_pairs={{0,8},{2,10},{4,12},{6,14},{8,0},{10,2},{12,4},{14,6},{16,24},{18,... | collective-permute-start | bytes 9224 | tf_op jit(solution)/shard_map/ppermute | solution.py:40
  145.1 2.7 %collective-permute-start.24 = (bf16[15,1536]{1,0:T(8,128)(2,1)S(1)}, bf16[15,1536]{1,0:T(8,128)(2,1)S(1)}, u32[]{:S(2)}, u32[]{:S(2)}) collective-permute-start(bf16[15,1536]{1,0:T(8,128)(2,1)S(1)} %get-tuple-element.57), channel_id=1, source_target_pairs={{0,2},{2,4},{4,6},{6,8},{8,10},{10,12},{12,14},{14,16},{16,18},{18... | collective-permute-start | bytes 138248 | tf_op jit(solution)/shard_map/ppermute | solution.py:394
  148.8 3.4 %collective-permute-start.34 = (f32[32,12]{1,0:T(8,128)S(1)}, f32[32,12]{1,0:T(8,128)S(1)}, u32[]{:S(2)}, u32[]{:S(2)}) collective-permute-start(f32[32,12]{1,0:T(8,128)S(1)} %constant_dynamic-slice_fusion), channel_id=1, source_target_pairs={{0,2},{2,0},{4,6},{6,4},{8,10},{10,8},{12,14},{14,12},{16,18},{18,... | collective-permute-start | bytes 4616 | tf_op jit(solution)/shard_map/ppermute | solution.py:48
  152.2 4.3 %collective-permute-done.25.right = bf16[15,1536]{1,0:T(8,128)(2,1)S(1)} collective-permute-done((bf16[15,1536]{1,0:T(8,128)(2,1)S(1)}, bf16[15,1536]{1,0:T(8,128)(2,1)S(1)}, u32[]{:S(2)}, u32[]{:S(2)}) %collective-permute-start.25) | collective-permute-done | bytes 46112 | tf_op jit(solution)/shard_map/ppermute | solution.py:395
  156.5 4.1 %shard_map.110 = bf16[128,1536]{1,0:T(8,128)(2,1)S(1)} custom-call(s32[1]{0:T(128)} %bitcast.place, bf16[15,1536]{1,0:T(8,128)(2,1)S(1)} %collective-permute-done.24.left, bf16[128,1536]{1,0:T(8,128)(2,1)S(1)} %get-tuple-element.58.own, bf16[15,1536]{1,0:T(8,128)(2,1)S(1)} %collective-permute-done.25.right, f32[31,1536]{1,0:T(8,128)S(1)} %copy-done.4), custom_call_target="tpu_custom_call" | custom-call | tf_op jit(solution)/shard_map/pallas_call | solution.py:86
  (83 shorter events, 56.3 us)
Async XLA Ops:
  1.6 6.5 %collective-permute-start = (bf16[15,1536]{1,0:T(8,128)(2,1)S(1)}, bf16[15,1536]{1,0:T(8,128)(2,1)S(1)}, u32[]{:S(2)}, u32[]{:S(2)}) collective-permute-start(bf16[15,1536]{1,0:T(8,128)(2,1)S(1)} %get-tuple-element.67), channel_id=1, source_target_pairs={{0,2},{2,4},{4,6},{6,8},{8,10},{10,12},{12,14},{14,16},{16,18},{18... | collective-permute-start | bytes 138248 | tf_op jit(solution)/shard_map/ppermute | solution.py:394
  4.2 8.6 %collective-permute-start.1 = (bf16[15,1536]{1,0:T(8,128)(2,1)S(1)}, bf16[15,1536]{1,0:T(8,128)(2,1)S(1)}, u32[]{:S(2)}, u32[]{:S(2)}) collective-permute-start(bf16[15,1536]{1,0:T(8,128)(2,1)S(1)} %get-tuple-element.66), channel_id=1, source_target_pairs={{2,0},{4,2},{6,4},{8,6},{10,8},{12,10},{14,12},{16,14},{18,16},{20... | collective-permute-start | bytes 138248 | tf_op jit(solution)/shard_map/ppermute | solution.py:395
  18.7 10.5 %collective-permute-start.2 = (bf16[384,128]{1,0:T(8,128)(2,1)S(1)}, bf16[384,128]{1,0:T(8,128)(2,1)S(1)}, u32[]{:S(2)}, u32[]{:S(2)}) collective-permute-start(bf16[384,128]{1,0:T(8,128)(2,1)S(1)} %get-tuple-element.36), channel_id=1, source_target_pairs={{0,32},{2,34},{4,36},{6,38},{8,40},{10,42},{12,44},{14,46},{16,48}... | collective-permute-start | bytes 294920 | tf_op jit(solution)/shard_map/ppermute | solution.py:32
  22.1 10.9 %collective-permute-start.3 = (bf16[384,128]{1,0:T(8,128)(2,1)S(1)}, bf16[384,128]{1,0:T(8,128)(2,1)S(1)}, u32[]{:S(2)}, u32[]{:S(2)}) collective-permute-start(bf16[384,128]{1,0:T(8,128)(2,1)S(1)} %get-tuple-element.37), channel_id=1, source_target_pairs={{0,64},{2,66},{4,68},{6,70},{8,72},{10,74},{12,76},{14,78},{16,80}... | collective-permute-start | bytes 294920 | tf_op jit(solution)/shard_map/ppermute | solution.py:32
  26.6 8.4 %collective-permute-start.4 = (bf16[384,128]{1,0:T(8,128)(2,1)S(1)}, bf16[384,128]{1,0:T(8,128)(2,1)S(1)}, u32[]{:S(2)}, u32[]{:S(2)}) collective-permute-start(bf16[384,128]{1,0:T(8,128)(2,1)S(1)} %get-tuple-element.38), channel_id=1, source_target_pairs={{0,96},{2,98},{4,100},{6,102},{8,104},{10,106},{12,108},{14,110},{... | collective-permute-start | bytes 294920 | tf_op jit(solution)/shard_map/ppermute | solution.py:32
  35.2 7.7 %collective-permute-start.6 = (bf16[192,512]{1,0:T(8,128)(2,1)S(1)}, bf16[192,512]{1,0:T(8,128)(2,1)S(1)}, u32[]{:S(2)}, u32[]{:S(2)}) collective-permute-start(bf16[192,512]{1,0:T(8,128)(2,1)S(1)} %get-tuple-element.39.refs_0_.refs_4_), channel_id=1, source_target_pairs={{0,8},{2,10},{4,12},{6,14},{8,0},{10,2},{12,4},{14,6},{16,24},{18,... | collective-permute-start | bytes 589832 | tf_op jit(solution)/shard_map/ppermute | solution.py:40
  35.8 8.7 %collective-permute-start.7 = (bf16[192,512]{1,0:T(8,128)(2,1)S(1)}, bf16[192,512]{1,0:T(8,128)(2,1)S(1)}, u32[]{:S(2)}, u32[]{:S(2)}) collective-permute-start(bf16[192,512]{1,0:T(8,128)(2,1)S(1)} %get-tuple-element.39.refs_0_.refs_4_), channel_id=1, source_target_pairs={{0,12},{2,14},{4,0},{6,2},{8,4},{10,6},{12,8},{14,10},{16,28},{18,... | collective-permute-start | bytes 589832 | tf_op jit(solution)/shard_map/ppermute | solution.py:40
  37.2 7.4 %collective-permute-start.8 = (bf16[192,512]{1,0:T(8,128)(2,1)S(1)}, bf16[192,512]{1,0:T(8,128)(2,1)S(1)}, u32[]{:S(2)}, u32[]{:S(2)}) collective-permute-start(bf16[192,512]{1,0:T(8,128)(2,1)S(1)} %get-tuple-element.40.refs_4_.refs_8_), channel_id=1, source_target_pairs={{0,16},{2,18},{4,20},{6,22},{8,24},{10,26},{12,28},{14,30},{16,0},... | collective-permute-start | bytes 589832 | tf_op jit(solution)/shard_map/ppermute | solution.py:48
  39.9 9.6 %collective-permute-start.9 = (bf16[192,512]{1,0:T(8,128)(2,1)S(1)}, bf16[192,512]{1,0:T(8,128)(2,1)S(1)}, u32[]{:S(2)}, u32[]{:S(2)}) collective-permute-start(bf16[192,512]{1,0:T(8,128)(2,1)S(1)} %get-tuple-element.40.refs_4_.refs_8_), channel_id=1, source_target_pairs={{0,2},{2,0},{4,6},{6,4},{8,10},{10,8},{12,14},{14,12},{16,18},{18,... | collective-permute-start | bytes 589832 | tf_op jit(solution)/shard_map/ppermute | solution.py:48
  40.9 8.7 %collective-permute-start.10 = (bf16[192,512]{1,0:T(8,128)(2,1)S(1)}, bf16[192,512]{1,0:T(8,128)(2,1)S(1)}, u32[]{:S(2)}, u32[]{:S(2)}) collective-permute-start(bf16[192,512]{1,0:T(8,128)(2,1)S(1)} %get-tuple-element.40.refs_4_.refs_8_), channel_id=1, source_target_pairs={{0,18},{2,16},{4,22},{6,20},{8,26},{10,24},{12,30},{14,28},{16,2},... | collective-permute-start | bytes 589832 | tf_op jit(solution)/shard_map/ppermute | solution.py:48
  78.8 10.4 %collective-permute-start.17 = (bf16[192,512]{1,0:T(8,128)(2,1)S(1)}, bf16[192,512]{1,0:T(8,128)(2,1)S(1)}, u32[]{:S(2)}, u32[]{:S(2)}) collective-permute-start(bf16[192,512]{1,0:T(8,128)(2,1)S(1)} %get-tuple-element.47), channel_id=1, source_target_pairs={{0,12},{2,14},{4,0},{6,2},{8,4},{10,6},{12,8},{14,10},{16,28},{18,... | collective-permute-start | bytes 589832 | tf_op jit(solution)/shard_map/ppermute | solution.py:40
  78.9 15.9 %collective-permute-start.14 = (bf16[288,512]{1,0:T(8,128)(2,1)S(1)}, bf16[288,512]{1,0:T(8,128)(2,1)S(1)}, u32[]{:S(2)}, u32[]{:S(2)}) collective-permute-start(bf16[288,512]{1,0:T(8,128)(2,1)S(1)} %get-tuple-element.43), channel_id=1, source_target_pairs={{0,16},{2,18},{4,20},{6,22},{8,24},{10,26},{12,28},{14,30},{16,0},... | collective-permute-start | bytes 884744 | tf_op jit(solution)/shard_map/ppermute | solution.py:48
  80.9 13.9 %collective-permute-start.15 = (bf16[288,512]{1,0:T(8,128)(2,1)S(1)}, bf16[288,512]{1,0:T(8,128)(2,1)S(1)}, u32[]{:S(2)}, u32[]{:S(2)}) collective-permute-start(bf16[288,512]{1,0:T(8,128)(2,1)S(1)} %get-tuple-element.44), channel_id=1, source_target_pairs={{0,2},{2,0},{4,6},{6,4},{8,10},{10,8},{12,14},{14,12},{16,18},{18,... | collective-permute-start | bytes 884744 | tf_op jit(solution)/shard_map/ppermute | solution.py:48
  82.3 12.6 %collective-permute-start.16 = (bf16[288,512]{1,0:T(8,128)(2,1)S(1)}, bf16[288,512]{1,0:T(8,128)(2,1)S(1)}, u32[]{:S(2)}, u32[]{:S(2)}) collective-permute-start(bf16[288,512]{1,0:T(8,128)(2,1)S(1)} %get-tuple-element.45), channel_id=1, source_target_pairs={{0,18},{2,16},{4,22},{6,20},{8,26},{10,24},{12,30},{14,28},{16,2},... | collective-permute-start | bytes 884744 | tf_op jit(solution)/shard_map/ppermute | solution.py:48
  84.0 8.8 %collective-permute-start.18 = (bf16[192,512]{1,0:T(8,128)(2,1)S(1)}, bf16[192,512]{1,0:T(8,128)(2,1)S(1)}, u32[]{:S(2)}, u32[]{:S(2)}) collective-permute-start(bf16[192,512]{1,0:T(8,128)(2,1)S(1)} %get-tuple-element.48), channel_id=1, source_target_pairs={{0,8},{2,10},{4,12},{6,14},{8,0},{10,2},{12,4},{14,6},{16,24},{18,... | collective-permute-start | bytes 589832 | tf_op jit(solution)/shard_map/ppermute | solution.py:40
  95.2 7.7 %collective-permute-start.20 = (bf16[384,128]{1,0:T(8,128)(2,1)S(1)}, bf16[384,128]{1,0:T(8,128)(2,1)S(1)}, u32[]{:S(2)}, u32[]{:S(2)}) collective-permute-start(bf16[384,128]{1,0:T(8,128)(2,1)S(1)} %get-tuple-element.51), channel_id=1, source_target_pairs={{0,96},{2,98},{4,100},{6,102},{8,104},{10,106},{12,108},{14,110},{... | collective-permute-start | bytes 294920 | tf_op jit(solution)/shard_map/ppermute | solution.py:32
  98.9 10.1 %collective-permute-start.21 = (bf16[384,128]{1,0:T(8,128)(2,1)S(1)}, bf16[384,128]{1,0:T(8,128)(2,1)S(1)}, u32[]{:S(2)}, u32[]{:S(2)}) collective-permute-start(bf16[384,128]{1,0:T(8,128)(2,1)S(1)} %get-tuple-element.52), channel_id=1, source_target_pairs={{0,64},{2,66},{4,68},{6,70},{8,72},{10,74},{12,76},{14,78},{16,80}... | collective-permute-start | bytes 294920 | tf_op jit(solution)/shard_map/ppermute | solution.py:32
  101.4 7.7 %collective-permute-start.22 = (bf16[384,128]{1,0:T(8,128)(2,1)S(1)}, bf16[384,128]{1,0:T(8,128)(2,1)S(1)}, u32[]{:S(2)}, u32[]{:S(2)}) collective-permute-start(bf16[384,128]{1,0:T(8,128)(2,1)S(1)} %get-tuple-element.53), channel_id=1, source_target_pairs={{0,32},{2,34},{4,36},{6,38},{8,40},{10,42},{12,44},{14,46},{16,48}... | collective-permute-start | bytes 294920 | tf_op jit(solution)/shard_map/ppermute | solution.py:32
  123.3 7.9 %collective-permute-start.28 = (f32[32,192]{1,0:T(8,128)S(1)}, f32[32,192]{1,0:T(8,128)S(1)}, u32[]{:S(2)}, u32[]{:S(2)}) collective-permute-start(f32[32,192]{1,0:T(8,128)S(1)} %get-tuple-element.70), channel_id=1, source_target_pairs={{0,64},{2,66},{4,68},{6,70},{8,72},{10,74},{12,76},{14,78},{16,80}... | collective-permute-start | bytes 73736 | tf_op jit(solution)/shard_map/ppermute | solution.py:32
  138.0 10.6 %collective-permute-start.32 = (f32[32,24]{1,0:T(8,128)S(1)}, f32[32,24]{1,0:T(8,128)S(1)}, u32[]{:S(2)}, u32[]{:S(2)}) collective-permute-start(f32[32,24]{1,0:T(8,128)S(1)} %get-tuple-element.73), channel_id=1, source_target_pairs={{0,8},{2,10},{4,12},{6,14},{8,0},{10,2},{12,4},{14,6},{16,24},{18,... | collective-permute-start | bytes 9224 | tf_op jit(solution)/shard_map/ppermute | solution.py:40
  141.9 6.8 %collective-permute-start.33 = (f32[32,24]{1,0:T(8,128)S(1)}, f32[32,24]{1,0:T(8,128)S(1)}, u32[]{:S(2)}, u32[]{:S(2)}) collective-permute-start(f32[32,24]{1,0:T(8,128)S(1)} %get-tuple-element.72), channel_id=1, source_target_pairs={{0,12},{2,14},{4,0},{6,2},{8,4},{10,6},{12,8},{14,10},{16,28},{18,... | collective-permute-start | bytes 9224 | tf_op jit(solution)/shard_map/ppermute | solution.py:40
  145.1 7.1 %collective-permute-start.24 = (bf16[15,1536]{1,0:T(8,128)(2,1)S(1)}, bf16[15,1536]{1,0:T(8,128)(2,1)S(1)}, u32[]{:S(2)}, u32[]{:S(2)}) collective-permute-start(bf16[15,1536]{1,0:T(8,128)(2,1)S(1)} %get-tuple-element.57), channel_id=1, source_target_pairs={{0,2},{2,4},{4,6},{6,8},{8,10},{10,12},{12,14},{14,16},{16,18},{18... | collective-permute-start | bytes 138248 | tf_op jit(solution)/shard_map/ppermute | solution.py:394
  147.9 8.6 %collective-permute-start.25 = (bf16[15,1536]{1,0:T(8,128)(2,1)S(1)}, bf16[15,1536]{1,0:T(8,128)(2,1)S(1)}, u32[]{:S(2)}, u32[]{:S(2)}) collective-permute-start(bf16[15,1536]{1,0:T(8,128)(2,1)S(1)} %get-tuple-element.59), channel_id=1, source_target_pairs={{2,0},{4,2},{6,4},{8,6},{10,8},{12,10},{14,12},{16,14},{18,16},{20... | collective-permute-start | bytes 138248 | tf_op jit(solution)/shard_map/ppermute | solution.py:395
  148.8 12.4 %collective-permute-start.34 = (f32[32,12]{1,0:T(8,128)S(1)}, f32[32,12]{1,0:T(8,128)S(1)}, u32[]{:S(2)}, u32[]{:S(2)}) collective-permute-start(f32[32,12]{1,0:T(8,128)S(1)} %constant_dynamic-slice_fusion), channel_id=1, source_target_pairs={{0,2},{2,0},{4,6},{6,4},{8,10},{10,8},{12,14},{14,12},{16,18},{18,... | collective-permute-start | bytes 4616 | tf_op jit(solution)/shard_map/ppermute | solution.py:48
  (18 other events, 240.3 us)
